TPU v7x, 256 devices: a whole 4x4x8 slice. The times are simulated.
256 devices in a mesh: tm: 32 (over y, z), order: 8 (over x, core).
Axes of the slice: x: 4, y: 4, z: 8, core: 2. Of those that a mesh axis runs over, the one named last changes fastest.
Arguments:
- design: bfloat16 [3, 4096, 65536], P(None, 'tm', 'order'), may hold values from -0.0546875 to 0.0546875
- gap_flags: int32 [4096], P('tm'), may hold values 0 or 1
- segment_ids: int32 [4096], P('tm'), may hold values from 0 to 3, never falling along the last dimension, each value on 1 to 2048 neighbouring positions
- ar_order: int32 [3], replicated, may hold values from 1 to 4
- ma_order: int32 [3], replicated, may hold values from 1 to 4
- ar_roots: float32 [3, 4], replicated, may hold values from -0.5 to 1, as said below
- ma_roots: float32 [3, 4], replicated, may hold values from -0.5 to 1, as said below
- kaula: float32 [8, 8192], P('order', 'tm'), may hold values from 0.2 to 2
- precond: float32 [8, 64, 128, 128], P('order', 'tm'), as said below
- solution: float32 [16, 8, 8192], P(None, 'order', 'tm'), may hold values from -6 to 6
- residual: float32 [16, 8, 8192], P(None, 'order', 'tm'), may hold values from -6 to 6
- direction: float32 [16, 8, 8192], P(None, 'order', 'tm'), may hold values from -6 to 6
Outputs:
- new_solution: float32 [16, 8, 8192], P(None, 'order', 'tm')
- new_residual: float32 [16, 8, 8192], P(None, 'order', 'tm')
- new_direction: float32 [16, 8, 8192], P(None, 'order', 'tm')
Inputs may be any that keep to these rules, and one draw needn't show every extreme that they name: The first root of each component of ar_roots lies within 2 / 4096 below 1; the others lie within 0.5 of zero. The first root of each component of ma_roots lies within 12 / 4096 below 1; the others lie within 0.5 of zero. `precond`: every block is symmetric positive definite.
All inputs are finite; a program needn't handle non-finite values. No bound on the sum of `gap_flags` on one device may be relied on, other than what follows from the above.
Results may differ from a plain program's by a relative error of at most 0.0036.
Values may be sent and summed in bfloat16 or wider, within the bound.
No kernel may reach another device: no remote copies, remote signals or barrier semaphores. Data moves between devices by JAX's collectives and lax.ppermute only.
A program may use at most 64 MiB of HBM per device.

v0:
```python
import functools

import jax
import jax.numpy as jnp
from jax import lax
from jax.sharding import Mesh
from jax.sharding import PartitionSpec as P

PMAX = 4
QMAX = 4
TM = ("tm_0", "tm_1")
ORDER = ("order_0", "order_1")
TM_ORDER = ("tm_0", "tm_1", "order_0", "order_1")


precise = lax.Precision.HIGHEST


def extended_2(block, sides, width):
    for axis, dim in sides:
        count = lax.axis_size(axis)
        forward = [(i, i + 1) for i in range(count - 1)]
        backward = [(target, source) for source, target in forward]
        low = lax.ppermute(
            lax.slice_in_dim(block, block.shape[dim] - width, None, axis=dim), axis, forward
        )
        high = lax.ppermute(lax.slice_in_dim(block, 0, width, axis=dim), axis, backward)
        block = jnp.concatenate([low, block, high], axis=dim)
    return block


def shifted(block, axis, distance):
    devices = range(lax.axis_size(axis))
    route = [(i - distance, i) for i in devices if i - distance in devices]
    return lax.ppermute(block, axis, route)


def copy_for_each(value, axis):
    copies = jnp.broadcast_to(value, (lax.axis_size(axis), *value.shape))
    return lax.all_to_all(copies, axis, split_axis=0, concat_axis=0, tiled=True)


def collected_together(value, axis):
    leaves = jax.tree.leaves(value)
    turns = sorted(range(len(leaves)), key=lambda k: -leaves[k].size)
    width = (1, *leaves[turns[0]].shape)[-1]
    lines = [
        jnp.pad(leaves[k].reshape(-1), (0, -leaves[k].size % width)).reshape(-1, width)
        for k in turns
    ]
    both, at, found = (copy_for_each(jnp.concatenate(lines), axis), 0, {})
    for k, line in zip(turns, lines):
        piece = both[:, at : at + len(line)].reshape(len(both), -1)
        found[k] = piece[:, : leaves[k].size].reshape(-1, *leaves[k].shape)
        at += len(line)
    numbers = iter(range(len(leaves)))
    return jax.tree.map(lambda _: found[next(numbers)], value)


def joined_by_halves(pieces, combine):
    while len(jax.tree.leaves(pieces)[0]) > 1:
        pieces = jax.vmap(combine)(
            *(jax.tree.map(lambda part: part[side::2], pieces) for side in (0, 1))
        )
    return jax.tree.map(lambda part: part[0], pieces)


def carried_in(value, axis, combine, identity):
    size, place = (lax.axis_size(axis), lax.axis_index(axis))
    passed = jnp.arange(size) < place

    def carried_kept(part, zero, own):
        part = jnp.where(
            passed.reshape(-1, *(1 for _ in own.shape)), part, jnp.asarray(zero, own.dtype)
        )
        return part

    pieces = collected_together(value, axis)
    return joined_by_halves(jax.tree.map(carried_kept, pieces, identity, value), combine)


def collected_alike(value, axis):
    leaves, found = (jax.tree.leaves(value), {})
    for first, a in enumerate(leaves):
        if first not in found:
            alike = [k for k, b in enumerate(leaves) if b.dtype == a.dtype]
            got = (
                collected_together([leaves[k] for k in alike], axis)
                if len(alike) > 1
                else [copy_for_each(a, axis)]
            )
            for k, b in zip(alike, got):
                found[k] = b
    numbers = iter(range(len(leaves)))
    return jax.tree.map(lambda _: found[next(numbers)], value)


def entering(value, axis, combine, identity):
    size, place = (lax.axis_size(axis), lax.axis_index(axis))
    passed = jnp.arange(size) > place

    def entering_kept(part, zero, own):
        part = jnp.where(
            passed.reshape(-1, *(1 for _ in own.shape)), part, jnp.asarray(zero, own.dtype)
        )
        return part[::-1]

    pieces = collected_alike(value, axis)
    return joined_by_halves(jax.tree.map(entering_kept, pieces, identity, value), combine)


def joined_along(parts, dim):
    parts = jnp.moveaxis(parts, 0, dim)
    dims = parts.shape
    return parts.reshape(*dims[:dim], dims[dim] * dims[dim + 1], *dims[dim + 2 :])


def gathered_copies(value, axis, dim):
    return joined_along(copy_for_each(value, axis), dim)


def over_copies(value, axis):
    everything = copy_for_each(value, axis)
    return jnp.sum(everything, axis=0)


def cut_along(value, dim, size):
    dims = value.shape
    parts = value.reshape(*dims[:dim], size, dims[dim] // size, *dims[dim + 1 :])
    return jnp.moveaxis(parts, dim, 0)


def sent_and_summed(value, axis, dim):
    parts = cut_along(value, dim, lax.axis_size(axis))
    arrived = lax.all_to_all(parts, axis, split_axis=0, concat_axis=0, tiled=True)
    return arrived.sum(axis=0)


def one_axis_at_a_time(value, axes):
    return functools.reduce(lax.psum, axes, value)


def polynomial(root_values, filter_order):
    number_roots = root_values.shape[1]
    coeffs = jnp.concatenate(
        [jnp.ones((3, 1), jnp.float32), jnp.zeros((3, number_roots), jnp.float32)], axis=1
    )
    for position in range(number_roots):
        active = jnp.where(
            position < filter_order,
            root_values[:, position],
            jnp.zeros_like(root_values[:, position]),
        )
        lagged = jnp.concatenate([jnp.zeros_like(coeffs[:, :1]), coeffs[:, :-1]], axis=1)
        coeffs = coeffs - active[:, None] * lagged
    return coeffs


def same_ids(left_ids, right_ids):
    return jnp.where(left_ids == right_ids, 1.0, 0.0).astype(jnp.float32)


def chain_combine(earlier, later):
    first_maps, first_shift = earlier
    second_maps, second_shift = later
    joined_maps = jnp.einsum("cij,cjk->cik", second_maps, first_maps, precision=precise)
    joined_shift = (
        jnp.einsum("cij,rcj->rci", second_maps, first_shift, precision=precise) + second_shift
    )
    return (joined_maps, joined_shift)


def on_device(
    design,
    gap_flags,
    segment_ids,
    ar_order,
    ma_order,
    ar_roots,
    ma_roots,
    kaula,
    precond,
    solution,
    residual,
    direction,
):
    epochs = segment_ids.shape[0]
    columns = design.shape[2]
    share_len = direction.shape[2]
    rhs_count = direction.shape[0]
    ar_coeffs = polynomial(ar_roots, ar_order)
    ma_coeffs = polynomial(ma_roots, ma_order)
    rim_ids = extended_2(segment_ids + 1, ((TM, 0),), PMAX)
    local_ids = rim_ids[PMAX : PMAX + epochs]
    row_grid = lax.broadcasted_iota(jnp.int32, (epochs, epochs), 0)
    col_grid = lax.broadcasted_iota(jnp.int32, (epochs, epochs), 1)
    pair_same = same_ids(local_ids[:, None], local_ids[None, :])
    identity = jnp.eye(epochs, dtype=jnp.float32)
    lower = jnp.broadcast_to(identity, (3, epochs, epochs))
    time_grid = lax.broadcasted_iota(jnp.int32, (epochs, PMAX), 0)
    state_grid = lax.broadcasted_iota(jnp.int32, (epochs, PMAX), 1)
    same_before = same_ids(local_ids[:, None], rim_ids[:PMAX][::-1][None, :])
    same_after = same_ids(local_ids[:, None], rim_ids[PMAX + epochs :][None, :])
    enter_before = jnp.zeros((3, epochs, PMAX), jnp.float32)
    enter_after = jnp.zeros((3, epochs, PMAX), jnp.float32)
    for lag_step in range(1, PMAX + 1):
        lag_weight = ar_coeffs[:, lag_step][:, None, None]
        lower = (
            lower + lag_weight * jnp.where(row_grid - col_grid == lag_step, pair_same, 0.0)[None]
        )
        enter_before = (
            enter_before
            + lag_weight * jnp.where(time_grid + 1 + state_grid == lag_step, same_before, 0.0)[None]
        )
        enter_after = (
            enter_after
            + lag_weight
            * jnp.where(epochs + state_grid - time_grid == lag_step, same_after, 0.0)[None]
        )
    inverse = jax.scipy.linalg.solve_triangular(
        lower, jnp.broadcast_to(identity, (3, epochs, epochs)), lower=True
    )
    from_before = -jnp.einsum("cts,csm->ctm", inverse, enter_before, precision=precise)
    from_after = -jnp.einsum("cst,csm->ctm", inverse, enter_after, precision=precise)
    gaps = gap_flags.astype(jnp.float32)
    ident_maps = jnp.broadcast_to(jnp.eye(PMAX, dtype=jnp.float32), (3, PMAX, PMAX))
    packed = direction.astype(jnp.bfloat16)
    design_flat = design.reshape(3 * epochs, columns)
    partial_obs = lax.dot_general(
        gathered_copies(packed, TM, 2)[:, 0, :],
        design_flat,
        (((1,), (1,)), ((), ())),
        preferred_element_type=jnp.float32,
    )
    partial_obs = partial_obs.reshape(rhs_count, 3, epochs)
    whole_obs = over_copies(partial_obs, ORDER)
    masked = whole_obs * gaps[None, None, :]
    before_vals = shifted(masked[:, :, epochs - QMAX :], TM, 1)
    extended = jnp.concatenate([before_vals, masked], axis=2)
    moving = jnp.zeros_like(masked)
    for lag_step in range(QMAX + 1):
        joined = same_ids(rim_ids[PMAX - lag_step : PMAX - lag_step + epochs], local_ids)
        moving = (
            moving
            + ma_coeffs[:, lag_step][None, :, None]
            * extended[:, :, QMAX - lag_step : QMAX - lag_step + epochs]
            * joined[None, None, :]
        )
    local_fwd = jnp.einsum("cts,rcs->rct", inverse, moving, precision=precise)
    fwd_maps = from_before[:, ::-1, :][:, :PMAX, :]
    fwd_shift = local_fwd[:, :, ::-1][:, :, :PMAX]
    ident_shift = jnp.zeros_like(fwd_shift)
    _, state_in = carried_in((fwd_maps, fwd_shift), TM, chain_combine, (ident_maps, ident_shift))
    filtered = local_fwd + jnp.einsum("ctm,rcm->rct", from_before, state_in, precision=precise)
    local_back = jnp.einsum("cst,rcs->rct", inverse, filtered, precision=precise)
    _, state_back = entering(
        (from_after[:, :PMAX, :], local_back[:, :, :PMAX]),
        TM,
        chain_combine,
        (ident_maps, ident_shift),
    )
    adjoint = local_back + jnp.einsum("ctm,rcm->rct", from_after, state_back, precision=precise)
    after_vals = shifted(adjoint[:, :, :QMAX], TM, -1)
    extended_back = jnp.concatenate([adjoint, after_vals], axis=2)
    moved_back = jnp.zeros_like(adjoint)
    for lag_step in range(QMAX + 1):
        joined = same_ids(local_ids, rim_ids[PMAX + lag_step : PMAX + lag_step + epochs])
        moved_back = (
            moved_back
            + ma_coeffs[:, lag_step][None, :, None]
            * extended_back[:, :, lag_step : lag_step + epochs]
            * joined[None, None, :]
        )
    weighted = (moved_back * gaps[None, None, :]).astype(jnp.bfloat16)
    gradient = lax.dot_general(
        weighted.reshape(rhs_count, 3 * epochs),
        design_flat,
        (((1,), (0,)), ((), ())),
        preferred_element_type=jnp.float32,
    )
    owned = sent_and_summed(gradient, TM, 1)
    image = owned.reshape(rhs_count, 1, share_len) + kaula[None] * direction

    def precondition(vector):
        blocks = precond[0]
        shaped = vector.reshape(rhs_count, blocks.shape[0], blocks.shape[1])
        return jnp.einsum("bij,rbj->rbi", blocks, shaped, precision=precise).reshape(vector.shape)

    applied = precondition(residual)
    image_applied = precondition(image)
    old_rz, curvature, cross_term, image_term = (
        one_axis_at_a_time(jnp.sum(residual * applied, axis=(1, 2)), TM_ORDER),
        one_axis_at_a_time(jnp.sum(direction * image, axis=(1, 2)), TM_ORDER),
        one_axis_at_a_time(jnp.sum(image * applied, axis=(1, 2)), TM_ORDER),
        one_axis_at_a_time(jnp.sum(image * image_applied, axis=(1, 2)), TM_ORDER),
    )
    step_len = old_rz / curvature
    new_solution = solution + step_len[:, None, None] * direction
    new_residual = residual - step_len[:, None, None] * image
    new_applied = applied - step_len[:, None, None] * image_applied
    new_rz = old_rz - 2.0 * step_len * cross_term + step_len * step_len * image_term
    new_direction = new_applied + (new_rz / old_rz)[:, None, None] * direction
    return (new_solution, new_residual, new_direction)


def solution(mesh):
    split = Mesh(mesh.devices.reshape(4, 8, 4, 2), ("tm_0", "tm_1", "order_0", "order_1"))
    in_specs = (
        P(None, TM, ORDER),
        P(TM),
        P(TM),
        P(),
        P(),
        P(),
        P(),
        P(ORDER, TM),
        P(ORDER, TM, None, None),
        P(None, ORDER, TM),
        P(None, ORDER, TM),
        P(None, ORDER, TM),
    )
    out_specs = (P(None, ORDER, TM), P(None, ORDER, TM), P(None, ORDER, TM))
    return jax.shard_map(
        on_device, mesh=split, in_specs=in_specs, out_specs=out_specs, check_vma=False
    )
```

profile of v0, /device:TPU:1, one launch (start us, length us, event | category | flops | bytes accessed | tf_op | source)
XLA Modules:
  0.0 201.7 jit_solution(4728391206816486950)
XLA Ops:
  0.7 0.7 broadcast_add_fusion
  1.5 4.4 %collective-permute-start.1 = (s32[4]{0:T(128)S(1)}, s32[4]{0:T(128)S(1)}, u32[]{:S(2)}, u32[]{:S(2)}) collective-permute-start(s32[4]{0:T(128)S(1)} %get-tuple-element.86), channel_id=1, source_target_pairs={{0,8},{8,16},{16,24},{24,32},{32,40},{40,48},{48,56},{56,64},{64,7... | collective-permute-start | bytes 56 | tf_op jit(solution)/shard_map/ppermute | solution.py:24
  5.8 1.3 collective-permute-start.2
  7.1 0.7 convert_element_type.21
  7.9 0.7 broadcast_in_dim.159
  8.6 12.9 %all-to-all-start = ((bf16[32,16,1,256]{3,1,2,0:T(8,128)(2,1)}), bf16[32,16,1,256]{3,1,2,0:T(8,128)(2,1)S(1)}, u32[]{:S(2)}, u32[]{:S(2)}) async-start(bf16[32,16,1,256]{3,1,2,0:T(8,128)(2,1)} %broadcast_in_dim.159), calls=%async_computation | async-start | bytes 524288 | tf_op jit(solution)/shard_map/all_to_all | solution.py:40
  21.6 1.0 slice_reduce_fusion.4
  22.7 1.1 slice_reduce_fusion
  24.4 0.7 multiply_subtract_fusion.8
  25.1 0.7 multiply_subtract_fusion.7
  25.8 0.7 multiply_subtract_fusion.6
  26.8 29.5 %custom-call.4 = f32[3,1,128,128]{2,3,1,0:T(8,128)S(1)} custom-call(f32[3,1,128,128]{3,2,1,0:T(8,128)S(1)} %add_select_fusion), custom_call_target="InvertDiagBlocksLowerTriangular" | custom-call | tf_op jit(solution)/shard_map/jit(_solve_triangular)/vmap()/triangular_solve | solution.py:220
  57.9 4.5 %fusion.151 = f32[16,3,128]{2,0,1:T(8,128)S(1)} fusion(bf16[16,8192,1]{1,0,2:T(8,128)(2,1)S(1)} %reshape.650, bf16[3,128,8192]{2,1,0:T(8,128)(2,1)} %param.12), kind=kOutput, calls=%fused_computation.270 | convolution fusion | flops 100663296 | bytes 6578176 | tf_op jit(solution)/shard_map/dot_general | solution.py:229
  62.4 0.7 broadcast_in_dim.160
  63.1 5.8 %all-to-all-start.1 = ((f32[8,16,3,128]{3,1,2,0:T(8,128)}), f32[8,16,3,128]{3,1,2,0:T(8,128)S(1)}, u32[]{:S(2)}, u32[]{:S(2)}) async-start(f32[8,16,3,128]{3,1,2,0:T(8,128)} %broadcast_in_dim.160), calls=%async_computation.1 | async-start | bytes 393216 | tf_op jit(solution)/shard_map/all_to_all | solution.py:40
  69.4 5.5 %all-to-all-done.1 = f32[8,16,3,128]{3,1,2,0:T(8,128)S(1)} async-done(((f32[8,16,3,128]{3,1,2,0:T(8,128)}), f32[8,16,3,128]{3,1,2,0:T(8,128)S(1)}, u32[]{:S(2)}, u32[]{:S(2)}) %all-to-all-start.1) | async-done | bytes 196640 | tf_op jit(solution)/shard_map/all_to_all | solution.py:40
  75.0 3.4 %collective-permute-start = (f32[16,3,4]{2,0,1:T(8,128)S(1)}, f32[16,3,4]{2,0,1:T(8,128)S(1)}, u32[]{:S(2)}, u32[]{:S(2)}) collective-permute-start(f32[16,3,4]{2,0,1:T(8,128)S(1)} %slice.405), channel_id=1, source_target_pairs={{0,8},{8,16},{16,24},{24,32},{32,40},{40,48},{48,56},{56,64},{64,7... | collective-permute-start | bytes 2312 | tf_op jit(solution)/shard_map/ppermute | solution.py:35
  80.4 0.7 reshape.662
  81.1 10.9 %all-to-all-start.2 = ((f32[32,1,240]{2,1,0:T(1,128)}), f32[32,1,240]{2,1,0:T(1,128)S(1)}, u32[]{:S(2)}, u32[]{:S(2)}) async-start(f32[32,1,240]{2,1,0:T(1,128)} %reshape.662), calls=%async_computation.2 | async-start | bytes 65536 | tf_op jit(solution)/shard_map/all_to_all | solution.py:40
  92.4 8.4 %all-to-all-done.2 = f32[32,1,240]{2,1,0:T(1,128)S(1)} async-done(((f32[32,1,240]{2,1,0:T(1,128)}), f32[32,1,240]{2,1,0:T(1,128)S(1)}, u32[]{:S(2)}, u32[]{:S(2)}) %all-to-all-start.2) | async-done | bytes 30752 | tf_op jit(solution)/shard_map/all_to_all | solution.py:40
  101.3 0.7 reduce.16
  106.5 11.7 %all_to_all.25 = f32[32,1,240]{2,1,0:T(1,128)S(1)} all-to-all(f32[32,1,240]{2,1,0:T(1,128)S(1)} %reshape.664), channel_id=1, replica_groups=mesh['tm_0'=4,'tm_1'=8,'order_0'=4,'order_1'=2] {'tm_0','tm_1'}, dimensions={0} | all-to-all | bytes 61440 | tf_op jit(solution)/shard_map/all_to_all | solution.py:40
  118.2 0.7 reduce.17
  122.8 1.3 collective-permute-start.3
  124.1 8.7 %copy.70 = bf16[8192,384]{1,0:T(8,128)(2,1)} copy(bf16[8192,384]{0,1:T(8,128)(2,1)} %bitcast.164) | data formatting | bytes 12582912 | tf_op jit(solution)/shard_map/dot_general | solution.py:275
  132.9 5.3 %convolution_bitcast_fusion = f32[32,16,256]{2,1,0:T(8,128)} fusion(bf16[16,384,1]{1,0,2:T(8,128)(2,1)S(1)} %reshape.651, bf16[32,256,384]{2,1,0:T(8,128)(2,1)} %bitcast.165), kind=kOutput, calls=%fused_computation | convolution fusion | flops 100663296 | bytes 6828032 | tf_op jit(solution)/shard_map/dot_general | solution.py:275
  138.3 5.8 %all-to-all-start.4 = ((f32[32,16,256]{2,1,0:T(8,128)}), f32[32,16,256]{2,1,0:T(8,128)S(1)}, u32[]{:S(2)}, u32[]{:S(2)}) async-start(f32[32,16,256]{2,1,0:T(8,128)} %convolution_bitcast_fusion), calls=%async_computation.4 | async-start | bytes 1048576 | tf_op jit(solution)/shard_map/all_to_all | solution.py:135
  144.5 11.1 %all-to-all-done.4 = f32[32,16,256]{2,1,0:T(8,128)S(1)} async-done(((f32[32,16,256]{2,1,0:T(8,128)}), f32[32,16,256]{2,1,0:T(8,128)S(1)}, u32[]{:S(2)}, u32[]{:S(2)}) %all-to-all-start.4) | async-done | bytes 524320 | tf_op jit(solution)/shard_map/all_to_all | solution.py:135
  156.2 7.4 %all-reduce.8 = (f32[16]{0:T(128)S(1)}, f32[16]{0:T(128)S(1)}, f32[16]{0:T(128)S(1)}, f32[16]{0:T(128)S(1)}) all-reduce(f32[16]{0:T(128)S(1)} %get-tuple-element.10, f32[16]{0:T(128)S(1)} %get-tuple-element.12, f32[16]{0:T(128)S(1)} %get-tuple-element.11, ...), channel_id=1, replica_groups=mesh['tm_0'=4,'tm_1'=8,'order_0'=4,'order_1'=2] {'tm_0'}, use_global_device_ids=true, to_apply=%region_1.2 | all-reduce | flops 64 | bytes 512 | tf_op jit(solution)/shard_map/psum | solution.py:140
  163.6 13.1 %all-reduce.6 = (f32[16]{0:T(128)S(1)}, f32[16]{0:T(128)S(1)}, f32[16]{0:T(128)S(1)}, f32[16]{0:T(128)S(1)}) all-reduce(f32[16]{0:T(128)S(1)} %get-tuple-element.29, f32[16]{0:T(128)S(1)} %get-tuple-element.30, f32[16]{0:T(128)S(1)} %get-tuple-element.31, ...), channel_id=1, replica_groups=mesh['tm_0'=4,'tm_1'=8,'order_0'=4,'order_1'=2] {'tm_1'}, use_global_device_ids=true, to_apply=%region_2.3 | all-reduce | flops 64 | bytes 512 | tf_op jit(solution)/shard_map/psum | solution.py:140
  176.7 7.1 %all-reduce.7 = (f32[16]{0:T(128)S(1)}, f32[16]{0:T(128)S(1)}, f32[16]{0:T(128)S(1)}, f32[16]{0:T(128)S(1)}) all-reduce(f32[16]{0:T(128)S(1)} %get-tuple-element.21, f32[16]{0:T(128)S(1)} %get-tuple-element.22, f32[16]{0:T(128)S(1)} %get-tuple-element.23, ...), channel_id=1, replica_groups=mesh['tm_0'=4,'tm_1'=8,'order_0'=4,'order_1'=2] {'order_0'}, use_global_device_ids=true, to_apply=%region_3.4 | all-reduce | flops 64 | bytes 512 | tf_op jit(solution)/shard_map/psum | solution.py:140
  183.8 15.9 %all-reduce.9 = (f32[16]{0:T(128)S(1)}, f32[16]{0:T(128)S(1)}, f32[16]{0:T(128)S(1)}, f32[16]{0:T(128)S(1)}) all-reduce(f32[16]{0:T(128)S(1)} %get-tuple-element.25, f32[16]{0:T(128)S(1)} %get-tuple-element.26, f32[16]{0:T(128)S(1)} %get-tuple-element.27, ...), channel_id=1, replica_groups=mesh['tm_0'=4,'tm_1'=8,'order_0'=4,'order_1'=2] {'order_1'}, use_global_device_ids=true, to_apply=%region_4.5 | all-reduce | flops 64 | bytes 512 | tf_op jit(solution)/shard_map/psum | solution.py:140
  (130 shorter events, 17.1 us)
Async XLA Ops:
  0.6 143.5 %copy-start = (f32[1,2,128,128]{3,2,1,0:T(8,128)S(1)}, f32[1,2,128,128]{3,2,1,0:T(8,128)}, u32[]{:S(2)}) copy-start(f32[1,2,128,128]{3,2,1,0:T(8,128)} %param.20) | copy-start | bytes 393220
  0.6 77.7 %copy-start.5 = (s32[128]{0:T(128)S(1)}, s32[128]{0:T(128)}, u32[]{:S(2)}) copy-start(s32[128]{0:T(128)} %param.14) | copy-start | bytes 1540
  1.5 56.0 %collective-permute-start.1 = (s32[4]{0:T(128)S(1)}, s32[4]{0:T(128)S(1)}, u32[]{:S(2)}, u32[]{:S(2)}) collective-permute-start(s32[4]{0:T(128)S(1)} %get-tuple-element.86), channel_id=1, source_target_pairs={{0,8},{8,16},{16,24},{24,32},{32,40},{40,48},{48,56},{56,64},{64,7... | collective-permute-start | bytes 56 | tf_op jit(solution)/shard_map/ppermute | solution.py:24
  5.8 51.7 %collective-permute-start.2 = (s32[4]{0:T(128)S(1)}, s32[4]{0:T(128)S(1)}, u32[]{:S(2)}, u32[]{:S(2)}) collective-permute-start(s32[4]{0:T(128)S(1)} %get-tuple-element.85), channel_id=1, source_target_pairs={{8,0},{16,8},{24,16},{32,24},{40,32},{48,40},{56,48},{64,56},{72,6... | collective-permute-start | bytes 56 | tf_op jit(solution)/shard_map/ppermute | solution.py:27
  8.6 49.1 %all-to-all-start = ((bf16[32,16,1,256]{3,1,2,0:T(8,128)(2,1)}), bf16[32,16,1,256]{3,1,2,0:T(8,128)(2,1)S(1)}, u32[]{:S(2)}, u32[]{:S(2)}) async-start(bf16[32,16,1,256]{3,1,2,0:T(8,128)(2,1)} %broadcast_in_dim.159), calls=%async_computation | async-start | bytes 524288 | tf_op jit(solution)/shard_map/all_to_all | solution.py:40
  63.1 11.7 %all-to-all-start.1 = ((f32[8,16,3,128]{3,1,2,0:T(8,128)}), f32[8,16,3,128]{3,1,2,0:T(8,128)S(1)}, u32[]{:S(2)}, u32[]{:S(2)}) async-start(f32[8,16,3,128]{3,1,2,0:T(8,128)} %broadcast_in_dim.160), calls=%async_computation.1 | async-start | bytes 393216 | tf_op jit(solution)/shard_map/all_to_all | solution.py:40
  75.0 4.3 %collective-permute-start = (f32[16,3,4]{2,0,1:T(8,128)S(1)}, f32[16,3,4]{2,0,1:T(8,128)S(1)}, u32[]{:S(2)}, u32[]{:S(2)}) collective-permute-start(f32[16,3,4]{2,0,1:T(8,128)S(1)} %slice.405), channel_id=1, source_target_pairs={{0,8},{8,16},{16,24},{24,32},{32,40},{40,48},{48,56},{56,64},{64,7... | collective-permute-start | bytes 2312 | tf_op jit(solution)/shard_map/ppermute | solution.py:35
  81.1 19.7 %all-to-all-start.2 = ((f32[32,1,240]{2,1,0:T(1,128)}), f32[32,1,240]{2,1,0:T(1,128)S(1)}, u32[]{:S(2)}, u32[]{:S(2)}) async-start(f32[32,1,240]{2,1,0:T(1,128)} %reshape.662), calls=%async_computation.2 | async-start | bytes 65536 | tf_op jit(solution)/shard_map/all_to_all | solution.py:40
  122.8 10.0 %collective-permute-start.3 = (f32[16,3,4]{2,0,1:T(8,128)S(1)}, f32[16,3,4]{2,0,1:T(8,128)S(1)}, u32[]{:S(2)}, u32[]{:S(2)}) collective-permute-start(f32[16,3,4]{2,0,1:T(8,128)S(1)} %bitcast.177), channel_id=1, source_target_pairs={{8,0},{16,8},{24,16},{32,24},{40,32},{48,40},{56,48},{64,56},{72,6... | collective-permute-start | bytes 2312 | tf_op jit(solution)/shard_map/ppermute | solution.py:35
  132.7 11.4 %copy-start.2 = (f32[16,1,256]{2,1,0:T(1,128)S(1)}, f32[16,1,256]{2,1,0:T(1,128)}, u32[]{:S(2)}) copy-start(f32[16,1,256]{2,1,0:T(1,128)} %param.22) | copy-start | bytes 49156
  132.7 22.9 %copy-start.1 = (f32[16,1,256]{2,1,0:T(1,128)S(1)}, f32[16,1,256]{2,1,0:T(1,128)}, u32[]{:S(2)}) copy-start(f32[16,1,256]{2,1,0:T(1,128)} %param.23) | copy-start | bytes 49156
  132.7 22.9 %copy-start.4 = (f32[1,256]{1,0:T(1,128)S(1)}, f32[1,256]{1,0:T(1,128)}, u32[]{:S(2)}) copy-start(f32[1,256]{1,0:T(1,128)} %param.19) | copy-start | bytes 3076
  132.7 67.1 %copy-start.3 = (f32[16,1,256]{2,1,0:T(1,128)S(1)}, f32[16,1,256]{2,1,0:T(1,128)}, u32[]{:S(2)}) copy-start(f32[16,1,256]{2,1,0:T(1,128)} %param.21) | copy-start | bytes 49156
  138.3 17.3 %all-to-all-start.4 = ((f32[32,16,256]{2,1,0:T(8,128)}), f32[32,16,256]{2,1,0:T(8,128)S(1)}, u32[]{:S(2)}, u32[]{:S(2)}) async-start(f32[32,16,256]{2,1,0:T(8,128)} %convolution_bitcast_fusion), calls=%async_computation.4 | async-start | bytes 1048576 | tf_op jit(solution)/shard_map/all_to_all | solution.py:135
where the time goes:
time: 203 us; the launch traced here: 202 us
  blocking collectives  55.2 us (27%)
  starting transfers between devices  45.8 us (23%)
  other arithmetic  37.4 us (18%)
  waiting for transfers between devices  25.5 us (13%)
  local copies, waits for them, and re-layouts  18.7 us (9%)
  matrix products  17.7 us (9%)
    psum x4, blocking collectives, one_axis_at_a_time(): return functools.reduce(lax.psum, axes, value)  43.6 us
    another operation x3, other arithmetic, on_device(): jax.scipy.linalg.solve_triangular(lower, jnp.broadcast_to(identity, (3, e...  29.7 us
    all_to_all x3, starting transfers between devices, copy_for_each(): return lax.all_to_all(copies, axis, split_axis=0, concat_axis=0, tiled=True)  29.6 us
    all_to_all x3, waiting for transfers between devices, copy_for_each(): return lax.all_to_all(copies, axis, split_axis=0, concat_axis=0, tiled=True)  13.8 us
    all_to_all x1, blocking collectives, copy_for_each(): return lax.all_to_all(copies, axis, split_axis=0, concat_axis=0, tiled=True)  11.7 us
    all_to_all x1, waiting for transfers between devices, sent_and_summed(): lax.all_to_all(parts, axis, split_axis=0, concat_axis=0, tiled=True)  11.1 us
    dot_general x1, local copies, waits for them, and re-layouts, on_device(): lax.dot_general(weighted.reshape(rhs_count, 3 * epochs), design_flat, (((...  8.67 us
    all_to_all x1, starting transfers between devices, sent_and_summed(): lax.all_to_all(parts, axis, split_axis=0, concat_axis=0, tiled=True)  5.84 us
  transfers between devices with their start and end apart: 8, of which 4 were waited for; matrix products, arithmetic and copies ran while one was open for 24% of the time, Pallas kernels for 0%

commit v1 on v0

v1 whole, which is shorter than its diff:
```python
import jax
import jax.numpy as jnp
from jax import lax
from jax.experimental import pallas as pl
from jax.experimental.pallas import tpu as pltpu
from jax.sharding import Mesh
from jax.sharding import PartitionSpec as P

TM = ("tm_0", "tm_1")
ORDER = ("order_0", "order_1")
TM_ORDER = TM + ORDER
CHUNKS = 8
VMEM_LIMIT = 32 * 1024 * 1024

precise = lax.Precision.HIGHEST
LEVELS = 12
RADIX = 7


def dot(a, b, dims):
    return lax.dot_general(
        a, b, (dims, ((), ())), precision=precise, preferred_element_type=jnp.float32
    )


def splat_rows(read):
    row = lax.broadcasted_iota(jnp.int32, (8, 128), 0)
    out = jnp.zeros((8, 128), jnp.float32)
    for c in range(3):
        out = jnp.where(row == c, read(c), out)
    return out


LOWER = [(i, j) for i in range(4) for j in range(i + 1)]
UPPER = [(i, j) for i in range(4) for j in range(i, 4)]


def active_roots(roots_ref, order_ref):
    return [
        splat_rows(lambda c: jnp.where(k < order_ref[c], roots_ref[c, k], jnp.float32(0.0)))
        for k in range(4)
    ]


def sum_of(terms):
    while len(terms) > 1:
        terms = [
            terms[k] + terms[k + 1] if k + 1 < len(terms) else terms[k]
            for k in range(0, len(terms), 2)
        ]
    return terms[0]


def times(left, right):
    return {
        (i, j): sum_of([left[i, k] * right[k, j] for k in range(j, i + 1)]) for i, j in LOWER
    }


def gram_step(gram, power):
    half = {
        (i, j): sum_of([gram[min(i, k), max(i, k)] * power[k, j] for k in range(j, 4)])
        for i in range(4)
        for j in range(4)
    }
    return {(i, j): sum_of([power[k, i] * half[k, j] for k in range(i, 4)]) for i, j in UPPER}


def row_times(vector, power):
    return [sum_of([vector[i] * power[i, j] for i in range(j, 4)]) for j in range(4)]


def row_power(vector, powers, number, bits):
    for k in range(bits):
        on = ((number >> k) & 1) == 1
        moved = row_times(vector, powers[k])
        vector = [jnp.where(on, moved[j], vector[j]) for j in range(4)]
    return vector


def column_power(vector, powers, number, bits):
    for k in range(bits):
        on = ((number >> k) & 1) == 1
        moved = [sum_of([powers[k][i, j] * vector[j] for j in range(i + 1)]) for i in range(4)]
        vector = [jnp.where(on, moved[i], vector[i]) for i in range(4)]
    return vector


def response_kernel(
    place_ref, aro_ref, mao_ref, arr_ref, mar_ref, toep_ref, gam_ref, fin_ref, reach_ref, pow_ref, gram_ref
):
    poles = active_roots(arr_ref, aro_ref)
    zeros = active_roots(mar_ref, mao_ref)
    kappa = [poles[j] - zeros[j] for j in range(4)]
    one = jnp.ones((8, 128), jnp.float32)
    powers = [{(i, j): poles[i] if i == j else kappa[j] for i, j in LOWER}]
    for _ in range(LEVELS - 1):
        powers.append(times(powers[-1], powers[-1]))
    gram = {(i, j): kappa[i] * kappa[j] for i, j in UPPER}
    for k in range(LEVELS - 1):
        for at, (i, j) in enumerate(LOWER):
            pow_ref[k, at] = powers[k][i, j]
        for at, (i, j) in enumerate(UPPER):
            gram_ref[k, at] = gram[i, j]
        if k < LEVELS - 2:
            add = gram_step(gram, powers[k])
            gram = {at: gram[at] + add[at] for at in UPPER}
    lane = lax.broadcasted_iota(jnp.int32, (8, 128), 1)
    gam = row_power(kappa, powers, lane, RADIX)
    fin = column_power([one] * 4, powers, 127 - lane, RADIX)
    for i in range(4):
        gam_ref[i] = gam[i]
        fin_ref[i] = fin[i]
    eta = jnp.where(lane == 0, 1.0, pltpu.roll(sum_of(gam), 1, 1))
    big_row = lax.broadcasted_iota(jnp.int32, (128, 128), 0)
    big_lane = lax.broadcasted_iota(jnp.int32, (128, 128), 1)
    for c in range(3):
        base = jnp.broadcast_to(eta[c : c + 1, :], (128, 128))
        turned = pltpu.roll(base, 0, 1, stride=1, stride_axis=0)
        toep_ref[c] = jnp.where(big_lane >= big_row, turned, 0.0)
    place = place_ref[0, 0]
    row = lax.broadcasted_iota(jnp.int32, (8, 128), 0)
    front = row < 4
    for side in range(2):
        wide = lane + 128 * side
        peer, kind = wide >> 3, wide & 7
        gap = jnp.where(front, place - 1 - peer, peer - 1 - place)
        steps = jnp.maximum(gap, 0)
        for c in range(3):
            vector = [jnp.where((row & 3) == j, 1.0, 0.0) for j in range(4)]
            for k in range(5):
                cut = {at: powers[RADIX + k][at][c : c + 1, :] for at in LOWER}
                on = ((steps >> k) & 1) == 1
                moved = []
                for j in range(4):
                    terms = [vector[j] * cut[j, j]]
                    for i in range(4):
                        if i > j:
                            terms.append(vector[i] * jnp.where(front, cut[i, j], 0.0))
                        if i < j:
                            terms.append(vector[i] * jnp.where(front, 0.0, cut[j, i]))
                    moved.append(sum_of(terms))
                vector = [jnp.where(on, moved[j], vector[j]) for j in range(4)]
            picked = jnp.zeros((8, 128), jnp.float32)
            for j in range(4):
                picked = jnp.where((kind & 3) == j, vector[j], picked)
            used = ((kind < 4) == front) & (gap >= 0)
            reach_ref[c, :, 128 * side : 128 * side + 128] = jnp.where(used, picked, 0.0)


def segment_kernel(
    place_ref, got_ref, toep_ref, gam_ref, fin_ref, reach_ref, pow_ref, gram_ref, own_ref, near_ref, far_ref
):
    place = place_ref[0, 0]
    ids = got_ref[:, 32:40, :].astype(jnp.float32)
    peer = lax.broadcasted_iota(jnp.int32, (32, 8, 128), 0)
    mine = jnp.sum(jnp.where(peer == place, ids, 0.0), axis=0)
    before = jnp.sum(jnp.where(peer == place - 1, ids, 0.0), axis=0)
    ends = jnp.broadcast_to(ids[:, :, 127:128], (32, 8, 128))
    last = jnp.broadcast_to(mine[:, 127:128], (8, 128))
    prev = jnp.where(place > 0, jnp.broadcast_to(before[:, 127:128], (8, 128)), -1.0)
    count = jnp.sum(jnp.where((peer > place) & (ids == last[None]), 1.0, 0.0), axis=0)
    left = jnp.broadcast_to(jnp.sum(count, axis=1, keepdims=True), (8, 128)).astype(jnp.int32)
    ends_before = jnp.concatenate([ends[:1], ends[:-1]], axis=0)
    sub = lax.broadcasted_iota(jnp.int32, (32, 8, 128), 1)
    keep = jnp.where(
        sub < 4,
        jnp.where((peer < place) & (ends == prev[None]), 1.0, 0.0),
        jnp.where((peer > place) & (ends_before == last[None]), 1.0, 0.0),
    ).reshape(256, 128)
    gram = {at: jnp.zeros((8, 128), jnp.float32) for at in UPPER}
    for k in range(LEVELS - 1):
        power = {pair: pow_ref[k, at] for at, pair in enumerate(LOWER)}
        add = gram_step(gram, power)
        on = ((left >> k) & 1) == 1
        gram = {
            pair: jnp.where(on, gram_ref[k, at] + add[pair], gram[pair])
            for at, pair in enumerate(UPPER)
        }
    lead = jnp.where(mine == prev, 1.0, 0.0)
    trail = jnp.where(mine == last, 1.0, 0.0)
    cont = jnp.where(last == prev, 1.0, 0.0)
    fin = [fin_ref[i] * trail for i in range(4)]
    gam = [gam_ref[i] * lead for i in range(4)]
    fold = [
        sum_of([fin[j] * gram[min(i, j), max(i, j)] for j in range(4)]) for i in range(4)
    ]
    block = {pair: pow_ref[RADIX, at] for at, pair in enumerate(LOWER)}
    past = [cont * value for value in row_times(fold, block)]
    row = lax.broadcasted_iota(jnp.int32, (8, 128), 0)
    big_row = lax.broadcasted_iota(jnp.int32, (128, 128), 0)
    big_lane = lax.broadcasted_iota(jnp.int32, (128, 128), 1)
    wide = jnp.broadcast_to(mine[0:1, :], (128, 128))
    tall = jnp.sum(jnp.where(big_row == big_lane, wide, 0.0), axis=1, keepdims=True)
    same = wide == jnp.broadcast_to(tall, (128, 128))

    def rows(values, c, start):
        out = jnp.zeros((8, 128), jnp.float32)
        for i in range(4):
            out = jnp.where(row == start + i, values[i][c : c + 1, :], out)
        return out

    for c in range(3):
        toep = jnp.where(same, toep_ref[c], 0.0)
        probe = dot(rows(gam, c, 0), toep, ((1,), (1,)))
        out_p = jnp.where(row < 4, probe, 0.0) + rows(past, c, 0)
        fin_low = rows(fin, c, 0)
        near_ref[c] = dot(toep, toep, ((1,), (1,))) + dot(rows(fold, c, 0), fin_low, ((0,), (0,)))
        own_ref[c] = fin_low + pltpu.roll(out_p, 4, 0)
        far_ref[c] = keep * dot(reach_ref[c], out_p + rows(fin, c, 4), ((0,), (0,)))


def state_kernel(parts_ref, gaps_ref, own_ref, message_ref, masked_ref):
    total = parts_ref[0]
    for o in range(1, parts_ref.shape[0]):
        total = total + parts_ref[o]
    gaps = gaps_ref[...].astype(jnp.float32)
    masked = jnp.concatenate([total[:, 128 * c : 128 * c + 128] * gaps for c in range(3)], axis=0)
    masked_ref[...] = masked
    padded = jnp.concatenate([masked, jnp.zeros((80, 128), jnp.float32)], axis=0)
    lane = lax.broadcasted_iota(jnp.int32, (8, 128), 1)
    out = jnp.zeros((8, 128), jnp.float32)
    for c in range(3):
        out = jnp.where((lane >> 4) == c, dot(own_ref[c], padded, ((1,), (1,))), out)
    message_ref[...] = jnp.broadcast_to(out[None], message_ref.shape)


def weighted_rows(masked_ref, near_ref, far_ref, gaps_ref, states_ref):
    gaps = gaps_ref[...].astype(jnp.float32)
    states = states_ref[...].reshape(256, 128)
    pieces = []
    for c in range(3):
        here = dot(masked_ref[16 * c : 16 * c + 16, :], near_ref[c], ((1,), (0,)))
        there = dot(states, far_ref[c], ((0,), (0,)))[16 * c : 16 * c + 16, :]
        pieces.append((here + there) * gaps)
    return pieces


def pack_kernel(direction_ref, ids_ref, out_ref):
    packed = direction_ref[:, 0, :].astype(jnp.bfloat16)
    ids = jnp.broadcast_to(ids_ref[...].astype(jnp.float32), (8, 128)).astype(jnp.bfloat16)
    sheet = jnp.concatenate([packed[:, :128], packed[:, 128:], ids], axis=0)
    out_ref[...] = jnp.broadcast_to(sheet[None], out_ref.shape)


def chunk_copies(design_ref, held_ref, sems):
    width = held_ref.shape[3]
    return [
        pltpu.make_async_copy(
            design_ref.at[:, :, pl.ds(width * k, width)], held_ref.at[k], sems.at[k]
        )
        for k in range(held_ref.shape[0])
    ]


def observe_kernel(got_ref, design_ref, out_ref, held_ref, sems):
    copies = chunk_copies(design_ref, held_ref, sems)
    for copy in copies:
        copy.start()
    count, _, _, width = held_ref.shape
    peers = width // 256
    total = jnp.zeros((384, 128), jnp.float32)
    for k in range(count):
        pieces = []
        for p in range(peers * k, peers * k + peers):
            pieces += [got_ref[p, 0:16, :], got_ref[p, 16:32, :]]
        packed = jnp.concatenate(pieces, axis=1)
        packed = jnp.concatenate([packed, jnp.zeros((112, width), jnp.bfloat16)], axis=0)
        copies[k].wait()
        total = total + lax.dot_general(
            held_ref[k].reshape(384, width),
            packed,
            (((1,), (1,)), ((), ())),
            preferred_element_type=jnp.float32,
        )
    out_ref[...] = jnp.broadcast_to(total.T[None, 0:16, :], out_ref.shape)


def gradient_kernel(
    masked_ref, near_ref, far_ref, gaps_ref, states_ref, design_ref, out_ref, held_ref, sems
):
    copies = chunk_copies(design_ref, held_ref, sems)
    for copy in copies:
        copy.start()
    pieces = weighted_rows(masked_ref, near_ref, far_ref, gaps_ref, states_ref)
    weighted = jnp.concatenate(pieces, axis=1).astype(jnp.bfloat16)
    count, _, _, width = held_ref.shape
    peers = width // 256
    for k in range(count):
        copies[k].wait()
        part = jnp.dot(
            weighted, held_ref[k].reshape(384, width), preferred_element_type=jnp.float32
        ).astype(jnp.bfloat16)
        for p in range(peers):
            out_ref[peers * k + p] = part[:, 256 * p : 256 * p + 256]


def image_kernel(
    arrived_ref, kaula_ref, precond_ref, residual_ref, direction_ref, message_ref, image_ref, applied_ref, both_ref
):
    total = arrived_ref[0].astype(jnp.float32)
    for p in range(1, arrived_ref.shape[0]):
        total = total + arrived_ref[p].astype(jnp.float32)
    direction = direction_ref[:, 0, :]
    residual = residual_ref[:, 0, :]
    image = total + kaula_ref[...] * direction
    stack = jnp.concatenate([residual, image], axis=0)
    mixed = jnp.concatenate(
        [dot(stack[:, 128 * k : 128 * k + 128], precond_ref[0, k], ((1,), (1,))) for k in range(2)],
        axis=1,
    )
    applied, image_applied = mixed[0:16], mixed[16:32]
    products = jnp.concatenate(
        [
            residual * applied,
            direction * image,
            image * applied,
            image * image_applied,
            jnp.zeros((64, 256), jnp.float32),
        ],
        axis=0,
    )
    sums = dot(jnp.ones((8, 256), jnp.float32), products, ((1,), (1,)))
    message_ref[...] = jnp.broadcast_to(sums[None, 0:1, :], message_ref.shape)
    image_ref[...] = image
    applied_ref[...] = applied
    both_ref[...] = image_applied


def update_kernel(
    sums_ref, image_ref, applied_ref, both_ref, solution_ref, residual_ref, direction_ref, sol_ref, res_ref, dir_ref
):
    total = jnp.sum(sums_ref[...], axis=0)
    row = lax.broadcasted_iota(jnp.int32, (16, 128), 0)
    lane = lax.broadcasted_iota(jnp.int32, (16, 128), 1)
    wide = jnp.broadcast_to(total, (16, 128))
    old_rz, curvature, cross, square = [
        jnp.sum(jnp.where(lane == row + 16 * k, wide, 0.0), axis=1, keepdims=True)
        for k in range(4)
    ]
    step = old_rz / curvature
    new_rz = old_rz - 2.0 * step * cross + step * step * square
    direction = direction_ref[:, 0, :]
    fresh = applied_ref[...] - step * both_ref[...] + (new_rz / old_rz) * direction
    sol_ref[:, 0, :] = solution_ref[:, 0, :] + step * direction
    res_ref[:, 0, :] = residual_ref[:, 0, :] - step * image_ref[...]
    dir_ref[:, 0, :] = fresh


def run(kernel, outs, args, scalars=(), anywhere=(), scratch=(), flops=100000, limit=None):
    spaces = [
        pltpu.SMEM if i in scalars else pl.ANY if i in anywhere else pltpu.VMEM
        for i in range(len(args))
    ]
    shapes = [jax.ShapeDtypeStruct(*out) for out in outs]
    found = pl.pallas_call(
        kernel,
        out_shape=shapes,
        in_specs=[pl.BlockSpec(memory_space=space) for space in spaces],
        out_specs=[pl.BlockSpec(memory_space=pltpu.VMEM) for _ in shapes],
        scratch_shapes=list(scratch),
        cost_estimate=pl.CostEstimate(flops=flops, bytes_accessed=1000000, transcendentals=0),
        compiler_params=pltpu.CompilerParams(vmem_limit_bytes=limit),
    )(*args)
    return found


def exchange(value, axes):
    return lax.all_to_all(value, axes, split_axis=0, concat_axis=0, tiled=True)


def on_device(
    design,
    gap_flags,
    segment_ids,
    ar_order,
    ma_order,
    ar_roots,
    ma_roots,
    kaula,
    precond,
    solution,
    residual,
    direction,
):
    f32, bf16 = jnp.float32, jnp.bfloat16
    count = lax.axis_size(TM)
    others = lax.axis_size(ORDER)
    everyone = count * others
    place = lax.axis_index(TM).astype(jnp.int32).reshape(1, 1)
    gaps = gap_flags.reshape(1, 128)
    (sheets,) = run(
        pack_kernel, [((count, 40, 128), bf16)], [direction, segment_ids.reshape(1, 128)]
    )
    tables = run(
        response_kernel,
        [
            ((3, 128, 128), f32),
            ((4, 8, 128), f32),
            ((4, 8, 128), f32),
            ((3, 8, 256), f32),
            ((LEVELS - 1, 10, 8, 128), f32),
            ((LEVELS - 1, 10, 8, 128), f32),
        ],
        [place, ar_order, ma_order, ar_roots, ma_roots],
        scalars=(0, 1, 2, 3, 4),
        flops=10000000,
    )
    got = exchange(sheets, TM)
    held = [
        pltpu.VMEM((CHUNKS, 3, 128, design.shape[2] // CHUNKS), bf16),
        pltpu.SemaphoreType.DMA((CHUNKS,)),
    ]
    (partial,) = run(
        observe_kernel,
        [((others, 16, 384), f32)],
        [got, design],
        anywhere=(1,),
        scratch=held,
        limit=VMEM_LIMIT,
    )
    parts = exchange(partial, ORDER)
    own, near, far = run(
        segment_kernel,
        [((3, 8, 128), f32), ((3, 128, 128), f32), ((3, 256, 128), f32)],
        [place, got, *tables],
        scalars=(0,),
        flops=10000000,
    )
    message, masked = run(
        state_kernel, [((count, 8, 128), f32), ((48, 128), f32)], [parts, gaps, own]
    )
    states = exchange(message, TM)
    (gradient,) = run(
        gradient_kernel,
        [((count, 16, 256), bf16)],
        [masked, near, far, gaps, states, design],
        anywhere=(5,),
        scratch=held,
        limit=VMEM_LIMIT,
    )
    arrived = exchange(gradient, TM)
    sums, image, applied, image_applied = run(
        image_kernel,
        [((everyone, 1, 128), f32)] + [((16, 256), f32)] * 3,
        [arrived, kaula, precond, residual, direction],
    )
    gathered = exchange(sums, TM_ORDER)
    return tuple(
        run(
            update_kernel,
            [((16, 1, 256), f32)] * 3,
            [gathered, image, applied, image_applied, solution, residual, direction],
        )
    )


def solution(mesh):
    split = Mesh(mesh.devices.reshape(4, 8, 4, 2), TM_ORDER)
    in_specs = (
        P(None, TM, ORDER),
        P(TM),
        P(TM),
        P(),
        P(),
        P(),
        P(),
        P(ORDER, TM),
        P(ORDER, TM, None, None),
        P(None, ORDER, TM),
        P(None, ORDER, TM),
        P(None, ORDER, TM),
    )
    out_specs = (P(None, ORDER, TM),) * 3
    return jax.shard_map(
        on_device, mesh=split, in_specs=in_specs, out_specs=out_specs, check_vma=False
    )
```

time: 203 us -> 115 us (0.57)
  other arithmetic: 37.4 us -> 0 us
  starting transfers between devices: 45.8 us -> 8.65 us
  waiting for transfers between devices: 25.5 us -> 0.01 us
  Pallas kernels: 0 us -> 21.9 us
  blocking collectives: 55.2 us -> 73.9 us
  matrix products: 17.7 us -> 0 us
  local copies, waits for them, and re-layouts: 18.7 us -> 8.91 us
    all_to_all x1 -> x4, blocking collectives: 11.7 us -> 73.9 us  [exchange(): return lax.all_to_all(value, axes, split_axis=0, concat_axis=0, tiled=True)]
    psum x4 -> x0, blocking collectives: 43.6 us -> none  [one_axis_at_a_time(): return functools.reduce(lax.psum, axes, value)]
    another operation x3 -> x0, other arithmetic: 29.7 us -> none  [on_device(): jax.scipy.linalg.solve_triangular(lower, jnp.broadcast_to(identity, (3, e...]
    all_to_all x4 -> x1, starting transfers between devices: 35.5 us -> 8.65 us  [exchange(): return lax.all_to_all(value, axes, split_axis=0, concat_axis=0, tiled=True)]
    all_to_all x4 -> x1, waiting for transfers between devices: 24.9 us -> 0.01 us  [exchange(): return lax.all_to_all(value, axes, split_axis=0, concat_axis=0, tiled=True)]
    pallas_call x0 -> x8, Pallas kernels: none -> 21.9 us  [run(): pl.pallas_call(kernel, out_shape=shapes, in_specs=[pl.BlockSpec(memory_sp...]
    dot_general x26 -> x0, matrix products: 17 us -> none  [the longest x1 5.34 us: on_device(): lax.dot_general(weighted.reshape(rhs_count, 3 * epochs), design_flat, (((...]
    ppermute x4 -> x0, starting transfers between devices: 10.3 us -> none  [the longest x2 4.7 us: shifted(): return lax.ppermute(block, axis, route)]
  transfers between devices with their start and end apart: 8 -> 1, of which waited for: 4 -> 0; matrix products, arithmetic and copies ran while one was open for 24% -> 0% of each run, Pallas kernels for 0% -> 5%
where the time goes in v1:
time: 115 us; the launch traced here: 114 us
  blocking collectives  73.9 us (64%)
  Pallas kernels  21.9 us (19%)
  local copies, waits for them, and re-layouts  8.91 us (8%)
  starting transfers between devices  8.65 us (8%)
    all_to_all x4, blocking collectives, exchange(): return lax.all_to_all(value, axes, split_axis=0, concat_axis=0, tiled=True)  73.9 us
    pallas_call x8, Pallas kernels, run(): pl.pallas_call(kernel, out_shape=shapes, in_specs=[pl.BlockSpec(memory_sp...  21.9 us
    unnamed x16, local copies, waits for them, and re-layouts  8.91 us
    all_to_all x1, starting transfers between devices, exchange(): return lax.all_to_all(value, axes, split_axis=0, concat_axis=0, tiled=True)  8.65 us
  transfers between devices with their start and end apart: 1, of which 0 were waited for; matrix products, arithmetic and copies ran while one was open for 0% of the time, Pallas kernels for 5%

profile of v1, /device:TPU:1, one launch (start us, length us, event | category | flops | bytes accessed | tf_op | source)
XLA Modules:
  0.0 114.0 jit_solution(8016259517003638041)
XLA Ops:
  0.6 0.0 copy-start.6
  0.6 1.5 %shard_map.139 = bf16[32,40,128]{2,1,0:T(8,128)(2,1)} custom-call(f32[16,1,256]{2,1,0:T(1,128)} %direction_ref.5, s32[1,128]{1,0:T(1,128)} %bitcast.5), custom_call_target="tpu_custom_call" | custom-call | flops 100000 | bytes 1000000 | tf_op jit(solution)/shard_map/pallas_call | solution.py:356
  2.1 22.2 %all_to_all.25.got_ref = bf16[32,40,128]{2,1,0:T(8,128)(2,1)S(1)} all-to-all(bf16[32,40,128]{2,1,0:T(8,128)(2,1)} %shard_map.139), channel_id=1, replica_groups=mesh['tm_0'=4,'tm_1'=8,'order_0'=4,'order_1'=2] {'tm_0','tm_1'}, dimensions={0} | all-to-all | bytes 655360 | tf_op jit(solution)/shard_map/all_to_all | solution.py:369
  24.3 0.0 copy-start
  24.3 2.8 %copy-done = bf16[3,128,8192]{2,1,0:T(8,128)(2,1)S(1)} copy-done((bf16[3,128,8192]{2,1,0:T(8,128)(2,1)S(1)}, bf16[3,128,8192]{2,1,0:T(8,128)(2,1)}, u32[]{:S(2)}) %copy-start) | copy-done | bytes 6291480
  27.1 0.0 copy-start.2
  27.1 4.9 %shard_map.140 = f32[8,16,384]{2,1,0:T(8,128)} custom-call(bf16[32,40,128]{2,1,0:T(8,128)(2,1)S(1)} %all_to_all.25.got_ref, bf16[3,128,8192]{2,1,0:T(8,128)(2,1)S(1)} %copy-done), custom_call_target="tpu_custom_call" | custom-call | flops 100000 | bytes 1000000 | tf_op jit(solution)/shard_map/pallas_call | solution.py:356
  32.0 8.6 %all-to-all-start.1 = ((f32[8,16,384]{2,1,0:T(8,128)}), f32[8,16,384]{2,1,0:T(8,128)S(1)}, u32[]{:S(2)}, u32[]{:S(2)}) async-start(f32[8,16,384]{2,1,0:T(8,128)} %shard_map.140), calls=%async_computation.1 | async-start | bytes 393216 | tf_op jit(solution)/shard_map/all_to_all | solution.py:369
  40.7 2.1 %shard_map.141 = (f32[3,128,128]{2,1,0:T(8,128)}, f32[4,8,128]{2,1,0:T(8,128)}, f32[4,8,128]{2,1,0:T(8,128)}, f32[3,8,256]{2,1,0:T(8,128)}, f32[11,10,8,128]{3,2,1,0:T(8,128)}, /*index=5*/f32[11,10,8,128]{3,2,1,0:T(8,128)}) custom-call(s32[1,1]{1,0:T(1,128)} %bitcast.2.place_ref, s32[3]{0:T(128)} %aro_ref.1, s32[3]{0:T(128)} %mao_ref.1, f32[3,4]{1,0:T(4,128)} %arr_ref.1, ...), custom_call_target="tpu_custom_call" | custom-call | flops 10000000 | bytes 1000000 | tf_op jit(solution)/shard_map/pallas_call | solution.py:356
  42.8 0.0 copy-done.2
  42.8 4.1 %shard_map.142 = (f32[3,8,128]{2,1,0:T(8,128)}, f32[3,128,128]{2,1,0:T(8,128)}, f32[3,256,128]{2,1,0:T(8,128)}) custom-call(s32[1,1]{1,0:T(1,128)} %bitcast.2.place_ref, bf16[32,40,128]{2,1,0:T(8,128)(2,1)} %copy-done.2, f32[3,128,128]{2,1,0:T(8,128)} %get-tuple-element.18.toep_ref, f32[4,8,128]{2,1,0:T(8,128)} %get-tuple-element.19.gam_ref, ...), custom_call_target="tpu_custom_call" | custom-call | flops 10000000 | bytes 1000000 | tf_op jit(solution)/shard_map/pallas_call | solution.py:356
  46.9 0.0 all-to-all-done.1.parts_ref
  46.9 0.0 copy-start.7
  46.9 0.7 copy-done.7
  47.6 1.8 %shard_map.143 = (f32[32,8,128]{2,1,0:T(8,128)}, f32[48,128]{1,0:T(8,128)}) custom-call(f32[8,16,384]{2,1,0:T(8,128)} %copy-done.7, s32[1,128]{1,0:T(1,128)} %bitcast.3, f32[3,8,128]{2,1,0:T(8,128)} %get-tuple-element.24.own_ref), custom_call_target="tpu_custom_call" | custom-call | flops 100000 | bytes 1000000 | tf_op jit(solution)/shard_map/pallas_call | solution.py:356
  49.5 13.7 %all_to_all.26.states_ref = f32[32,8,128]{2,1,0:T(8,128)S(1)} all-to-all(f32[32,8,128]{2,1,0:T(8,128)} %get-tuple-element.28), channel_id=1, replica_groups=mesh['tm_0'=4,'tm_1'=8,'order_0'=4,'order_1'=2] {'tm_0','tm_1'}, dimensions={0} | all-to-all | bytes 262144 | tf_op jit(solution)/shard_map/all_to_all | solution.py:369
  63.1 0.0 copy-done.6
  63.1 0.0 copy-start.1
  63.1 2.8 %copy-done.1 = bf16[3,128,8192]{2,1,0:T(8,128)(2,1)S(1)} copy-done((bf16[3,128,8192]{2,1,0:T(8,128)(2,1)S(1)}, bf16[3,128,8192]{2,1,0:T(8,128)(2,1)}, u32[]{:S(2)}) %copy-start.1) | copy-done | bytes 6291480
  65.9 0.0 copy-start.3
  65.9 1.0 copy-done.3
  66.9 0.0 copy-start.4
  66.9 0.9 copy-done.4
  67.8 0.0 copy-start.5
  67.8 0.7 copy-done.5
  68.6 3.2 %shard_map.144 = bf16[32,16,256]{2,1,0:T(8,128)(2,1)S(1)} custom-call(f32[48,128]{1,0:T(8,128)S(1)} %copy-done.5, f32[3,128,128]{2,1,0:T(8,128)S(1)} %copy-done.4, f32[3,256,128]{2,1,0:T(8,128)S(1)} %copy-done.3, s32[1,128]{1,0:T(1,128)S(1)} %bitcast.4, f32[32,8,128]{2,1,0:T(8,128)S(1)} %all_to_all.26.states_ref, bf16[3,128,8192]{2,1,0:T(8,128)(2,1)S(1)} %copy-done.1), custom_call_target="tpu_custom_call" | custom-call | flops 100000 | bytes 1000000 | tf_op jit(solution)/shard_map/pallas_call | solution.py:356
  71.8 13.4 %all_to_all.27.arrived_ref = bf16[32,16,256]{2,1,0:T(8,128)(2,1)} all-to-all(bf16[32,16,256]{2,1,0:T(8,128)(2,1)S(1)} %shard_map.144), channel_id=1, replica_groups=mesh['tm_0'=4,'tm_1'=8,'order_0'=4,'order_1'=2] {'tm_0','tm_1'}, dimensions={0} | all-to-all | bytes 524288 | tf_op jit(solution)/shard_map/all_to_all | solution.py:369
  85.2 2.3 %shard_map.145 = (f32[256,1,128]{2,1,0:T(1,128)}, f32[16,256]{1,0:T(8,128)}, f32[16,256]{1,0:T(8,128)}, f32[16,256]{1,0:T(8,128)}) custom-call(bf16[32,16,256]{2,1,0:T(8,128)(2,1)} %all_to_all.27.arrived_ref, f32[1,256]{1,0:T(1,128)} %kaula_ref.1, f32[1,2,128,128]{3,2,1,0:T(8,128)} %precond_ref.1, f32[16,1,256]{2,1,0:T(1,128)} %residual_ref.3, ...), custom_call_target="tpu_custom_call" | custom-call | flops 100000 | bytes 1000000 | tf_op jit(solution)/shard_map/pallas_call | solution.py:356
  87.5 24.6 %all_to_all.28.sums_ref = f32[256,1,128]{2,1,0:T(1,128)} all-to-all(f32[256,1,128]{2,1,0:T(1,128)} %get-tuple-element.29), channel_id=1, replica_groups=mesh['tm_0'=4,'tm_1'=8,'order_0'=4,'order_1'=2] {'tm_0','tm_1','order_0'..., dimensions={0} | all-to-all | bytes 262144 | tf_op jit(solution)/shard_map/all_to_all | solution.py:369
  112.1 1.9 %shard_map.146 = (f32[16,1,256]{2,1,0:T(1,128)}, f32[16,1,256]{2,1,0:T(1,128)}, f32[16,1,256]{2,1,0:T(1,128)}) custom-call(f32[256,1,128]{2,1,0:T(1,128)} %all_to_all.28.sums_ref, f32[16,256]{1,0:T(8,128)} %get-tuple-element.30.image_ref, f32[16,256]{1,0:T(8,128)} %get-tuple-element.31.applied_ref, f32[16,256]{1,0:T(8,128)} %get-tuple-element.32.both_ref, ...), custom_call_target="tpu_custom_call" | custom-call | flops 100000 | bytes 1000000 | tf_op jit(solution)/shard_map/pallas_call | solution.py:356
Async XLA Ops:
  0.6 62.5 %copy-start.6 = (s32[128]{0:T(128)S(1)}, s32[128]{0:T(128)}, u32[]{:S(2)}) copy-start(s32[128]{0:T(128)} %param.13) | copy-start | bytes 1540
  24.3 2.8 %copy-start = (bf16[3,128,8192]{2,1,0:T(8,128)(2,1)S(1)}, bf16[3,128,8192]{2,1,0:T(8,128)(2,1)}, u32[]{:S(2)}) copy-start(bf16[3,128,8192]{2,1,0:T(8,128)(2,1)} %design_ref.3) | copy-start | bytes 18874372
  27.1 15.7 %copy-start.2 = (bf16[32,40,128]{2,1,0:T(8,128)(2,1)}, bf16[32,40,128]{2,1,0:T(8,128)(2,1)S(1)}, u32[]{:S(2)}) copy-start(bf16[32,40,128]{2,1,0:T(8,128)(2,1)S(1)} %all_to_all.25.got_ref) | copy-start | bytes 983044
  32.0 14.9 %all-to-all-start.1 = ((f32[8,16,384]{2,1,0:T(8,128)}), f32[8,16,384]{2,1,0:T(8,128)S(1)}, u32[]{:S(2)}, u32[]{:S(2)}) async-start(f32[8,16,384]{2,1,0:T(8,128)} %shard_map.140), calls=%async_computation.1 | async-start | bytes 393216 | tf_op jit(solution)/shard_map/all_to_all | solution.py:369
  46.9 0.7 copy-start.7
  63.1 2.8 %copy-start.1 = (bf16[3,128,8192]{2,1,0:T(8,128)(2,1)S(1)}, bf16[3,128,8192]{2,1,0:T(8,128)(2,1)}, u32[]{:S(2)}) copy-start(bf16[3,128,8192]{2,1,0:T(8,128)(2,1)} %design_ref.3) | copy-start | bytes 18874372
  65.9 1.0 copy-start.3
  66.9 0.9 copy-start.4
  67.8 0.7 copy-start.5

commit v2 on v1

--- a/solution.py
+++ b/solution.py
@@ -10,7 +10,9 @@
 ORDER = ("order_0", "order_1")
 TM_ORDER = TM + ORDER
 CHUNKS = 8
-VMEM_LIMIT = 32 * 1024 * 1024
+VMEM_LIMIT = 50 * 1024 * 1024
+PACK_LIMIT = 59 * 1024 * 1024
+SMALL_LIMIT = 8 * 1024 * 1024
 
 precise = lax.Precision.HIGHEST
 LEVELS = 12
@@ -253,7 +255,7 @@
     ]
 
 
-def observe_kernel(got_ref, design_ref, out_ref, held_ref, sems):
+def observe_kernel(got_ref, design_ref, early_ref, out_ref, held_ref, sems):
     copies = chunk_copies(design_ref, held_ref, sems)
     for copy in copies:
         copy.start()
@@ -347,9 +349,9 @@
     dir_ref[:, 0, :] = fresh
 
 
-def run(kernel, outs, args, scalars=(), anywhere=(), scratch=(), flops=100000, limit=None):
+def run(kernel, outs, args, scalars=(), anywhere=(), scratch=(), flops=100000, limit=SMALL_LIMIT):
     spaces = [
-        pltpu.SMEM if i in scalars else pl.ANY if i in anywhere else pltpu.VMEM
+        pltpu.SMEM if i in scalars else pltpu.HBM if i in anywhere else pltpu.VMEM
         for i in range(len(args))
     ]
     shapes = [jax.ShapeDtypeStruct(*out) for out in outs]
@@ -390,7 +392,10 @@
     place = lax.axis_index(TM).astype(jnp.int32).reshape(1, 1)
     gaps = gap_flags.reshape(1, 128)
     (sheets,) = run(
-        pack_kernel, [((count, 40, 128), bf16)], [direction, segment_ids.reshape(1, 128)]
+        pack_kernel,
+        [((count, 40, 128), bf16)],
+        [direction, segment_ids.reshape(1, 128)],
+        limit=PACK_LIMIT,
     )
     tables = run(
         response_kernel,
@@ -414,7 +419,7 @@
     (partial,) = run(
         observe_kernel,
         [((others, 16, 384), f32)],
-        [got, design],
+        [got, design, tables[2]],
         anywhere=(1,),
         scratch=held,
         limit=VMEM_LIMIT,

time: 115 us -> 99 us (0.86)
  blocking collectives: 73.9 us -> 48.3 us
  starting transfers between devices: 8.65 us -> 20.8 us
  waiting for transfers between devices: 0.01 us -> 10.2 us
  local copies, waits for them, and re-layouts: 8.91 us -> 2.7 us
  Pallas kernels: 21.9 us -> 15.7 us
    all_to_all x4 -> x3, blocking collectives: 73.9 us -> 48.3 us  [exchange(): return lax.all_to_all(value, axes, split_axis=0, concat_axis=0, tiled=True)]
    all_to_all x1 -> x2, starting transfers between devices: 8.65 us -> 20.8 us  [exchange(): return lax.all_to_all(value, axes, split_axis=0, concat_axis=0, tiled=True)]
    all_to_all x1 -> x2, waiting for transfers between devices: 0.01 us -> 10.2 us  [exchange(): return lax.all_to_all(value, axes, split_axis=0, concat_axis=0, tiled=True)]
    unnamed x16 -> x20, local copies, waits for them, and re-layouts: 8.91 us -> 2.7 us
    pallas_call x8, Pallas kernels: 21.9 us -> 15.7 us  [run(): pl.pallas_call(kernel, out_shape=shapes, in_specs=[pl.BlockSpec(memory_sp...]
  transfers between devices with their start and end apart: 1 -> 2, of which waited for: 0 -> 2; matrix products, arithmetic and copies ran while one was open for 0% -> 0% of each run, Pallas kernels for 5% -> 3%
where the time goes in v2:
time: 99 us; the launch traced here: 98.6 us
  blocking collectives  48.3 us (49%)
  starting transfers between devices  20.8 us (21%)
  Pallas kernels  15.7 us (16%)
  waiting for transfers between devices  10.2 us (10%)
  local copies, waits for them, and re-layouts  2.7 us (3%)
    all_to_all x3, blocking collectives, exchange(): return lax.all_to_all(value, axes, split_axis=0, concat_axis=0, tiled=True)  48.3 us
    all_to_all x2, starting transfers between devices, exchange(): return lax.all_to_all(value, axes, split_axis=0, concat_axis=0, tiled=True)  20.8 us
    pallas_call x8, Pallas kernels, run(): pl.pallas_call(kernel, out_shape=shapes, in_specs=[pl.BlockSpec(memory_sp...  15.7 us
    all_to_all x2, waiting for transfers between devices, exchange(): return lax.all_to_all(value, axes, split_axis=0, concat_axis=0, tiled=True)  10.2 us
    unnamed x20, local copies, waits for them, and re-layouts  2.7 us
  transfers between devices with their start and end apart: 2, of which 2 were waited for; matrix products, arithmetic and copies ran while one was open for 0% of the time, Pallas kernels for 3%

profile of v2, /device:TPU:1, one launch (start us, length us, event | category | flops | bytes accessed | tf_op | source)
XLA Modules:
  0.0 98.6 jit_solution(13074840785620392313)
XLA Ops:
  0.6 0.0 copy-start.4
  0.6 1.5 %shard_map.139 = bf16[32,40,128]{2,1,0:T(8,128)(2,1)} custom-call(f32[16,1,256]{2,1,0:T(1,128)} %direction_ref.5, s32[1,128]{1,0:T(1,128)} %bitcast.5), custom_call_target="tpu_custom_call" | custom-call | flops 100000 | bytes 1000000 | tf_op jit(solution)/shard_map/pallas_call | solution.py:358
  2.1 12.0 %all-to-all-start = ((bf16[32,40,128]{2,1,0:T(8,128)(2,1)}), bf16[32,40,128]{2,1,0:T(8,128)(2,1)S(1)}, u32[]{:S(2)}, u32[]{:S(2)}) async-start(bf16[32,40,128]{2,1,0:T(8,128)(2,1)} %shard_map.139), calls=%async_computation | async-start | bytes 655360 | tf_op jit(solution)/shard_map/all_to_all | solution.py:371
  14.2 0.0 copy-start.6
  14.2 0.7 copy-done.6
  14.9 0.7 copy-done.7
  15.6 0.7 copy-done.8
  16.2 0.7 copy-done.9
  16.9 1.2 %shard_map.140 = (f32[3,128,128]{2,1,0:T(8,128)S(1)}, f32[4,8,128]{2,1,0:T(8,128)S(1)}, f32[4,8,128]{2,1,0:T(8,128)S(1)}, f32[3,8,256]{2,1,0:T(8,128)S(1)}, f32[...) custom-call(s32[1,1]{1,0:T(1,128)} %bitcast.1.place_ref, s32[3]{0:T(128)S(1)} %copy-done.8, s32[3]{0:T(128)S(1)} %copy-done.9, ...), custom_call_target="tpu_custom_call" | custom-call | flops 10000000 | bytes 1000000 | tf_op jit(solution)/shard_map/pallas_call | solution.py:358
  18.0 6.3 %all-to-all-done.got_ref = bf16[32,40,128]{2,1,0:T(8,128)(2,1)S(1)} async-done(((bf16[32,40,128]{2,1,0:T(8,128)(2,1)}), bf16[32,40,128]{2,1,0:T(8,128)(2,1)S(1)}, u32[]{:S(2)}, u32[]{:S(2)}) %all-to-all-start) | async-done | bytes 327712 | tf_op jit(solution)/shard_map/all_to_all | solution.py:371
  24.4 5.6 %shard_map.141 = f32[8,16,384]{2,1,0:T(8,128)} custom-call(bf16[32,40,128]{2,1,0:T(8,128)(2,1)S(1)} %all-to-all-done.got_ref, bf16[3,128,8192]{2,1,0:T(8,128)(2,1)} %design_ref.3, f32[4,8,128]{2,1,0:T(8,128)S(1)} %get-tuple-element.18.early_ref.fin_ref), custom_call_target="tpu_custom_call" | custom-call | flops 100000 | bytes 1000000 | tf_op jit(solution)/shard_map/pallas_call | solution.py:358
  30.0 0.0 copy-start
  30.0 0.0 copy-start.1
  30.0 0.0 copy-start.2
  30.0 0.0 copy-start.5
  30.0 0.0 copy-start.3
  30.1 8.8 %all-to-all-start.1 = ((f32[8,16,384]{2,1,0:T(8,128)}), f32[8,16,384]{2,1,0:T(8,128)S(1)}, u32[]{:S(2)}, u32[]{:S(2)}) async-start(f32[8,16,384]{2,1,0:T(8,128)} %shard_map.141), calls=%async_computation.1 | async-start | bytes 393216 | tf_op jit(solution)/shard_map/all_to_all | solution.py:371
  38.8 1.9 %shard_map.142 = (f32[3,8,128]{2,1,0:T(8,128)S(1)}, f32[3,128,128]{2,1,0:T(8,128)S(1)}, f32[3,256,128]{2,1,0:T(8,128)S(1)}) custom-call(s32[1,1]{1,0:T(1,128)} %bitcast.1.place_ref, bf16[32,40,128]{2,1,0:T(8,128)(2,1)S(1)} %all-to-all-done.got_ref, f32[3,128,128]{2,1,0:T(8,128)S(1)} %get-tuple-element.19.toep_ref, ...), custom_call_target="tpu_custom_call" | custom-call | flops 10000000 | bytes 1000000 | tf_op jit(solution)/shard_map/pallas_call | solution.py:358
  40.8 3.9 %all-to-all-done.1.parts_ref = f32[8,16,384]{2,1,0:T(8,128)S(1)} async-done(((f32[8,16,384]{2,1,0:T(8,128)}), f32[8,16,384]{2,1,0:T(8,128)S(1)}, u32[]{:S(2)}, u32[]{:S(2)}) %all-to-all-start.1) | async-done | bytes 196640 | tf_op jit(solution)/shard_map/all_to_all | solution.py:371
  44.7 0.0 copy-done.4
  44.7 0.2 shard_map.143
  45.0 13.4 %all_to_all.25.states_ref = f32[32,8,128]{2,1,0:T(8,128)S(1)} all-to-all(f32[32,8,128]{2,1,0:T(8,128)S(1)} %get-tuple-element.28), channel_id=1, replica_groups=mesh['tm_0'=4,'tm_1'=8,'order_0'=4,'order_1'=2] {'tm_0','tm_1'}, dimensions={0} | all-to-all | bytes 262144 | tf_op jit(solution)/shard_map/all_to_all | solution.py:371
  58.4 3.6 %shard_map.144 = bf16[32,16,256]{2,1,0:T(8,128)(2,1)S(1)} custom-call(f32[48,128]{1,0:T(8,128)S(1)} %get-tuple-element.25.masked_ref, f32[3,128,128]{2,1,0:T(8,128)S(1)} %get-tuple-element.26.near_ref, f32[3,256,128]{2,1,0:T(8,128)S(1)} %get-tuple-element.27.far_ref, s32[1,128]{1,0:T(1,128)S(1)} %bitcast.4, f32[32,8,128]{2,1,0:T(8,128)S(1)} %all_to_all.25.states_ref, ...), custom_call_target="tpu_custom_call" | custom-call | flops 100000 | bytes 1000000 | tf_op jit(solution)/shard_map/pallas_call | solution.py:358
  62.0 13.2 %all_to_all.26.arrived_ref = bf16[32,16,256]{2,1,0:T(8,128)(2,1)S(1)} all-to-all(bf16[32,16,256]{2,1,0:T(8,128)(2,1)S(1)} %shard_map.144), channel_id=1, replica_groups=mesh['tm_0'=4,'tm_1'=8,'order_0'=4,'order_1'=2] {'tm_0','tm_1'}, dimensions={0} | all-to-all | bytes 524288 | tf_op jit(solution)/shard_map/all_to_all | solution.py:371
  75.2 0.0 copy-done
  75.2 0.0 copy-done.1
  75.2 0.0 copy-done.2
  75.2 0.0 copy-done.5
  75.2 0.6 shard_map.145
  75.8 21.7 %all_to_all.27.sums_ref = f32[256,1,128]{2,1,0:T(1,128)S(1)} all-to-all(f32[256,1,128]{2,1,0:T(1,128)S(1)} %get-tuple-element.29), channel_id=1, replica_groups=mesh['tm_0'=4,'tm_1'=8,'order_0'=4,'order_1'=2] {'tm_0','tm_1','order_0'..., dimensions={0} | all-to-all | bytes 262144 | tf_op jit(solution)/shard_map/all_to_all | solution.py:371
  97.6 0.0 copy-done.3
  97.6 1.0 shard_map.146
  (3 shorter events, 0.0 us)
Async XLA Ops:
  0.6 44.1 %copy-start.4 = (s32[128]{0:T(128)S(1)}, s32[128]{0:T(128)}, u32[]{:S(2)}) copy-start(s32[128]{0:T(128)} %param.13) | copy-start | bytes 1540
  2.1 22.2 %all-to-all-start = ((bf16[32,40,128]{2,1,0:T(8,128)(2,1)}), bf16[32,40,128]{2,1,0:T(8,128)(2,1)S(1)}, u32[]{:S(2)}, u32[]{:S(2)}) async-start(bf16[32,40,128]{2,1,0:T(8,128)(2,1)} %shard_map.139), calls=%async_computation | async-start | bytes 655360 | tf_op jit(solution)/shard_map/all_to_all | solution.py:371
  14.2 0.7 copy-start.6
  14.9 0.7 copy-start.7
  15.5 0.7 copy-start.8
  16.2 0.7 copy-start.9
  30.0 45.2 %copy-start = (f32[16,1,256]{2,1,0:T(1,128)S(1)}, f32[16,1,256]{2,1,0:T(1,128)}, u32[]{:S(2)}) copy-start(f32[16,1,256]{2,1,0:T(1,128)} %direction_ref.5) | copy-start | bytes 49156
  30.0 45.2 %copy-start.1 = (f32[1,2,128,128]{3,2,1,0:T(8,128)S(1)}, f32[1,2,128,128]{3,2,1,0:T(8,128)}, u32[]{:S(2)}) copy-start(f32[1,2,128,128]{3,2,1,0:T(8,128)} %precond_ref.1) | copy-start | bytes 393220
  30.0 45.2 %copy-start.2 = (f32[16,1,256]{2,1,0:T(1,128)S(1)}, f32[16,1,256]{2,1,0:T(1,128)}, u32[]{:S(2)}) copy-start(f32[16,1,256]{2,1,0:T(1,128)} %residual_ref.3) | copy-start | bytes 49156
  30.0 45.2 %copy-start.5 = (f32[1,256]{1,0:T(1,128)S(1)}, f32[1,256]{1,0:T(1,128)}, u32[]{:S(2)}) copy-start(f32[1,256]{1,0:T(1,128)} %kaula_ref.1) | copy-start | bytes 3076
  30.0 67.5 %copy-start.3 = (f32[16,1,256]{2,1,0:T(1,128)S(1)}, f32[16,1,256]{2,1,0:T(1,128)}, u32[]{:S(2)}) copy-start(f32[16,1,256]{2,1,0:T(1,128)} %solution_ref.1) | copy-start | bytes 49156
  30.1 14.7 %all-to-all-start.1 = ((f32[8,16,384]{2,1,0:T(8,128)}), f32[8,16,384]{2,1,0:T(8,128)S(1)}, u32[]{:S(2)}, u32[]{:S(2)}) async-start(f32[8,16,384]{2,1,0:T(8,128)} %shard_map.141), calls=%async_computation.1 | async-start | bytes 393216 | tf_op jit(solution)/shard_map/all_to_all | solution.py:371

commit v3 on v2

--- a/solution.py
+++ b/solution.py
@@ -9,7 +9,6 @@
 TM = ("tm_0", "tm_1")
 ORDER = ("order_0", "order_1")
 TM_ORDER = TM + ORDER
-CHUNKS = 8
 VMEM_LIMIT = 50 * 1024 * 1024
 PACK_LIMIT = 59 * 1024 * 1024
 SMALL_LIMIT = 8 * 1024 * 1024
@@ -125,7 +124,7 @@
     front = row < 4
     for side in range(2):
         wide = lane + 128 * side
-        peer, kind = wide >> 3, wide & 7
+        peer, kind = wide & 31, wide >> 5
         gap = jnp.where(front, place - 1 - peer, peer - 1 - place)
         steps = jnp.maximum(gap, 0)
         for c in range(3):
@@ -154,22 +153,29 @@
     place_ref, got_ref, toep_ref, gam_ref, fin_ref, reach_ref, pow_ref, gram_ref, own_ref, near_ref, far_ref
 ):
     place = place_ref[0, 0]
-    ids = got_ref[:, 32:40, :].astype(jnp.float32)
-    peer = lax.broadcasted_iota(jnp.int32, (32, 8, 128), 0)
-    mine = jnp.sum(jnp.where(peer == place, ids, 0.0), axis=0)
-    before = jnp.sum(jnp.where(peer == place - 1, ids, 0.0), axis=0)
-    ends = jnp.broadcast_to(ids[:, :, 127:128], (32, 8, 128))
-    last = jnp.broadcast_to(mine[:, 127:128], (8, 128))
-    prev = jnp.where(place > 0, jnp.broadcast_to(before[:, 127:128], (8, 128)), -1.0)
-    count = jnp.sum(jnp.where((peer > place) & (ids == last[None]), 1.0, 0.0), axis=0)
-    left = jnp.broadcast_to(jnp.sum(count, axis=1, keepdims=True), (8, 128)).astype(jnp.int32)
-    ends_before = jnp.concatenate([ends[:1], ends[:-1]], axis=0)
-    sub = lax.broadcasted_iota(jnp.int32, (32, 8, 128), 1)
-    keep = jnp.where(
-        sub < 4,
-        jnp.where((peer < place) & (ends == prev[None]), 1.0, 0.0),
-        jnp.where((peer > place) & (ends_before == last[None]), 1.0, 0.0),
-    ).reshape(256, 128)
+    row = lax.broadcasted_iota(jnp.int32, (8, 128), 0)
+    groups = []
+    for g in range(4):
+        group = jnp.zeros((8, 128), jnp.float32)
+        for s in range(8):
+            group = jnp.where(row == s, got_ref[8 * g + s, 32:40, :].astype(jnp.float32), group)
+        groups.append(group)
+    ids = jnp.concatenate(groups, axis=0)
+    peer = lax.broadcasted_iota(jnp.int32, (32, 128), 0)
+    mine = jnp.sum(jnp.where(peer == place, ids, 0.0), axis=0, keepdims=True)
+    before = jnp.sum(jnp.where(peer == place - 1, ids, 0.0), axis=0, keepdims=True)
+    ends = jnp.broadcast_to(ids[:, 127:128], (32, 128))
+    last = jnp.broadcast_to(mine[:, 127:128], (1, 128))
+    prev = jnp.where(place > 0, jnp.broadcast_to(before[:, 127:128], (1, 128)), -1.0)
+    count = jnp.sum(
+        jnp.where((peer > place) & (ids == last), 1.0, 0.0), axis=0, keepdims=True
+    )
+    left = jnp.sum(count, axis=1, keepdims=True).astype(jnp.int32)
+    left = jnp.broadcast_to(left, (8, 128))
+    ends_before = pltpu.roll(ends, 1, 0)
+    keep_past = jnp.where((peer < place) & (ends == prev), 1.0, 0.0)
+    keep_next = jnp.where((peer > place) & (ends_before == last), 1.0, 0.0)
+    keep = jnp.concatenate([keep_past] * 4 + [keep_next] * 4, axis=0)
     gram = {at: jnp.zeros((8, 128), jnp.float32) for at in UPPER}
     for k in range(LEVELS - 1):
         power = {pair: pow_ref[k, at] for at, pair in enumerate(LOWER)}
@@ -189,10 +195,9 @@
     ]
     block = {pair: pow_ref[RADIX, at] for at, pair in enumerate(LOWER)}
     past = [cont * value for value in row_times(fold, block)]
-    row = lax.broadcasted_iota(jnp.int32, (8, 128), 0)
     big_row = lax.broadcasted_iota(jnp.int32, (128, 128), 0)
     big_lane = lax.broadcasted_iota(jnp.int32, (128, 128), 1)
-    wide = jnp.broadcast_to(mine[0:1, :], (128, 128))
+    wide = jnp.broadcast_to(mine, (128, 128))
     tall = jnp.sum(jnp.where(big_row == big_lane, wide, 0.0), axis=1, keepdims=True)
     same = wide == jnp.broadcast_to(tall, (128, 128))
 
@@ -213,27 +218,30 @@
 
 
 def state_kernel(parts_ref, gaps_ref, own_ref, message_ref, masked_ref):
-    total = parts_ref[0]
+    total = parts_ref[0].astype(jnp.float32)
     for o in range(1, parts_ref.shape[0]):
-        total = total + parts_ref[o]
+        total = total + parts_ref[o].astype(jnp.float32)
     gaps = gaps_ref[...].astype(jnp.float32)
-    masked = jnp.concatenate([total[:, 128 * c : 128 * c + 128] * gaps for c in range(3)], axis=0)
-    masked_ref[...] = masked
-    padded = jnp.concatenate([masked, jnp.zeros((80, 128), jnp.float32)], axis=0)
-    lane = lax.broadcasted_iota(jnp.int32, (8, 128), 1)
-    out = jnp.zeros((8, 128), jnp.float32)
+    rows = []
     for c in range(3):
-        out = jnp.where((lane >> 4) == c, dot(own_ref[c], padded, ((1,), (1,))), out)
-    message_ref[...] = jnp.broadcast_to(out[None], message_ref.shape)
+        masked = total[:, 128 * c : 128 * c + 128] * gaps
+        masked_ref[16 * c : 16 * c + 16, :] = masked
+        padded = jnp.concatenate([masked, jnp.zeros((112, 128), jnp.float32)], axis=0)
+        spread = pltpu.roll(
+            dot(own_ref[c], padded, ((1,), (1,))), 0, 1, stride=16, stride_axis=0
+        )
+        rows.append(jnp.sum(spread, axis=0, keepdims=True))
+    message_ref[...] = jnp.broadcast_to(jnp.concatenate(rows, axis=0)[None], message_ref.shape)
 
 
 def weighted_rows(masked_ref, near_ref, far_ref, gaps_ref, states_ref):
     gaps = gaps_ref[...].astype(jnp.float32)
-    states = states_ref[...].reshape(256, 128)
     pieces = []
     for c in range(3):
         here = dot(masked_ref[16 * c : 16 * c + 16, :], near_ref[c], ((1,), (0,)))
-        there = dot(states, far_ref[c], ((0,), (0,)))[16 * c : 16 * c + 16, :]
+        states = states_ref[:, c, :]
+        turned = [states] + [pltpu.roll(states, 128 - 16 * i, 1) for i in range(1, 8)]
+        there = dot(jnp.concatenate(turned, axis=0), far_ref[c], ((0,), (0,)))[0:16, :]
         pieces.append((here + there) * gaps)
     return pieces
 
@@ -261,21 +269,20 @@
         copy.start()
     count, _, _, width = held_ref.shape
     peers = width // 256
-    total = jnp.zeros((384, 128), jnp.float32)
+    total = jnp.zeros((16, 384), jnp.float32)
     for k in range(count):
         pieces = []
         for p in range(peers * k, peers * k + peers):
             pieces += [got_ref[p, 0:16, :], got_ref[p, 16:32, :]]
         packed = jnp.concatenate(pieces, axis=1)
-        packed = jnp.concatenate([packed, jnp.zeros((112, width), jnp.bfloat16)], axis=0)
         copies[k].wait()
         total = total + lax.dot_general(
+            packed,
             held_ref[k].reshape(384, width),
-            packed,
             (((1,), (1,)), ((), ())),
             preferred_element_type=jnp.float32,
         )
-    out_ref[...] = jnp.broadcast_to(total.T[None, 0:16, :], out_ref.shape)
+    out_ref[...] = jnp.broadcast_to(total.astype(jnp.bfloat16)[None], out_ref.shape)
 
 
 def gradient_kernel(
@@ -412,16 +419,19 @@
         flops=10000000,
     )
     got = exchange(sheets, TM)
-    held = [
-        pltpu.VMEM((CHUNKS, 3, 128, design.shape[2] // CHUNKS), bf16),
-        pltpu.SemaphoreType.DMA((CHUNKS,)),
-    ]
+
+    def held(chunks):
+        return [
+            pltpu.VMEM((chunks, 3, 128, design.shape[2] // chunks), bf16),
+            pltpu.SemaphoreType.DMA((chunks,)),
+        ]
+
     (partial,) = run(
         observe_kernel,
-        [((others, 16, 384), f32)],
+        [((others, 16, 384), bf16)],
         [got, design, tables[2]],
         anywhere=(1,),
-        scratch=held,
+        scratch=held(16),
         limit=VMEM_LIMIT,
     )
     parts = exchange(partial, ORDER)
@@ -433,7 +443,7 @@
         flops=10000000,
     )
     message, masked = run(
-        state_kernel, [((count, 8, 128), f32), ((48, 128), f32)], [parts, gaps, own]
+        state_kernel, [((count, 3, 128), f32), ((48, 128), f32)], [parts, gaps, own]
     )
     states = exchange(message, TM)
     (gradient,) = run(
@@ -441,7 +451,7 @@
         [((count, 16, 256), bf16)],
         [masked, near, far, gaps, states, design],
         anywhere=(5,),
-        scratch=held,
+        scratch=held(8),
         limit=VMEM_LIMIT,
     )
     arrived = exchange(gradient, TM)

time: 99 us -> 96.3 us (0.973)
  Pallas kernels: 15.7 us -> 14.7 us
    pallas_call x8, Pallas kernels: 15.7 us -> 14.7 us  [run(): pl.pallas_call(kernel, out_shape=shapes, in_specs=[pl.BlockSpec(memory_sp...]
where the time goes in v3:
time: 96.3 us; the launch traced here: 95.8 us
  blocking collectives  47.5 us (49%)
  starting transfers between devices  20.8 us (22%)
  Pallas kernels  14.7 us (15%)
  waiting for transfers between devices  9.39 us (10%)
  local copies, waits for them, and re-layouts  2.7 us (3%)
    all_to_all x3, blocking collectives, exchange(): return lax.all_to_all(value, axes, split_axis=0, concat_axis=0, tiled=True)  47.5 us
    all_to_all x2, starting transfers between devices, exchange(): return lax.all_to_all(value, axes, split_axis=0, concat_axis=0, tiled=True)  20.8 us
    pallas_call x8, Pallas kernels, run(): pl.pallas_call(kernel, out_shape=shapes, in_specs=[pl.BlockSpec(memory_sp...  14.7 us
    all_to_all x2, waiting for transfers between devices, exchange(): return lax.all_to_all(value, axes, split_axis=0, concat_axis=0, tiled=True)  9.39 us
    unnamed x20, local copies, waits for them, and re-layouts  2.7 us
  transfers between devices with their start and end apart: 2, of which 2 were waited for; matrix products, arithmetic and copies ran while one was open for 0% of the time, Pallas kernels for 3%

profile of v3, /device:TPU:1, one launch (start us, length us, event | category | flops | bytes accessed | tf_op | source)
XLA Modules:
  0.0 95.8 jit_solution(5093222405457881538)
XLA Ops:
  0.6 0.0 copy-start.4
  0.6 1.5 %shard_map.139 = bf16[32,40,128]{2,1,0:T(8,128)(2,1)} custom-call(f32[16,1,256]{2,1,0:T(1,128)} %direction_ref.5, s32[1,128]{1,0:T(1,128)} %bitcast.5), custom_call_target="tpu_custom_call" | custom-call | flops 100000 | bytes 1000000 | tf_op jit(solution)/shard_map/pallas_call | solution.py:365
  2.1 12.0 %all-to-all-start = ((bf16[32,40,128]{2,1,0:T(8,128)(2,1)}), bf16[32,40,128]{2,1,0:T(8,128)(2,1)S(1)}, u32[]{:S(2)}, u32[]{:S(2)}) async-start(bf16[32,40,128]{2,1,0:T(8,128)(2,1)} %shard_map.139), calls=%async_computation | async-start | bytes 655360 | tf_op jit(solution)/shard_map/all_to_all | solution.py:378
  14.2 0.0 copy-start.6
  14.2 0.7 copy-done.6
  14.9 0.7 copy-done.7
  15.6 0.7 copy-done.8
  16.2 0.7 copy-done.9
  16.9 1.2 %shard_map.140 = (f32[3,128,128]{2,1,0:T(8,128)S(1)}, f32[4,8,128]{2,1,0:T(8,128)S(1)}, f32[4,8,128]{2,1,0:T(8,128)S(1)}, f32[3,8,256]{2,1,0:T(8,128)S(1)}, f32[...) custom-call(s32[1,1]{1,0:T(1,128)} %bitcast.1.place_ref, s32[3]{0:T(128)S(1)} %copy-done.8, s32[3]{0:T(128)S(1)} %copy-done.9, ...), custom_call_target="tpu_custom_call" | custom-call | flops 10000000 | bytes 1000000 | tf_op jit(solution)/shard_map/pallas_call | solution.py:365
  18.0 6.3 %all-to-all-done.got_ref = bf16[32,40,128]{2,1,0:T(8,128)(2,1)S(1)} async-done(((bf16[32,40,128]{2,1,0:T(8,128)(2,1)}), bf16[32,40,128]{2,1,0:T(8,128)(2,1)S(1)}, u32[]{:S(2)}, u32[]{:S(2)}) %all-to-all-start) | async-done | bytes 327712 | tf_op jit(solution)/shard_map/all_to_all | solution.py:378
  24.4 4.5 %shard_map.141 = bf16[8,16,384]{2,1,0:T(8,128)(2,1)} custom-call(bf16[32,40,128]{2,1,0:T(8,128)(2,1)S(1)} %all-to-all-done.got_ref, bf16[3,128,8192]{2,1,0:T(8,128)(2,1)} %design_ref.3, f32[4,8,128]{2,1,0:T(8,128)S(1)} %get-tuple-element.18.early_ref.fin_ref), custom_call_target="tpu_custom_call" | custom-call | flops 100000 | bytes 1000000 | tf_op jit(solution)/shard_map/pallas_call | solution.py:365
  28.9 0.0 copy-start
  28.9 0.0 copy-start.1
  28.9 0.0 copy-start.2
  28.9 0.0 copy-start.5
  29.0 0.0 copy-start.3
  29.0 8.8 %all-to-all-start.1 = ((bf16[8,16,384]{2,1,0:T(8,128)(2,1)}), bf16[8,16,384]{2,1,0:T(8,128)(2,1)S(1)}, u32[]{:S(2)}, u32[]{:S(2)}) async-start(bf16[8,16,384]{2,1,0:T(8,128)(2,1)} %shard_map.141), calls=%async_computation.1 | async-start | bytes 196608 | tf_op jit(solution)/shard_map/all_to_all | solution.py:378
  37.7 1.9 %shard_map.142 = (f32[3,8,128]{2,1,0:T(8,128)S(1)}, f32[3,128,128]{2,1,0:T(8,128)S(1)}, f32[3,256,128]{2,1,0:T(8,128)S(1)}) custom-call(s32[1,1]{1,0:T(1,128)} %bitcast.1.place_ref, bf16[32,40,128]{2,1,0:T(8,128)(2,1)S(1)} %all-to-all-done.got_ref, f32[3,128,128]{2,1,0:T(8,128)S(1)} %get-tuple-element.19.toep_ref, ...), custom_call_target="tpu_custom_call" | custom-call | flops 10000000 | bytes 1000000 | tf_op jit(solution)/shard_map/pallas_call | solution.py:365
  39.7 3.1 %all-to-all-done.1.parts_ref = bf16[8,16,384]{2,1,0:T(8,128)(2,1)S(1)} async-done(((bf16[8,16,384]{2,1,0:T(8,128)(2,1)}), bf16[8,16,384]{2,1,0:T(8,128)(2,1)S(1)}, u32[]{:S(2)}, u32[]{:S(2)}) %all-to-all-start.1) | async-done | bytes 98336 | tf_op jit(solution)/shard_map/all_to_all | solution.py:378
  42.7 0.0 copy-done.4
  42.7 0.2 shard_map.143
  43.0 13.1 %all_to_all.25.states_ref = f32[32,3,128]{2,1,0:T(4,128)S(1)} all-to-all(f32[32,3,128]{2,1,0:T(4,128)S(1)} %get-tuple-element.28), channel_id=1, replica_groups=mesh['tm_0'=4,'tm_1'=8,'order_0'=4,'order_1'=2] {'tm_0','tm_1'}, dimensions={0} | all-to-all | bytes 98304 | tf_op jit(solution)/shard_map/all_to_all | solution.py:378
  56.1 3.7 %shard_map.144 = bf16[32,16,256]{2,1,0:T(8,128)(2,1)S(1)} custom-call(f32[48,128]{1,0:T(8,128)S(1)} %get-tuple-element.25.masked_ref, f32[3,128,128]{2,1,0:T(8,128)S(1)} %get-tuple-element.26.near_ref, f32[3,256,128]{2,1,0:T(8,128)S(1)} %get-tuple-element.27.far_ref, s32[1,128]{1,0:T(1,128)S(1)} %bitcast.4, f32[32,3,128]{2,1,0:T(4,128)S(1)} %all_to_all.25.states_ref, ...), custom_call_target="tpu_custom_call" | custom-call | flops 100000 | bytes 1000000 | tf_op jit(solution)/shard_map/pallas_call | solution.py:365
  59.8 12.8 %all_to_all.26.arrived_ref = bf16[32,16,256]{2,1,0:T(8,128)(2,1)S(1)} all-to-all(bf16[32,16,256]{2,1,0:T(8,128)(2,1)S(1)} %shard_map.144), channel_id=1, replica_groups=mesh['tm_0'=4,'tm_1'=8,'order_0'=4,'order_1'=2] {'tm_0','tm_1'}, dimensions={0} | all-to-all | bytes 524288 | tf_op jit(solution)/shard_map/all_to_all | solution.py:378
  72.6 0.0 copy-done
  72.6 0.0 copy-done.1
  72.6 0.0 copy-done.2
  72.6 0.0 copy-done.5
  72.6 0.6 shard_map.145
  73.2 21.6 %all_to_all.27.sums_ref = f32[256,1,128]{2,1,0:T(1,128)S(1)} all-to-all(f32[256,1,128]{2,1,0:T(1,128)S(1)} %get-tuple-element.29), channel_id=1, replica_groups=mesh['tm_0'=4,'tm_1'=8,'order_0'=4,'order_1'=2] {'tm_0','tm_1','order_0'..., dimensions={0} | all-to-all | bytes 262144 | tf_op jit(solution)/shard_map/all_to_all | solution.py:378
  94.8 0.0 copy-done.3
  94.8 1.0 %shard_map.146 = (f32[16,1,256]{2,1,0:T(1,128)}, f32[16,1,256]{2,1,0:T(1,128)}, f32[16,1,256]{2,1,0:T(1,128)}) custom-call(f32[256,1,128]{2,1,0:T(1,128)S(1)} %all_to_all.27.sums_ref, f32[16,256]{1,0:T(8,128)S(1)} %get-tuple-element.30.image_ref, f32[16,256]{1,0:T(8,128)S(1)} %get-tuple-element.31.applied_ref, f32[16,256]{1,0:T(8,128)S(1)} %get-tuple-element.32.both_ref, ...), custom_call_target="tpu_custom_call" | custom-call | flops 100000 | bytes 1000000 | tf_op jit(solution)/shard_map/pallas_call | solution.py:365
  (3 shorter events, 0.0 us)
Async XLA Ops:
  0.6 42.1 %copy-start.4 = (s32[128]{0:T(128)S(1)}, s32[128]{0:T(128)}, u32[]{:S(2)}) copy-start(s32[128]{0:T(128)} %param.13) | copy-start | bytes 1540
  2.1 22.2 %all-to-all-start = ((bf16[32,40,128]{2,1,0:T(8,128)(2,1)}), bf16[32,40,128]{2,1,0:T(8,128)(2,1)S(1)}, u32[]{:S(2)}, u32[]{:S(2)}) async-start(bf16[32,40,128]{2,1,0:T(8,128)(2,1)} %shard_map.139), calls=%async_computation | async-start | bytes 655360 | tf_op jit(solution)/shard_map/all_to_all | solution.py:378
  14.2 0.7 copy-start.6
  14.9 0.7 copy-start.7
  15.5 0.7 copy-start.8
  16.2 0.7 copy-start.9
  28.9 43.7 %copy-start = (f32[16,1,256]{2,1,0:T(1,128)S(1)}, f32[16,1,256]{2,1,0:T(1,128)}, u32[]{:S(2)}) copy-start(f32[16,1,256]{2,1,0:T(1,128)} %direction_ref.5) | copy-start | bytes 49156
  28.9 43.7 %copy-start.1 = (f32[1,2,128,128]{3,2,1,0:T(8,128)S(1)}, f32[1,2,128,128]{3,2,1,0:T(8,128)}, u32[]{:S(2)}) copy-start(f32[1,2,128,128]{3,2,1,0:T(8,128)} %precond_ref.1) | copy-start | bytes 393220
  28.9 43.7 %copy-start.2 = (f32[16,1,256]{2,1,0:T(1,128)S(1)}, f32[16,1,256]{2,1,0:T(1,128)}, u32[]{:S(2)}) copy-start(f32[16,1,256]{2,1,0:T(1,128)} %residual_ref.3) | copy-start | bytes 49156
  28.9 43.7 %copy-start.5 = (f32[1,256]{1,0:T(1,128)S(1)}, f32[1,256]{1,0:T(1,128)}, u32[]{:S(2)}) copy-start(f32[1,256]{1,0:T(1,128)} %kaula_ref.1) | copy-start | bytes 3076
  29.0 65.9 %copy-start.3 = (f32[16,1,256]{2,1,0:T(1,128)S(1)}, f32[16,1,256]{2,1,0:T(1,128)}, u32[]{:S(2)}) copy-start(f32[16,1,256]{2,1,0:T(1,128)} %solution_ref.1) | copy-start | bytes 49156
  29.0 13.8 %all-to-all-start.1 = ((bf16[8,16,384]{2,1,0:T(8,128)(2,1)}), bf16[8,16,384]{2,1,0:T(8,128)(2,1)S(1)}, u32[]{:S(2)}, u32[]{:S(2)}) async-start(bf16[8,16,384]{2,1,0:T(8,128)(2,1)} %shard_map.141), calls=%async_computation.1 | async-start | bytes 196608 | tf_op jit(solution)/shard_map/all_to_all | solution.py:378

commit v4 on v3

--- a/solution.py
+++ b/solution.py
@@ -10,7 +10,6 @@
 ORDER = ("order_0", "order_1")
 TM_ORDER = TM + ORDER
 VMEM_LIMIT = 50 * 1024 * 1024
-PACK_LIMIT = 59 * 1024 * 1024
 SMALL_LIMIT = 8 * 1024 * 1024
 
 precise = lax.Precision.HIGHEST
@@ -246,6 +245,13 @@
     return pieces
 
 
+def tables_kernel(
+    place_ref, aro_ref, mao_ref, arr_ref, mar_ref, got_ref, own_ref, near_ref, far_ref, *tables
+):
+    response_kernel(place_ref, aro_ref, mao_ref, arr_ref, mar_ref, *tables)
+    segment_kernel(place_ref, got_ref, *tables, own_ref, near_ref, far_ref)
+
+
 def pack_kernel(direction_ref, ids_ref, out_ref):
     packed = direction_ref[:, 0, :].astype(jnp.bfloat16)
     ids = jnp.broadcast_to(ids_ref[...].astype(jnp.float32), (8, 128)).astype(jnp.bfloat16)
@@ -263,7 +269,7 @@
     ]
 
 
-def observe_kernel(got_ref, design_ref, early_ref, out_ref, held_ref, sems):
+def observe_kernel(got_ref, design_ref, out_ref, held_ref, sems):
     copies = chunk_copies(design_ref, held_ref, sems)
     for copy in copies:
         copy.start()
@@ -402,21 +408,7 @@
         pack_kernel,
         [((count, 40, 128), bf16)],
         [direction, segment_ids.reshape(1, 128)],
-        limit=PACK_LIMIT,
-    )
-    tables = run(
-        response_kernel,
-        [
-            ((3, 128, 128), f32),
-            ((4, 8, 128), f32),
-            ((4, 8, 128), f32),
-            ((3, 8, 256), f32),
-            ((LEVELS - 1, 10, 8, 128), f32),
-            ((LEVELS - 1, 10, 8, 128), f32),
-        ],
-        [place, ar_order, ma_order, ar_roots, ma_roots],
-        scalars=(0, 1, 2, 3, 4),
-        flops=10000000,
+        limit=VMEM_LIMIT,
     )
     got = exchange(sheets, TM)
 
@@ -429,17 +421,25 @@
     (partial,) = run(
         observe_kernel,
         [((others, 16, 384), bf16)],
-        [got, design, tables[2]],
+        [got, design],
         anywhere=(1,),
         scratch=held(16),
         limit=VMEM_LIMIT,
     )
     parts = exchange(partial, ORDER)
     own, near, far = run(
-        segment_kernel,
+        tables_kernel,
         [((3, 8, 128), f32), ((3, 128, 128), f32), ((3, 256, 128), f32)],
-        [place, got, *tables],
-        scalars=(0,),
+        [place, ar_order, ma_order, ar_roots, ma_roots, got],
+        scalars=(0, 1, 2, 3, 4),
+        scratch=[
+            pltpu.VMEM((3, 128, 128), f32),
+            pltpu.VMEM((4, 8, 128), f32),
+            pltpu.VMEM((4, 8, 128), f32),
+            pltpu.VMEM((3, 8, 256), f32),
+            pltpu.VMEM((LEVELS - 1, 10, 8, 128), f32),
+            pltpu.VMEM((LEVELS - 1, 10, 8, 128), f32),
+        ],
         flops=10000000,
     )
     message, masked = run(

time: 96.3 us -> 95.8 us (level)
  blocking collectives: 47.5 us -> 69.5 us
  starting transfers between devices: 20.8 us -> 8.65 us
  waiting for transfers between devices: 9.39 us -> 2.21 us
  Pallas kernels: 14.7 us -> 12.9 us
  local copies, waits for them, and re-layouts: 2.7 us -> 1.42 us
    all_to_all x3 -> x4, blocking collectives: 47.5 us -> 69.5 us  [exchange(): return lax.all_to_all(value, axes, split_axis=0, concat_axis=0, tiled=True)]
    all_to_all x2 -> x1, starting transfers between devices: 20.8 us -> 8.65 us  [exchange(): return lax.all_to_all(value, axes, split_axis=0, concat_axis=0, tiled=True)]
    all_to_all x2 -> x1, waiting for transfers between devices: 9.39 us -> 2.21 us  [exchange(): return lax.all_to_all(value, axes, split_axis=0, concat_axis=0, tiled=True)]
    pallas_call x8 -> x7, Pallas kernels: 14.7 us -> 12.9 us  [run(): pl.pallas_call(kernel, out_shape=shapes, in_specs=[pl.BlockSpec(memory_sp...]
    unnamed x20 -> x24, local copies, waits for them, and re-layouts: 2.7 us -> 1.42 us
  transfers between devices with their start and end apart: 2 -> 1, of which waited for: 2 -> 1; matrix products, arithmetic and copies ran while one was open for 0% -> 0% of each run, Pallas kernels for 3% -> 3%
where the time goes in v4:
time: 95.8 us; the launch traced here: 95.4 us
  blocking collectives  69.5 us (73%)
  Pallas kernels  12.9 us (13%)
  starting transfers between devices  8.65 us (9%)
  waiting for transfers between devices  2.21 us (2%)
  local copies, waits for them, and re-layouts  1.42 us (1%)
    all_to_all x4, blocking collectives, exchange(): return lax.all_to_all(value, axes, split_axis=0, concat_axis=0, tiled=True)  69.5 us
    pallas_call x7, Pallas kernels, run(): pl.pallas_call(kernel, out_shape=shapes, in_specs=[pl.BlockSpec(memory_sp...  12.9 us
    all_to_all x1, starting transfers between devices, exchange(): return lax.all_to_all(value, axes, split_axis=0, concat_axis=0, tiled=True)  8.65 us
    all_to_all x1, waiting for transfers between devices, exchange(): return lax.all_to_all(value, axes, split_axis=0, concat_axis=0, tiled=True)  2.21 us
  transfers between devices with their start and end apart: 1, of which 1 were waited for; matrix products, arithmetic and copies ran while one was open for 0% of the time, Pallas kernels for 3%

profile of v4, /device:TPU:1, one launch (start us, length us, event | category | flops | bytes accessed | tf_op | source)
XLA Modules:
  0.0 95.4 jit_solution(11971334329238966767)
XLA Ops:
  0.6 0.0 copy-start.10
  0.6 0.0 copy-start.11
  0.7 0.0 copy-start.7
  0.7 0.0 copy-start
  0.7 0.7 copy-done
  1.4 0.0 copy-start.9
  1.4 0.7 copy-done.9
  2.1 0.0 copy-start.5
  2.1 0.1 shard_map.139
  2.1 22.0 %all_to_all.25.got_ref = bf16[32,40,128]{2,1,0:T(8,128)(2,1)S(1)} all-to-all(bf16[32,40,128]{2,1,0:T(8,128)(2,1)S(1)} %shard_map.139), channel_id=1, replica_groups=mesh['tm_0'=4,'tm_1'=8,'order_0'=4,'order_1'=2] {'tm_0','tm_1'}, dimensions={0} | all-to-all | bytes 655360 | tf_op jit(solution)/shard_map/all_to_all | solution.py:384
  24.1 4.6 %shard_map.140 = bf16[8,16,384]{2,1,0:T(8,128)(2,1)} custom-call(bf16[32,40,128]{2,1,0:T(8,128)(2,1)S(1)} %all_to_all.25.got_ref, bf16[3,128,8192]{2,1,0:T(8,128)(2,1)} %design_ref.3), custom_call_target="tpu_custom_call" | custom-call | flops 100000 | bytes 1000000 | tf_op jit(solution)/shard_map/pallas_call | solution.py:371
  28.7 0.0 copy-start.4
  28.7 8.6 %all-to-all-start.1 = ((bf16[8,16,384]{2,1,0:T(8,128)(2,1)}), bf16[8,16,384]{2,1,0:T(8,128)(2,1)S(1)}, u32[]{:S(2)}, u32[]{:S(2)}) async-start(bf16[8,16,384]{2,1,0:T(8,128)(2,1)} %shard_map.140), calls=%async_computation.1 | async-start | bytes 196608 | tf_op jit(solution)/shard_map/all_to_all | solution.py:384
  37.4 0.0 copy-done.10
  37.4 0.0 copy-done.11
  37.4 0.0 copy-done.5
  37.4 0.0 copy-done.6
  37.4 2.7 %shard_map.141 = (f32[3,8,128]{2,1,0:T(8,128)S(1)}, f32[3,128,128]{2,1,0:T(8,128)S(1)}, f32[3,256,128]{2,1,0:T(8,128)S(1)}) custom-call(s32[1,1]{1,0:T(1,128)} %bitcast.2.place_ref, s32[3]{0:T(128)S(1)} %copy-done.10, s32[3]{0:T(128)S(1)} %copy-done.11, f32[3,4]{1,0:T(4,128)S(1)} %copy-done.5, f32[3,4]{1,0:T(4,128)S(1)} %copy-done.6, ...), custom_call_target="tpu_custom_call" | custom-call | flops 10000000 | bytes 1000000 | tf_op jit(solution)/shard_map/pallas_call | solution.py:371
  40.2 2.2 %all-to-all-done.1.parts_ref = bf16[8,16,384]{2,1,0:T(8,128)(2,1)S(1)} async-done(((bf16[8,16,384]{2,1,0:T(8,128)(2,1)}), bf16[8,16,384]{2,1,0:T(8,128)(2,1)S(1)}, u32[]{:S(2)}, u32[]{:S(2)}) %all-to-all-start.1) | async-done | bytes 98336 | tf_op jit(solution)/shard_map/all_to_all | solution.py:384
  42.4 0.0 copy-done.7
  42.4 0.2 shard_map.142
  42.6 13.1 %all_to_all.26.states_ref = f32[32,3,128]{2,1,0:T(4,128)S(1)} all-to-all(f32[32,3,128]{2,1,0:T(4,128)S(1)} %get-tuple-element.16), channel_id=1, replica_groups=mesh['tm_0'=4,'tm_1'=8,'order_0'=4,'order_1'=2] {'tm_0','tm_1'}, dimensions={0} | all-to-all | bytes 98304 | tf_op jit(solution)/shard_map/all_to_all | solution.py:384
  55.7 3.7 %shard_map.143 = bf16[32,16,256]{2,1,0:T(8,128)(2,1)S(1)} custom-call(f32[48,128]{1,0:T(8,128)S(1)} %get-tuple-element.13.masked_ref, f32[3,128,128]{2,1,0:T(8,128)S(1)} %get-tuple-element.14.near_ref, f32[3,256,128]{2,1,0:T(8,128)S(1)} %get-tuple-element.15.far_ref, s32[1,128]{1,0:T(1,128)S(1)} %bitcast.4, f32[32,3,128]{2,1,0:T(4,128)S(1)} %all_to_all.26.states_ref, ...), custom_call_target="tpu_custom_call" | custom-call | flops 100000 | bytes 1000000 | tf_op jit(solution)/shard_map/pallas_call | solution.py:371
  59.4 12.8 %all_to_all.27.arrived_ref = bf16[32,16,256]{2,1,0:T(8,128)(2,1)S(1)} all-to-all(bf16[32,16,256]{2,1,0:T(8,128)(2,1)S(1)} %shard_map.143), channel_id=1, replica_groups=mesh['tm_0'=4,'tm_1'=8,'order_0'=4,'order_1'=2] {'tm_0','tm_1'}, dimensions={0} | all-to-all | bytes 524288 | tf_op jit(solution)/shard_map/all_to_all | solution.py:384
  72.2 0.0 copy-done.1
  72.2 0.0 copy-done.2
  72.2 0.0 copy-done.3
  72.2 0.0 copy-done.8
  72.2 0.6 shard_map.144
  72.9 21.6 %all_to_all.28.sums_ref = f32[256,1,128]{2,1,0:T(1,128)S(1)} all-to-all(f32[256,1,128]{2,1,0:T(1,128)S(1)} %get-tuple-element.17), channel_id=1, replica_groups=mesh['tm_0'=4,'tm_1'=8,'order_0'=4,'order_1'=2] {'tm_0','tm_1','order_0'..., dimensions={0} | all-to-all | bytes 262144 | tf_op jit(solution)/shard_map/all_to_all | solution.py:384
  94.4 0.0 copy-done.4
  94.4 1.0 %shard_map.145 = (f32[16,1,256]{2,1,0:T(1,128)}, f32[16,1,256]{2,1,0:T(1,128)}, f32[16,1,256]{2,1,0:T(1,128)}) custom-call(f32[256,1,128]{2,1,0:T(1,128)S(1)} %all_to_all.28.sums_ref, f32[16,256]{1,0:T(8,128)S(1)} %get-tuple-element.18.image_ref, f32[16,256]{1,0:T(8,128)S(1)} %get-tuple-element.19.applied_ref, f32[16,256]{1,0:T(8,128)S(1)} %get-tuple-element.20.both_ref, ...), custom_call_target="tpu_custom_call" | custom-call | flops 100000 | bytes 1000000 | tf_op jit(solution)/shard_map/pallas_call | solution.py:371
  (5 shorter events, 0.0 us)
Async XLA Ops:
  0.6 36.8 %copy-start.10 = (s32[3]{0:T(128)S(1)}, s32[3]{0:T(128)}, u32[]{:S(2)}) copy-start(s32[3]{0:T(128)} %aro_ref.1) | copy-start | bytes 40
  0.6 36.7 %copy-start.11 = (s32[3]{0:T(128)S(1)}, s32[3]{0:T(128)}, u32[]{:S(2)}) copy-start(s32[3]{0:T(128)} %mao_ref.1) | copy-start | bytes 40
  0.7 41.7 %copy-start.7 = (s32[128]{0:T(128)S(1)}, s32[128]{0:T(128)}, u32[]{:S(2)}) copy-start(s32[128]{0:T(128)} %param.13) | copy-start | bytes 1540
  0.7 0.7 copy-start
  1.4 0.7 copy-start.9
  2.1 35.3 %copy-start.5 = (f32[3,4]{1,0:T(4,128)S(1)}, f32[3,4]{1,0:T(4,128)}, u32[]{:S(2)}) copy-start(f32[3,4]{1,0:T(4,128)} %arr_ref.1) | copy-start | bytes 148
  2.1 35.3 %copy-start.6 = (f32[3,4]{1,0:T(4,128)S(1)}, f32[3,4]{1,0:T(4,128)}, u32[]{:S(2)}) copy-start(f32[3,4]{1,0:T(4,128)} %mar_ref.1) | copy-start | bytes 148
  24.1 48.1 %copy-start.1 = (f32[16,1,256]{2,1,0:T(1,128)S(1)}, f32[16,1,256]{2,1,0:T(1,128)}, u32[]{:S(2)}) copy-start(f32[16,1,256]{2,1,0:T(1,128)} %direction_ref.5) | copy-start | bytes 49156
  24.1 48.1 %copy-start.2 = (f32[1,2,128,128]{3,2,1,0:T(8,128)S(1)}, f32[1,2,128,128]{3,2,1,0:T(8,128)}, u32[]{:S(2)}) copy-start(f32[1,2,128,128]{3,2,1,0:T(8,128)} %precond_ref.1) | copy-start | bytes 393220
  24.1 48.1 %copy-start.3 = (f32[16,1,256]{2,1,0:T(1,128)S(1)}, f32[16,1,256]{2,1,0:T(1,128)}, u32[]{:S(2)}) copy-start(f32[16,1,256]{2,1,0:T(1,128)} %residual_ref.3) | copy-start | bytes 49156
  24.1 48.1 %copy-start.8 = (f32[1,256]{1,0:T(1,128)S(1)}, f32[1,256]{1,0:T(1,128)}, u32[]{:S(2)}) copy-start(f32[1,256]{1,0:T(1,128)} %kaula_ref.1) | copy-start | bytes 3076
  28.7 65.7 %copy-start.4 = (f32[16,1,256]{2,1,0:T(1,128)S(1)}, f32[16,1,256]{2,1,0:T(1,128)}, u32[]{:S(2)}) copy-start(f32[16,1,256]{2,1,0:T(1,128)} %solution_ref.1) | copy-start | bytes 49156
  28.7 13.6 %all-to-all-start.1 = ((bf16[8,16,384]{2,1,0:T(8,128)(2,1)}), bf16[8,16,384]{2,1,0:T(8,128)(2,1)S(1)}, u32[]{:S(2)}, u32[]{:S(2)}) async-start(bf16[8,16,384]{2,1,0:T(8,128)(2,1)} %shard_map.140), calls=%async_computation.1 | async-start | bytes 196608 | tf_op jit(solution)/shard_map/all_to_all | solution.py:384

commit v5 on v4

--- a/solution.py
+++ b/solution.py
@@ -149,7 +149,7 @@
 
 
 def segment_kernel(
-    place_ref, got_ref, toep_ref, gam_ref, fin_ref, reach_ref, pow_ref, gram_ref, own_ref, near_ref, far_ref
+    place_ref, got_ref, toep_ref, gam_ref, fin_ref, reach_ref, pow_ref, gram_ref, own_ref, near_ref, link_ref, edge_ref
 ):
     place = place_ref[0, 0]
     row = lax.broadcasted_iota(jnp.int32, (8, 128), 0)
@@ -174,7 +174,15 @@
     ends_before = pltpu.roll(ends, 1, 0)
     keep_past = jnp.where((peer < place) & (ends == prev), 1.0, 0.0)
     keep_next = jnp.where((peer > place) & (ends_before == last), 1.0, 0.0)
-    keep = jnp.concatenate([keep_past] * 4 + [keep_next] * 4, axis=0)
+    wide_past = jnp.concatenate([keep_past, jnp.zeros((96, 128), jnp.float32)], axis=0).T[0:1, :]
+    wide_next = jnp.concatenate([keep_next, jnp.zeros((96, 128), jnp.float32)], axis=0).T[0:1, :]
+    keeps = []
+    for wide_keep in (wide_past, wide_next):
+        part = wide_keep
+        for turn in (32, 64, 96):
+            part = part + pltpu.roll(wide_keep, turn, 1)
+        keeps.append(part)
+    keep = jnp.concatenate(keeps, axis=1)
     gram = {at: jnp.zeros((8, 128), jnp.float32) for at in UPPER}
     for k in range(LEVELS - 1):
         power = {pair: pow_ref[k, at] for at, pair in enumerate(LOWER)}
@@ -213,7 +221,8 @@
         fin_low = rows(fin, c, 0)
         near_ref[c] = dot(toep, toep, ((1,), (1,))) + dot(rows(fold, c, 0), fin_low, ((0,), (0,)))
         own_ref[c] = fin_low + pltpu.roll(out_p, 4, 0)
-        far_ref[c] = keep * dot(reach_ref[c], out_p + rows(fin, c, 4), ((0,), (0,)))
+        edge_ref[c] = out_p + rows(fin, c, 4)
+        link_ref[c] = reach_ref[c] * keep
 
 
 def state_kernel(parts_ref, gaps_ref, own_ref, message_ref, masked_ref):
@@ -233,23 +242,68 @@
     message_ref[...] = jnp.broadcast_to(jnp.concatenate(rows, axis=0)[None], message_ref.shape)
 
 
-def weighted_rows(masked_ref, near_ref, far_ref, gaps_ref, states_ref):
+def split_in_two(value):
+    high = value.astype(jnp.bfloat16)
+    return high, (value - high.astype(jnp.float32)).astype(jnp.bfloat16)
+
+
+def spread_kernel(
+    masked_ref, near_ref, edge_ref, gaps_ref, design_ref, here_ref, basis_ref, held_ref, sems
+):
+    copies = chunk_copies(design_ref, held_ref, sems)
+    for copy in copies:
+        copy.start()
     gaps = gaps_ref[...].astype(jnp.float32)
     pieces = []
+    highs, lows = [], []
+    blank = jnp.zeros((8, 128), jnp.bfloat16)
     for c in range(3):
-        here = dot(masked_ref[16 * c : 16 * c + 16, :], near_ref[c], ((1,), (0,)))
+        pieces.append(dot(masked_ref[16 * c : 16 * c + 16, :], near_ref[c], ((1,), (0,))) * gaps)
+        high, low = split_in_two(edge_ref[c] * gaps)
+        highs.append(jnp.concatenate([high if d == c else blank for d in range(3)], axis=1))
+        lows.append(jnp.concatenate([low if d == c else blank for d in range(3)], axis=1))
+    rows = jnp.concatenate(
+        [*split_in_two(jnp.concatenate(pieces, axis=1)), *highs, *lows], axis=0
+    )
+    count, _, _, width = held_ref.shape
+    for k in range(count):
+        copies[k].wait()
+        found = jnp.dot(
+            rows, held_ref[k].reshape(384, width), preferred_element_type=jnp.float32
+        )
+        here_ref[:, width * k : width * k + width] = found[0:16] + found[16:32]
+        high, low = split_in_two(found[32:56] + found[56:80])
+        basis_ref[0:24, width * k : width * k + width] = high
+        basis_ref[24:48, width * k : width * k + width] = low
+        basis_ref[48:72, width * k : width * k + width] = high
+
+
+def gradient_kernel(states_ref, link_ref, here_ref, basis_ref, out_ref):
+    parts = []
+    for c in range(3):
         states = states_ref[:, c, :]
         turned = [states] + [pltpu.roll(states, 128 - 16 * i, 1) for i in range(1, 8)]
-        there = dot(jnp.concatenate(turned, axis=0), far_ref[c], ((0,), (0,)))[0:16, :]
-        pieces.append((here + there) * gaps)
-    return pieces
+        parts.append(dot(link_ref[c], jnp.concatenate(turned, axis=0), ((1,), (0,))))
+    found = jnp.concatenate(parts, axis=0)
+    high = found.astype(jnp.bfloat16).astype(jnp.float32)
+    tall = jnp.concatenate(
+        [high, high, found - high, jnp.zeros((56, 128), jnp.float32)], axis=0
+    )
+    left = tall.T[0:16, 0:72].astype(jnp.bfloat16)
+    peers = out_ref.shape[0]
+    for p in range(0, peers, 4):
+        span = slice(256 * p, 256 * p + 1024)
+        there = jnp.dot(left, basis_ref[:, span], preferred_element_type=jnp.float32)
+        whole = (here_ref[:, span] + there).astype(out_ref.dtype)
+        for q in range(4):
+            out_ref[p + q] = whole[:, 256 * q : 256 * q + 256]
 
 
 def tables_kernel(
-    place_ref, aro_ref, mao_ref, arr_ref, mar_ref, got_ref, own_ref, near_ref, far_ref, *tables
+    place_ref, aro_ref, mao_ref, arr_ref, mar_ref, got_ref, own_ref, near_ref, link_ref, edge_ref, *tables
 ):
     response_kernel(place_ref, aro_ref, mao_ref, arr_ref, mar_ref, *tables)
-    segment_kernel(place_ref, got_ref, *tables, own_ref, near_ref, far_ref)
+    segment_kernel(place_ref, got_ref, *tables, own_ref, near_ref, link_ref, edge_ref)
 
 
 def pack_kernel(direction_ref, ids_ref, out_ref):
@@ -291,25 +345,6 @@
     out_ref[...] = jnp.broadcast_to(total.astype(jnp.bfloat16)[None], out_ref.shape)
 
 
-def gradient_kernel(
-    masked_ref, near_ref, far_ref, gaps_ref, states_ref, design_ref, out_ref, held_ref, sems
-):
-    copies = chunk_copies(design_ref, held_ref, sems)
-    for copy in copies:
-        copy.start()
-    pieces = weighted_rows(masked_ref, near_ref, far_ref, gaps_ref, states_ref)
-    weighted = jnp.concatenate(pieces, axis=1).astype(jnp.bfloat16)
-    count, _, _, width = held_ref.shape
-    peers = width // 256
-    for k in range(count):
-        copies[k].wait()
-        part = jnp.dot(
-            weighted, held_ref[k].reshape(384, width), preferred_element_type=jnp.float32
-        ).astype(jnp.bfloat16)
-        for p in range(peers):
-            out_ref[peers * k + p] = part[:, 256 * p : 256 * p + 256]
-
-
 def image_kernel(
     arrived_ref, kaula_ref, precond_ref, residual_ref, direction_ref, message_ref, image_ref, applied_ref, both_ref
 ):
@@ -427,9 +462,9 @@
         limit=VMEM_LIMIT,
     )
     parts = exchange(partial, ORDER)
-    own, near, far = run(
+    own, near, link, edge = run(
         tables_kernel,
-        [((3, 8, 128), f32), ((3, 128, 128), f32), ((3, 256, 128), f32)],
+        [((3, 8, 128), f32), ((3, 128, 128), f32), ((3, 8, 256), f32), ((3, 8, 128), f32)],
         [place, ar_order, ma_order, ar_roots, ma_roots, got],
         scalars=(0, 1, 2, 3, 4),
         scratch=[
@@ -446,13 +481,20 @@
         state_kernel, [((count, 3, 128), f32), ((48, 128), f32)], [parts, gaps, own]
     )
     states = exchange(message, TM)
+    here, basis = run(
+        spread_kernel,
+        [((16, design.shape[2]), f32), ((72, design.shape[2]), bf16)],
+        [masked, near, edge, gaps, design],
+        anywhere=(4,),
+        scratch=held(8),
+        flops=10000000,
+        limit=VMEM_LIMIT,
+    )
     (gradient,) = run(
         gradient_kernel,
         [((count, 16, 256), bf16)],
-        [masked, near, far, gaps, states, design],
-        anywhere=(5,),
-        scratch=held(8),
-        limit=VMEM_LIMIT,
+        [states, link, here, basis],
+        limit=16 * 1024 * 1024,
     )
     arrived = exchange(gradient, TM)
     sums, image, applied, image_applied = run(

time: 95.8 us -> 94.5 us (0.986)
  blocking collectives: 69.5 us -> 57 us
  waiting for transfers between devices: 2.21 us -> 8.04 us
  starting transfers between devices: 8.65 us -> 13.2 us
    all_to_all x4 -> x3, blocking collectives: 69.5 us -> 57 us  [exchange(): return lax.all_to_all(value, axes, split_axis=0, concat_axis=0, tiled=True)]
    all_to_all x1 -> x2, waiting for transfers between devices: 2.21 us -> 8.04 us  [exchange(): return lax.all_to_all(value, axes, split_axis=0, concat_axis=0, tiled=True)]
    all_to_all x1 -> x2, starting transfers between devices: 8.65 us -> 13.2 us  [exchange(): return lax.all_to_all(value, axes, split_axis=0, concat_axis=0, tiled=True)]
    pallas_call x7 -> x8, Pallas kernels: 12.9 us -> 13.5 us  [run(): pl.pallas_call(kernel, out_shape=shapes, in_specs=[pl.BlockSpec(memory_sp...]
  transfers between devices with their start and end apart: 1 -> 2, of which waited for: 1 -> 2; matrix products, arithmetic and copies ran while one was open for 0% -> 0% of each run, Pallas kernels for 3% -> 6%
where the time goes in v5:
time: 94.5 us; the launch traced here: 94 us
  blocking collectives  57 us (60%)
  Pallas kernels  13.5 us (14%)
  starting transfers between devices  13.2 us (14%)
  waiting for transfers between devices  8.04 us (9%)
  local copies, waits for them, and re-layouts  1.43 us (2%)
    all_to_all x3, blocking collectives, exchange(): return lax.all_to_all(value, axes, split_axis=0, concat_axis=0, tiled=True)  57 us
    pallas_call x8, Pallas kernels, run(): pl.pallas_call(kernel, out_shape=shapes, in_specs=[pl.BlockSpec(memory_sp...  13.5 us
    all_to_all x2, starting transfers between devices, exchange(): return lax.all_to_all(value, axes, split_axis=0, concat_axis=0, tiled=True)  13.2 us
    all_to_all x2, waiting for transfers between devices, exchange(): return lax.all_to_all(value, axes, split_axis=0, concat_axis=0, tiled=True)  8.04 us
  transfers between devices with their start and end apart: 2, of which 2 were waited for; matrix products, arithmetic and copies ran while one was open for 0% of the time, Pallas kernels for 6%

profile of v5, /device:TPU:1, one launch (start us, length us, event | category | flops | bytes accessed | tf_op | source)
XLA Modules:
  0.0 94.0 jit_solution(5012788168591365704)
XLA Ops:
  0.6 0.0 copy-start.11
  0.6 0.0 copy-start.10
  0.7 0.0 copy-start.7
  0.7 0.0 copy-start
  0.7 0.7 copy-done
  1.4 0.7 copy-done.9
  2.1 0.1 shard_map.139
  2.1 22.0 %all_to_all.25.got_ref = bf16[32,40,128]{2,1,0:T(8,128)(2,1)S(1)} all-to-all(bf16[32,40,128]{2,1,0:T(8,128)(2,1)S(1)} %shard_map.139), channel_id=1, replica_groups=mesh['tm_0'=4,'tm_1'=8,'order_0'=4,'order_1'=2] {'tm_0','tm_1'}, dimensions={0} | all-to-all | bytes 655360 | tf_op jit(solution)/shard_map/all_to_all | solution.py:419
  24.1 4.5 %shard_map.140 = bf16[8,16,384]{2,1,0:T(8,128)(2,1)} custom-call(bf16[32,40,128]{2,1,0:T(8,128)(2,1)S(1)} %all_to_all.25.got_ref, bf16[3,128,8192]{2,1,0:T(8,128)(2,1)} %design_ref.3), custom_call_target="tpu_custom_call" | custom-call | flops 100000 | bytes 1000000 | tf_op jit(solution)/shard_map/pallas_call | solution.py:406
  28.7 0.0 copy-start.1
  28.7 0.0 copy-start.2
  28.7 0.0 copy-start.3
  28.7 0.0 copy-start.8
  28.7 0.0 copy-start.4
  28.7 8.8 %all-to-all-start.1 = ((bf16[8,16,384]{2,1,0:T(8,128)(2,1)}), bf16[8,16,384]{2,1,0:T(8,128)(2,1)S(1)}, u32[]{:S(2)}, u32[]{:S(2)}) async-start(bf16[8,16,384]{2,1,0:T(8,128)(2,1)} %shard_map.140), calls=%async_computation.1 | async-start | bytes 196608 | tf_op jit(solution)/shard_map/all_to_all | solution.py:419
  37.5 0.0 copy-done.11
  37.5 0.0 copy-done.10
  37.5 0.0 copy-done.5
  37.5 0.0 copy-done.6
  37.5 2.1 %shard_map.141 = (f32[3,8,128]{2,1,0:T(8,128)S(1)}, f32[3,128,128]{2,1,0:T(8,128)S(1)}, f32[3,8,256]{2,1,0:T(8,128)S(1)}, f32[3,8,128]{2,1,0:T(8,128)S(1)}) custom-call(s32[1,1]{1,0:T(1,128)} %bitcast.2.place_ref, s32[3]{0:T(128)S(1)} %copy-done.10, s32[3]{0:T(128)S(1)} %copy-done.11, f32[3,4]{1,0:T(4,128)S(1)} %copy-done.5, f32[3,4]{1,0:T(4,128)S(1)} %copy-done.6, ...), custom_call_target="tpu_custom_call" | custom-call | flops 10000000 | bytes 1000000 | tf_op jit(solution)/shard_map/pallas_call | solution.py:406
  39.7 2.8 %all-to-all-done.1.parts_ref = bf16[8,16,384]{2,1,0:T(8,128)(2,1)S(1)} async-done(((bf16[8,16,384]{2,1,0:T(8,128)(2,1)}), bf16[8,16,384]{2,1,0:T(8,128)(2,1)S(1)}, u32[]{:S(2)}, u32[]{:S(2)}) %all-to-all-start.1) | async-done | bytes 98336 | tf_op jit(solution)/shard_map/all_to_all | solution.py:419
  42.5 0.9 shard_map.142
  43.4 4.4 %all-to-all-start.2 = ((f32[32,3,128]{2,1,0:T(4,128)}), f32[32,3,128]{2,1,0:T(4,128)S(1)}, u32[]{:S(2)}, u32[]{:S(2)}) async-start(f32[32,3,128]{2,1,0:T(4,128)} %get-tuple-element.16), calls=%async_computation.2 | async-start | bytes 131072 | tf_op jit(solution)/shard_map/all_to_all | solution.py:419
  47.8 3.6 %shard_map.143 = (f32[16,8192]{1,0:T(8,128)S(1)}, bf16[72,8192]{1,0:T(8,128)(2,1)S(1)}) custom-call(f32[48,128]{1,0:T(8,128)S(1)} %get-tuple-element.18.masked_ref, f32[3,128,128]{2,1,0:T(8,128)S(1)} %get-tuple-element.19.near_ref, f32[3,8,128]{2,1,0:T(8,128)S(1)} %get-tuple-element.20.edge_ref, s32[1,128]{1,0:T(1,128)S(1)} %bitcast.4, ...), custom_call_target="tpu_custom_call" | custom-call | flops 10000000 | bytes 1000000 | tf_op jit(solution)/shard_map/pallas_call | solution.py:406
  51.4 5.2 %all-to-all-done.2.states_ref = f32[32,3,128]{2,1,0:T(4,128)S(1)} async-done(((f32[32,3,128]{2,1,0:T(4,128)}), f32[32,3,128]{2,1,0:T(4,128)S(1)}, u32[]{:S(2)}, u32[]{:S(2)}) %all-to-all-start.2) | async-done | bytes 49184 | tf_op jit(solution)/shard_map/all_to_all | solution.py:419
  56.6 0.7 shard_map.144
  57.4 13.4 %all_to_all.26.arrived_ref = bf16[32,16,256]{2,1,0:T(8,128)(2,1)S(1)} all-to-all(bf16[32,16,256]{2,1,0:T(8,128)(2,1)S(1)} %shard_map.144), channel_id=1, replica_groups=mesh['tm_0'=4,'tm_1'=8,'order_0'=4,'order_1'=2] {'tm_0','tm_1'}, dimensions={0} | all-to-all | bytes 524288 | tf_op jit(solution)/shard_map/all_to_all | solution.py:419
  70.8 0.0 copy-done.2
  70.8 0.6 shard_map.145
  71.5 21.6 %all_to_all.27.sums_ref = f32[256,1,128]{2,1,0:T(1,128)S(1)} all-to-all(f32[256,1,128]{2,1,0:T(1,128)S(1)} %get-tuple-element.23), channel_id=1, replica_groups=mesh['tm_0'=4,'tm_1'=8,'order_0'=4,'order_1'=2] {'tm_0','tm_1','order_0'..., dimensions={0} | all-to-all | bytes 262144 | tf_op jit(solution)/shard_map/all_to_all | solution.py:419
  93.0 0.0 copy-done.4
  93.0 1.0 %shard_map.146 = (f32[16,1,256]{2,1,0:T(1,128)}, f32[16,1,256]{2,1,0:T(1,128)}, f32[16,1,256]{2,1,0:T(1,128)}) custom-call(f32[256,1,128]{2,1,0:T(1,128)S(1)} %all_to_all.27.sums_ref, f32[16,256]{1,0:T(8,128)S(1)} %get-tuple-element.24.image_ref, f32[16,256]{1,0:T(8,128)S(1)} %get-tuple-element.25.applied_ref, f32[16,256]{1,0:T(8,128)S(1)} %get-tuple-element.26.both_ref, ...), custom_call_target="tpu_custom_call" | custom-call | flops 100000 | bytes 1000000 | tf_op jit(solution)/shard_map/pallas_call | solution.py:406
  (7 shorter events, 0.0 us)
Async XLA Ops:
  0.6 36.9 %copy-start.11 = (s32[3]{0:T(128)S(1)}, s32[3]{0:T(128)}, u32[]{:S(2)}) copy-start(s32[3]{0:T(128)} %mao_ref.1) | copy-start | bytes 40
  0.6 36.9 %copy-start.10 = (s32[3]{0:T(128)S(1)}, s32[3]{0:T(128)}, u32[]{:S(2)}) copy-start(s32[3]{0:T(128)} %aro_ref.1) | copy-start | bytes 40
  0.7 41.8 %copy-start.7 = (s32[128]{0:T(128)S(1)}, s32[128]{0:T(128)}, u32[]{:S(2)}) copy-start(s32[128]{0:T(128)} %param.13) | copy-start | bytes 1540
  0.7 0.7 copy-start
  1.4 0.7 copy-start.9
  2.1 35.5 %copy-start.5 = (f32[3,4]{1,0:T(4,128)S(1)}, f32[3,4]{1,0:T(4,128)}, u32[]{:S(2)}) copy-start(f32[3,4]{1,0:T(4,128)} %arr_ref.1) | copy-start | bytes 148
  2.1 35.5 %copy-start.6 = (f32[3,4]{1,0:T(4,128)S(1)}, f32[3,4]{1,0:T(4,128)}, u32[]{:S(2)}) copy-start(f32[3,4]{1,0:T(4,128)} %mar_ref.1) | copy-start | bytes 148
  28.7 42.1 %copy-start.1 = (f32[16,1,256]{2,1,0:T(1,128)S(1)}, f32[16,1,256]{2,1,0:T(1,128)}, u32[]{:S(2)}) copy-start(f32[16,1,256]{2,1,0:T(1,128)} %direction_ref.5) | copy-start | bytes 49156
  28.7 42.1 %copy-start.2 = (f32[1,2,128,128]{3,2,1,0:T(8,128)S(1)}, f32[1,2,128,128]{3,2,1,0:T(8,128)}, u32[]{:S(2)}) copy-start(f32[1,2,128,128]{3,2,1,0:T(8,128)} %precond_ref.1) | copy-start | bytes 393220
  28.7 42.1 %copy-start.3 = (f32[16,1,256]{2,1,0:T(1,128)S(1)}, f32[16,1,256]{2,1,0:T(1,128)}, u32[]{:S(2)}) copy-start(f32[16,1,256]{2,1,0:T(1,128)} %residual_ref.3) | copy-start | bytes 49156
  28.7 42.1 %copy-start.8 = (f32[1,256]{1,0:T(1,128)S(1)}, f32[1,256]{1,0:T(1,128)}, u32[]{:S(2)}) copy-start(f32[1,256]{1,0:T(1,128)} %kaula_ref.1) | copy-start | bytes 3076
  28.7 64.3 %copy-start.4 = (f32[16,1,256]{2,1,0:T(1,128)S(1)}, f32[16,1,256]{2,1,0:T(1,128)}, u32[]{:S(2)}) copy-start(f32[16,1,256]{2,1,0:T(1,128)} %solution_ref.1) | copy-start | bytes 49156
  28.7 13.8 %all-to-all-start.1 = ((bf16[8,16,384]{2,1,0:T(8,128)(2,1)}), bf16[8,16,384]{2,1,0:T(8,128)(2,1)S(1)}, u32[]{:S(2)}, u32[]{:S(2)}) async-start(bf16[8,16,384]{2,1,0:T(8,128)(2,1)} %shard_map.140), calls=%async_computation.1 | async-start | bytes 196608 | tf_op jit(solution)/shard_map/all_to_all | solution.py:419
  43.4 13.3 %all-to-all-start.2 = ((f32[32,3,128]{2,1,0:T(4,128)}), f32[32,3,128]{2,1,0:T(4,128)S(1)}, u32[]{:S(2)}, u32[]{:S(2)}) async-start(f32[32,3,128]{2,1,0:T(4,128)} %get-tuple-element.16), calls=%async_computation.2 | async-start | bytes 131072 | tf_op jit(solution)/shard_map/all_to_all | solution.py:419

commit v6 on v5

--- a/solution.py
+++ b/solution.py
@@ -306,7 +306,15 @@
     segment_kernel(place_ref, got_ref, *tables, own_ref, near_ref, link_ref, edge_ref)
 
 
-def pack_kernel(direction_ref, ids_ref, out_ref):
+def pack_kernel(direction_any, ids_any, out_ref, direction_ref, ids_ref, sems):
+    copies = [
+        pltpu.make_async_copy(direction_any, direction_ref, sems.at[0]),
+        pltpu.make_async_copy(ids_any, ids_ref, sems.at[1]),
+    ]
+    for copy in copies:
+        copy.start()
+    for copy in copies:
+        copy.wait()
     packed = direction_ref[:, 0, :].astype(jnp.bfloat16)
     ids = jnp.broadcast_to(ids_ref[...].astype(jnp.float32), (8, 128)).astype(jnp.bfloat16)
     sheet = jnp.concatenate([packed[:, :128], packed[:, 128:], ids], axis=0)
@@ -442,7 +450,16 @@
     (sheets,) = run(
         pack_kernel,
         [((count, 40, 128), bf16)],
-        [direction, segment_ids.reshape(1, 128)],
+        [
+            pltpu.with_memory_space_constraint(direction, pltpu.HBM),
+            pltpu.with_memory_space_constraint(segment_ids.reshape(1, 128), pltpu.HBM),
+        ],
+        anywhere=(0, 1),
+        scratch=[
+            pltpu.VMEM((16, 1, 256), f32),
+            pltpu.VMEM((1, 128), jnp.int32),
+            pltpu.SemaphoreType.DMA((2,)),
+        ],
         limit=VMEM_LIMIT,
     )
     got = exchange(sheets, TM)

time: 94.5 us -> 93.8 us (level)
  local copies, waits for them, and re-layouts: 1.43 us -> 0.05 us
    unnamed x24 -> x20, local copies, waits for them, and re-layouts: 1.43 us -> 0.05 us
where the time goes in v6:
time: 93.8 us; the launch traced here: 93.4 us
  blocking collectives  57 us (61%)
  Pallas kernels  14.3 us (15%)
  starting transfers between devices  13.2 us (14%)
  waiting for transfers between devices  8.04 us (9%)
    all_to_all x3, blocking collectives, exchange(): return lax.all_to_all(value, axes, split_axis=0, concat_axis=0, tiled=True)  57 us
    pallas_call x8, Pallas kernels, run(): pl.pallas_call(kernel, out_shape=shapes, in_specs=[pl.BlockSpec(memory_sp...  14.3 us
    all_to_all x2, starting transfers between devices, exchange(): return lax.all_to_all(value, axes, split_axis=0, concat_axis=0, tiled=True)  13.2 us
    all_to_all x2, waiting for transfers between devices, exchange(): return lax.all_to_all(value, axes, split_axis=0, concat_axis=0, tiled=True)  8.04 us
  transfers between devices with their start and end apart: 2, of which 2 were waited for; matrix products, arithmetic and copies ran while one was open for 0% of the time, Pallas kernels for 6%

profile of v6, /device:TPU:1, one launch (start us, length us, event | category | flops | bytes accessed | tf_op | source)
XLA Modules:
  0.0 93.4 jit_solution(3419857268727864123)
XLA Ops:
  0.6 0.0 copy-start.5
  0.6 0.0 copy-start.4
  0.7 0.0 copy-start.9
  0.7 0.0 copy-start.8
  0.7 0.0 copy-start.6
  0.7 0.8 shard_map.139
  1.5 22.0 %all_to_all.25.got_ref = bf16[32,40,128]{2,1,0:T(8,128)(2,1)S(1)} all-to-all(bf16[32,40,128]{2,1,0:T(8,128)(2,1)S(1)} %shard_map.139), channel_id=1, replica_groups=mesh['tm_0'=4,'tm_1'=8,'order_0'=4,'order_1'=2] {'tm_0','tm_1'}, dimensions={0} | all-to-all | bytes 655360 | tf_op jit(solution)/shard_map/all_to_all | solution.py:427
  23.5 4.5 %shard_map.140 = bf16[8,16,384]{2,1,0:T(8,128)(2,1)} custom-call(bf16[32,40,128]{2,1,0:T(8,128)(2,1)S(1)} %all_to_all.25.got_ref, bf16[3,128,8192]{2,1,0:T(8,128)(2,1)} %design_ref.3), custom_call_target="tpu_custom_call" | custom-call | flops 100000 | bytes 1000000 | tf_op jit(solution)/shard_map/pallas_call | solution.py:414
  28.1 0.0 copy-start
  28.1 0.0 copy-start.1
  28.1 0.0 copy-start.2
  28.1 0.0 copy-start.7
  28.1 0.0 copy-start.3
  28.1 8.8 %all-to-all-start.1 = ((bf16[8,16,384]{2,1,0:T(8,128)(2,1)}), bf16[8,16,384]{2,1,0:T(8,128)(2,1)S(1)}, u32[]{:S(2)}, u32[]{:S(2)}) async-start(bf16[8,16,384]{2,1,0:T(8,128)(2,1)} %shard_map.140), calls=%async_computation.1 | async-start | bytes 196608 | tf_op jit(solution)/shard_map/all_to_all | solution.py:427
  36.9 0.0 copy-done.5
  36.9 0.0 copy-done.4
  36.9 0.0 copy-done.9
  36.9 0.0 copy-done.8
  36.9 2.1 %shard_map.141 = (f32[3,8,128]{2,1,0:T(8,128)S(1)}, f32[3,128,128]{2,1,0:T(8,128)S(1)}, f32[3,8,256]{2,1,0:T(8,128)S(1)}, f32[3,8,128]{2,1,0:T(8,128)S(1)}) custom-call(s32[1,1]{1,0:T(1,128)} %bitcast.2.place_ref, s32[3]{0:T(128)S(1)} %copy-done.8, s32[3]{0:T(128)S(1)} %copy-done.9, f32[3,4]{1,0:T(4,128)S(1)} %copy-done.4, f32[3,4]{1,0:T(4,128)S(1)} %copy-done.5, ...), custom_call_target="tpu_custom_call" | custom-call | flops 10000000 | bytes 1000000 | tf_op jit(solution)/shard_map/pallas_call | solution.py:414
  39.1 2.8 %all-to-all-done.1.parts_ref = bf16[8,16,384]{2,1,0:T(8,128)(2,1)S(1)} async-done(((bf16[8,16,384]{2,1,0:T(8,128)(2,1)}), bf16[8,16,384]{2,1,0:T(8,128)(2,1)S(1)}, u32[]{:S(2)}, u32[]{:S(2)}) %all-to-all-start.1) | async-done | bytes 98336 | tf_op jit(solution)/shard_map/all_to_all | solution.py:427
  41.9 0.0 copy-done.6
  41.9 0.9 shard_map.142
  42.8 4.4 %all-to-all-start.2 = ((f32[32,3,128]{2,1,0:T(4,128)}), f32[32,3,128]{2,1,0:T(4,128)S(1)}, u32[]{:S(2)}, u32[]{:S(2)}) async-start(f32[32,3,128]{2,1,0:T(4,128)} %get-tuple-element.16), calls=%async_computation.2 | async-start | bytes 131072 | tf_op jit(solution)/shard_map/all_to_all | solution.py:427
  47.2 3.6 %shard_map.143 = (f32[16,8192]{1,0:T(8,128)S(1)}, bf16[72,8192]{1,0:T(8,128)(2,1)S(1)}) custom-call(f32[48,128]{1,0:T(8,128)S(1)} %get-tuple-element.18.masked_ref, f32[3,128,128]{2,1,0:T(8,128)S(1)} %get-tuple-element.19.near_ref, f32[3,8,128]{2,1,0:T(8,128)S(1)} %get-tuple-element.20.edge_ref, s32[1,128]{1,0:T(1,128)S(1)} %bitcast.4, ...), custom_call_target="tpu_custom_call" | custom-call | flops 10000000 | bytes 1000000 | tf_op jit(solution)/shard_map/pallas_call | solution.py:414
  50.8 5.2 %all-to-all-done.2.states_ref = f32[32,3,128]{2,1,0:T(4,128)S(1)} async-done(((f32[32,3,128]{2,1,0:T(4,128)}), f32[32,3,128]{2,1,0:T(4,128)S(1)}, u32[]{:S(2)}, u32[]{:S(2)}) %all-to-all-start.2) | async-done | bytes 49184 | tf_op jit(solution)/shard_map/all_to_all | solution.py:427
  56.1 0.7 shard_map.144
  56.8 13.5 %all_to_all.26.arrived_ref = bf16[32,16,256]{2,1,0:T(8,128)(2,1)S(1)} all-to-all(bf16[32,16,256]{2,1,0:T(8,128)(2,1)S(1)} %shard_map.144), channel_id=1, replica_groups=mesh['tm_0'=4,'tm_1'=8,'order_0'=4,'order_1'=2] {'tm_0','tm_1'}, dimensions={0} | all-to-all | bytes 524288 | tf_op jit(solution)/shard_map/all_to_all | solution.py:427
  70.2 0.0 copy-done
  70.2 0.0 copy-done.7
  70.2 0.6 shard_map.145
  70.9 21.6 %all_to_all.27.sums_ref = f32[256,1,128]{2,1,0:T(1,128)S(1)} all-to-all(f32[256,1,128]{2,1,0:T(1,128)S(1)} %get-tuple-element.23), channel_id=1, replica_groups=mesh['tm_0'=4,'tm_1'=8,'order_0'=4,'order_1'=2] {'tm_0','tm_1','order_0'..., dimensions={0} | all-to-all | bytes 262144 | tf_op jit(solution)/shard_map/all_to_all | solution.py:427
  92.4 1.0 %shard_map.146 = (f32[16,1,256]{2,1,0:T(1,128)}, f32[16,1,256]{2,1,0:T(1,128)}, f32[16,1,256]{2,1,0:T(1,128)}) custom-call(f32[256,1,128]{2,1,0:T(1,128)S(1)} %all_to_all.27.sums_ref, f32[16,256]{1,0:T(8,128)S(1)} %get-tuple-element.24.image_ref, f32[16,256]{1,0:T(8,128)S(1)} %get-tuple-element.25.applied_ref, f32[16,256]{1,0:T(8,128)S(1)} %get-tuple-element.26.both_ref, ...), custom_call_target="tpu_custom_call" | custom-call | flops 100000 | bytes 1000000 | tf_op jit(solution)/shard_map/pallas_call | solution.py:414
  (3 shorter events, 0.0 us)
Async XLA Ops:
  0.6 36.3 %copy-start.5 = (f32[3,4]{1,0:T(4,128)S(1)}, f32[3,4]{1,0:T(4,128)}, u32[]{:S(2)}) copy-start(f32[3,4]{1,0:T(4,128)} %mar_ref.1) | copy-start | bytes 148
  0.6 36.3 %copy-start.4 = (f32[3,4]{1,0:T(4,128)S(1)}, f32[3,4]{1,0:T(4,128)}, u32[]{:S(2)}) copy-start(f32[3,4]{1,0:T(4,128)} %arr_ref.1) | copy-start | bytes 148
  0.7 36.3 %copy-start.9 = (s32[3]{0:T(128)S(1)}, s32[3]{0:T(128)}, u32[]{:S(2)}) copy-start(s32[3]{0:T(128)} %mao_ref.1) | copy-start | bytes 40
  0.7 36.3 %copy-start.8 = (s32[3]{0:T(128)S(1)}, s32[3]{0:T(128)}, u32[]{:S(2)}) copy-start(s32[3]{0:T(128)} %aro_ref.1) | copy-start | bytes 40
  0.7 41.2 %copy-start.6 = (s32[128]{0:T(128)S(1)}, s32[128]{0:T(128)}, u32[]{:S(2)}) copy-start(s32[128]{0:T(128)} %param.13) | copy-start | bytes 1540
  28.1 42.1 %copy-start = (f32[16,1,256]{2,1,0:T(1,128)S(1)}, f32[16,1,256]{2,1,0:T(1,128)}, u32[]{:S(2)}) copy-start(f32[16,1,256]{2,1,0:T(1,128)} %direction_ref.3) | copy-start | bytes 49156
  28.1 42.1 %copy-start.1 = (f32[1,2,128,128]{3,2,1,0:T(8,128)S(1)}, f32[1,2,128,128]{3,2,1,0:T(8,128)}, u32[]{:S(2)}) copy-start(f32[1,2,128,128]{3,2,1,0:T(8,128)} %precond_ref.1) | copy-start | bytes 393220
  28.1 42.1 %copy-start.2 = (f32[16,1,256]{2,1,0:T(1,128)S(1)}, f32[16,1,256]{2,1,0:T(1,128)}, u32[]{:S(2)}) copy-start(f32[16,1,256]{2,1,0:T(1,128)} %residual_ref.3) | copy-start | bytes 49156
  28.1 42.1 %copy-start.7 = (f32[1,256]{1,0:T(1,128)S(1)}, f32[1,256]{1,0:T(1,128)}, u32[]{:S(2)}) copy-start(f32[1,256]{1,0:T(1,128)} %kaula_ref.1) | copy-start | bytes 3076
  28.1 64.3 %copy-start.3 = (f32[16,1,256]{2,1,0:T(1,128)S(1)}, f32[16,1,256]{2,1,0:T(1,128)}, u32[]{:S(2)}) copy-start(f32[16,1,256]{2,1,0:T(1,128)} %solution_ref.1) | copy-start | bytes 49156
  28.1 13.8 %all-to-all-start.1 = ((bf16[8,16,384]{2,1,0:T(8,128)(2,1)}), bf16[8,16,384]{2,1,0:T(8,128)(2,1)S(1)}, u32[]{:S(2)}, u32[]{:S(2)}) async-start(bf16[8,16,384]{2,1,0:T(8,128)(2,1)} %shard_map.140), calls=%async_computation.1 | async-start | bytes 196608 | tf_op jit(solution)/shard_map/all_to_all | solution.py:427
  42.8 13.3 %all-to-all-start.2 = ((f32[32,3,128]{2,1,0:T(4,128)}), f32[32,3,128]{2,1,0:T(4,128)S(1)}, u32[]{:S(2)}, u32[]{:S(2)}) async-start(f32[32,3,128]{2,1,0:T(4,128)} %get-tuple-element.16), calls=%async_computation.2 | async-start | bytes 131072 | tf_op jit(solution)/shard_map/all_to_all | solution.py:427

commit v7 on v6

--- a/solution.py
+++ b/solution.py
@@ -11,6 +11,7 @@
 TM_ORDER = TM + ORDER
 VMEM_LIMIT = 50 * 1024 * 1024
 SMALL_LIMIT = 8 * 1024 * 1024
+EARLY = 3584
 
 precise = lax.Precision.HIGHEST
 LEVELS = 12
@@ -331,25 +332,35 @@
     ]
 
 
-def observe_kernel(got_ref, design_ref, out_ref, held_ref, sems):
-    copies = chunk_copies(design_ref, held_ref, sems)
+def observe_kernel(got_ref, design_ref, early_ref, out_ref, held_ref, sems):
+    count, _, _, width = held_ref.shape
+    start = early_ref.shape[2]
+    copies = [
+        pltpu.make_async_copy(
+            design_ref.at[:, :, pl.ds(start + width * k, width)], held_ref.at[k], sems.at[k]
+        )
+        for k in range(count)
+    ]
     for copy in copies:
         copy.start()
-    count, _, _, width = held_ref.shape
-    peers = width // 256
-    total = jnp.zeros((16, 384), jnp.float32)
-    for k in range(count):
+
+    def product(first, block):
         pieces = []
-        for p in range(peers * k, peers * k + peers):
+        for p in range(first, first + block.shape[1] // 256):
             pieces += [got_ref[p, 0:16, :], got_ref[p, 16:32, :]]
-        packed = jnp.concatenate(pieces, axis=1)
-        copies[k].wait()
-        total = total + lax.dot_general(
-            packed,
-            held_ref[k].reshape(384, width),
+        return lax.dot_general(
+            jnp.concatenate(pieces, axis=1),
+            block,
             (((1,), (1,)), ((), ())),
             preferred_element_type=jnp.float32,
         )
+
+    total = jnp.zeros((16, 384), jnp.float32)
+    for at in range(0, start, width):
+        total = total + product(at // 256, early_ref[:, :, at : at + width].reshape(384, width))
+    for k in range(count):
+        copies[k].wait()
+        total = total + product((start + width * k) // 256, held_ref[k].reshape(384, width))
     out_ref[...] = jnp.broadcast_to(total.astype(jnp.bfloat16)[None], out_ref.shape)
 
 
@@ -473,9 +484,12 @@
     (partial,) = run(
         observe_kernel,
         [((others, 16, 384), bf16)],
-        [got, design],
+        [got, design, lax.slice_in_dim(design, 0, EARLY, axis=2)],
         anywhere=(1,),
-        scratch=held(16),
+        scratch=[
+            pltpu.VMEM(((design.shape[2] - EARLY) // 512, 3, 128, 512), bf16),
+            pltpu.SemaphoreType.DMA(((design.shape[2] - EARLY) // 512,)),
+        ],
         limit=VMEM_LIMIT,
     )
     parts = exchange(partial, ORDER)

time: 93.8 us -> 93.4 us (level)
  blocking collectives: 57 us -> 35.1 us
  starting transfers between devices: 13.2 us -> 25.1 us
  waiting for transfers between devices: 8.04 us -> 16.1 us
  local copies, waits for them, and re-layouts: 0.05 us -> 2.02 us
    all_to_all x3 -> x2, blocking collectives: 57 us -> 35.1 us  [exchange(): return lax.all_to_all(value, axes, split_axis=0, concat_axis=0, tiled=True)]
    all_to_all x2 -> x3, starting transfers between devices: 13.2 us -> 25.1 us  [exchange(): return lax.all_to_all(value, axes, split_axis=0, concat_axis=0, tiled=True)]
    all_to_all x2 -> x3, waiting for transfers between devices: 8.04 us -> 16.1 us  [exchange(): return lax.all_to_all(value, axes, split_axis=0, concat_axis=0, tiled=True)]
    slice x0 -> x1, local copies, waits for them, and re-layouts: none -> 1.96 us  [on_device(): lax.slice_in_dim(design, 0, EARLY, axis=2)]
  transfers between devices with their start and end apart: 2 -> 3, of which waited for: 2 -> 3; matrix products, arithmetic and copies ran while one was open for 0% -> 2% of each run, Pallas kernels for 6% -> 6%
where the time goes in v7:
time: 93.4 us; the launch traced here: 92.9 us
  blocking collectives  35.1 us (38%)
  starting transfers between devices  25.1 us (27%)
  waiting for transfers between devices  16.1 us (17%)
  Pallas kernels  13.7 us (15%)
  local copies, waits for them, and re-layouts  2.02 us (2%)
    all_to_all x2, blocking collectives, exchange(): return lax.all_to_all(value, axes, split_axis=0, concat_axis=0, tiled=True)  35.1 us
    all_to_all x3, starting transfers between devices, exchange(): return lax.all_to_all(value, axes, split_axis=0, concat_axis=0, tiled=True)  25.1 us
    all_to_all x3, waiting for transfers between devices, exchange(): return lax.all_to_all(value, axes, split_axis=0, concat_axis=0, tiled=True)  16.1 us
    pallas_call x8, Pallas kernels, run(): pl.pallas_call(kernel, out_shape=shapes, in_specs=[pl.BlockSpec(memory_sp...  13.7 us
    slice x1, local copies, waits for them, and re-layouts, on_device(): lax.slice_in_dim(design, 0, EARLY, axis=2)  1.96 us
  transfers between devices with their start and end apart: 3, of which 3 were waited for; matrix products, arithmetic and copies ran while one was open for 2% of the time, Pallas kernels for 6%

profile of v7, /device:TPU:1, one launch (start us, length us, event | category | flops | bytes accessed | tf_op | source)
XLA Modules:
  0.0 92.9 jit_solution(2579316228577267737)
XLA Ops:
  0.6 1.5 %shard_map.139 = bf16[32,40,128]{2,1,0:T(8,128)(2,1)} custom-call(f32[16,1,256]{2,1,0:T(1,128)} %direction_ref.3, s32[1,128]{1,0:T(1,128)} %bitcast.5), custom_call_target="tpu_custom_call" | custom-call | flops 100000 | bytes 1000000 | tf_op jit(solution)/shard_map/pallas_call | solution.py:425
  2.2 12.0 %all-to-all-start = ((bf16[32,40,128]{2,1,0:T(8,128)(2,1)}), bf16[32,40,128]{2,1,0:T(8,128)(2,1)S(1)}, u32[]{:S(2)}, u32[]{:S(2)}) async-start(bf16[32,40,128]{2,1,0:T(8,128)(2,1)} %shard_map.139), calls=%async_computation | async-start | bytes 655360 | tf_op jit(solution)/shard_map/all_to_all | solution.py:438
  14.2 2.0 %slice.3.early_ref = bf16[3,128,3584]{2,1,0:T(8,128)(2,1)S(1)} slice(bf16[3,128,8192]{2,1,0:T(8,128)(2,1)} %design_ref.3), slice={[0:3], [0:128], [0:3584]} | slice | bytes 5505024 | tf_op jit(solution)/shard_map/slice | solution.py:487
  16.2 0.0 copy-start.4
  16.2 0.0 copy-start.5
  16.2 0.0 copy-start.8
  16.2 0.0 copy-start.9
  16.2 0.0 copy-start.6
  16.2 8.2 %all-to-all-done.got_ref = bf16[32,40,128]{2,1,0:T(8,128)(2,1)S(1)} async-done(((bf16[32,40,128]{2,1,0:T(8,128)(2,1)}), bf16[32,40,128]{2,1,0:T(8,128)(2,1)S(1)}, u32[]{:S(2)}, u32[]{:S(2)}) %all-to-all-start) | async-done | bytes 327712 | tf_op jit(solution)/shard_map/all_to_all | solution.py:438
  24.4 3.2 %shard_map.140 = bf16[8,16,384]{2,1,0:T(8,128)(2,1)} custom-call(bf16[32,40,128]{2,1,0:T(8,128)(2,1)S(1)} %all-to-all-done.got_ref, bf16[3,128,8192]{2,1,0:T(8,128)(2,1)} %design_ref.3, bf16[3,128,3584]{2,1,0:T(8,128)(2,1)S(1)} %slice.3.early_ref), custom_call_target="tpu_custom_call" | custom-call | flops 100000 | bytes 1000000 | tf_op jit(solution)/shard_map/pallas_call | solution.py:425
  27.6 8.6 %all-to-all-start.1 = ((bf16[8,16,384]{2,1,0:T(8,128)(2,1)}), bf16[8,16,384]{2,1,0:T(8,128)(2,1)S(1)}, u32[]{:S(2)}, u32[]{:S(2)}) async-start(bf16[8,16,384]{2,1,0:T(8,128)(2,1)} %shard_map.140), calls=%async_computation.1 | async-start | bytes 196608 | tf_op jit(solution)/shard_map/all_to_all | solution.py:438
  36.3 0.0 copy-done.4
  36.3 0.0 copy-done.5
  36.3 0.0 copy-done.8
  36.3 0.0 copy-done.9
  36.3 2.1 %shard_map.141 = (f32[3,8,128]{2,1,0:T(8,128)S(1)}, f32[3,128,128]{2,1,0:T(8,128)S(1)}, f32[3,8,256]{2,1,0:T(8,128)S(1)}, f32[3,8,128]{2,1,0:T(8,128)S(1)}) custom-call(s32[1,1]{1,0:T(1,128)} %bitcast.2.place_ref, s32[3]{0:T(128)S(1)} %copy-done.8, s32[3]{0:T(128)S(1)} %copy-done.9, f32[3,4]{1,0:T(4,128)S(1)} %copy-done.4, f32[3,4]{1,0:T(4,128)S(1)} %copy-done.5, ...), custom_call_target="tpu_custom_call" | custom-call | flops 10000000 | bytes 1000000 | tf_op jit(solution)/shard_map/pallas_call | solution.py:425
  38.4 2.8 %all-to-all-done.1.parts_ref = bf16[8,16,384]{2,1,0:T(8,128)(2,1)S(1)} async-done(((bf16[8,16,384]{2,1,0:T(8,128)(2,1)}), bf16[8,16,384]{2,1,0:T(8,128)(2,1)S(1)}, u32[]{:S(2)}, u32[]{:S(2)}) %all-to-all-start.1) | async-done | bytes 98336 | tf_op jit(solution)/shard_map/all_to_all | solution.py:438
  41.2 0.0 copy-done.6
  41.3 0.9 shard_map.142
  42.1 4.4 %all-to-all-start.2 = ((f32[32,3,128]{2,1,0:T(4,128)}), f32[32,3,128]{2,1,0:T(4,128)S(1)}, u32[]{:S(2)}, u32[]{:S(2)}) async-start(f32[32,3,128]{2,1,0:T(4,128)} %get-tuple-element.16), calls=%async_computation.2 | async-start | bytes 131072 | tf_op jit(solution)/shard_map/all_to_all | solution.py:438
  46.5 0.0 copy-start
  46.6 0.0 copy-start.1
  46.6 0.0 copy-start.2
  46.6 0.0 copy-start.7
  46.6 3.6 %shard_map.143 = (f32[16,8192]{1,0:T(8,128)S(1)}, bf16[72,8192]{1,0:T(8,128)(2,1)S(1)}) custom-call(f32[48,128]{1,0:T(8,128)S(1)} %get-tuple-element.18.masked_ref, f32[3,128,128]{2,1,0:T(8,128)S(1)} %get-tuple-element.19.near_ref, f32[3,8,128]{2,1,0:T(8,128)S(1)} %get-tuple-element.20.edge_ref, s32[1,128]{1,0:T(1,128)S(1)} %bitcast.4, ...), custom_call_target="tpu_custom_call" | custom-call | flops 10000000 | bytes 1000000 | tf_op jit(solution)/shard_map/pallas_call | solution.py:425
  50.2 0.0 copy-start.3
  50.2 5.2 %all-to-all-done.2.states_ref = f32[32,3,128]{2,1,0:T(4,128)S(1)} async-done(((f32[32,3,128]{2,1,0:T(4,128)}), f32[32,3,128]{2,1,0:T(4,128)S(1)}, u32[]{:S(2)}, u32[]{:S(2)}) %all-to-all-start.2) | async-done | bytes 49184 | tf_op jit(solution)/shard_map/all_to_all | solution.py:438
  55.4 0.7 shard_map.144
  56.1 13.5 %all_to_all.25.arrived_ref = bf16[32,16,256]{2,1,0:T(8,128)(2,1)S(1)} all-to-all(bf16[32,16,256]{2,1,0:T(8,128)(2,1)S(1)} %shard_map.144), channel_id=1, replica_groups=mesh['tm_0'=4,'tm_1'=8,'order_0'=4,'order_1'=2] {'tm_0','tm_1'}, dimensions={0} | all-to-all | bytes 524288 | tf_op jit(solution)/shard_map/all_to_all | solution.py:438
  69.7 0.6 shard_map.145
  70.3 21.6 %all_to_all.26.sums_ref = f32[256,1,128]{2,1,0:T(1,128)S(1)} all-to-all(f32[256,1,128]{2,1,0:T(1,128)S(1)} %get-tuple-element.23), channel_id=1, replica_groups=mesh['tm_0'=4,'tm_1'=8,'order_0'=4,'order_1'=2] {'tm_0','tm_1','order_0'..., dimensions={0} | all-to-all | bytes 262144 | tf_op jit(solution)/shard_map/all_to_all | solution.py:438
  91.9 1.0 %shard_map.146 = (f32[16,1,256]{2,1,0:T(1,128)}, f32[16,1,256]{2,1,0:T(1,128)}, f32[16,1,256]{2,1,0:T(1,128)}) custom-call(f32[256,1,128]{2,1,0:T(1,128)S(1)} %all_to_all.26.sums_ref, f32[16,256]{1,0:T(8,128)S(1)} %get-tuple-element.24.image_ref, f32[16,256]{1,0:T(8,128)S(1)} %get-tuple-element.25.applied_ref, f32[16,256]{1,0:T(8,128)S(1)} %get-tuple-element.26.both_ref, ...), custom_call_target="tpu_custom_call" | custom-call | flops 100000 | bytes 1000000 | tf_op jit(solution)/shard_map/pallas_call | solution.py:425
  (5 shorter events, 0.0 us)
Async XLA Ops:
  2.2 22.2 %all-to-all-start = ((bf16[32,40,128]{2,1,0:T(8,128)(2,1)}), bf16[32,40,128]{2,1,0:T(8,128)(2,1)S(1)}, u32[]{:S(2)}, u32[]{:S(2)}) async-start(bf16[32,40,128]{2,1,0:T(8,128)(2,1)} %shard_map.139), calls=%async_computation | async-start | bytes 655360 | tf_op jit(solution)/shard_map/all_to_all | solution.py:438
  16.2 20.1 %copy-start.4 = (f32[3,4]{1,0:T(4,128)S(1)}, f32[3,4]{1,0:T(4,128)}, u32[]{:S(2)}) copy-start(f32[3,4]{1,0:T(4,128)} %arr_ref.1) | copy-start | bytes 148
  16.2 20.1 %copy-start.5 = (f32[3,4]{1,0:T(4,128)S(1)}, f32[3,4]{1,0:T(4,128)}, u32[]{:S(2)}) copy-start(f32[3,4]{1,0:T(4,128)} %mar_ref.1) | copy-start | bytes 148
  16.2 20.1 %copy-start.8 = (s32[3]{0:T(128)S(1)}, s32[3]{0:T(128)}, u32[]{:S(2)}) copy-start(s32[3]{0:T(128)} %aro_ref.1) | copy-start | bytes 40
  16.2 20.1 %copy-start.9 = (s32[3]{0:T(128)S(1)}, s32[3]{0:T(128)}, u32[]{:S(2)}) copy-start(s32[3]{0:T(128)} %mao_ref.1) | copy-start | bytes 40
  16.2 25.0 %copy-start.6 = (s32[128]{0:T(128)S(1)}, s32[128]{0:T(128)}, u32[]{:S(2)}) copy-start(s32[128]{0:T(128)} %param.13) | copy-start | bytes 1540
  27.6 13.6 %all-to-all-start.1 = ((bf16[8,16,384]{2,1,0:T(8,128)(2,1)}), bf16[8,16,384]{2,1,0:T(8,128)(2,1)S(1)}, u32[]{:S(2)}, u32[]{:S(2)}) async-start(bf16[8,16,384]{2,1,0:T(8,128)(2,1)} %shard_map.140), calls=%async_computation.1 | async-start | bytes 196608 | tf_op jit(solution)/shard_map/all_to_all | solution.py:438
  42.1 13.3 %all-to-all-start.2 = ((f32[32,3,128]{2,1,0:T(4,128)}), f32[32,3,128]{2,1,0:T(4,128)S(1)}, u32[]{:S(2)}, u32[]{:S(2)}) async-start(f32[32,3,128]{2,1,0:T(4,128)} %get-tuple-element.16), calls=%async_computation.2 | async-start | bytes 131072 | tf_op jit(solution)/shard_map/all_to_all | solution.py:438
  46.5 23.1 %copy-start = (f32[16,1,256]{2,1,0:T(1,128)S(1)}, f32[16,1,256]{2,1,0:T(1,128)}, u32[]{:S(2)}) copy-start(f32[16,1,256]{2,1,0:T(1,128)} %direction_ref.3) | copy-start | bytes 49156
  46.6 23.1 %copy-start.1 = (f32[1,2,128,128]{3,2,1,0:T(8,128)S(1)}, f32[1,2,128,128]{3,2,1,0:T(8,128)}, u32[]{:S(2)}) copy-start(f32[1,2,128,128]{3,2,1,0:T(8,128)} %precond_ref.1) | copy-start | bytes 393220
  46.6 23.1 %copy-start.2 = (f32[16,1,256]{2,1,0:T(1,128)S(1)}, f32[16,1,256]{2,1,0:T(1,128)}, u32[]{:S(2)}) copy-start(f32[16,1,256]{2,1,0:T(1,128)} %residual_ref.3) | copy-start | bytes 49156
  46.6 23.1 %copy-start.7 = (f32[1,256]{1,0:T(1,128)S(1)}, f32[1,256]{1,0:T(1,128)}, u32[]{:S(2)}) copy-start(f32[1,256]{1,0:T(1,128)} %kaula_ref.1) | copy-start | bytes 3076
  50.2 41.7 %copy-start.3 = (f32[16,1,256]{2,1,0:T(1,128)S(1)}, f32[16,1,256]{2,1,0:T(1,128)}, u32[]{:S(2)}) copy-start(f32[16,1,256]{2,1,0:T(1,128)} %solution_ref.1) | copy-start | bytes 49156

commit v8 on v7

--- a/solution.py
+++ b/solution.py
@@ -364,8 +364,19 @@
     out_ref[...] = jnp.broadcast_to(total.astype(jnp.bfloat16)[None], out_ref.shape)
 
 
+def precondition(vector, precond_ref):
+    return jnp.concatenate(
+        [dot(vector[:, 128 * k : 128 * k + 128], precond_ref[0, k], ((1,), (1,))) for k in range(2)],
+        axis=1,
+    )
+
+
+def applied_kernel(precond_ref, residual_ref, applied_ref):
+    applied_ref[...] = precondition(residual_ref[:, 0, :], precond_ref)
+
+
 def image_kernel(
-    arrived_ref, kaula_ref, precond_ref, residual_ref, direction_ref, message_ref, image_ref, applied_ref, both_ref
+    arrived_ref, kaula_ref, precond_ref, residual_ref, direction_ref, applied_ref, message_ref, image_ref, both_ref
 ):
     total = arrived_ref[0].astype(jnp.float32)
     for p in range(1, arrived_ref.shape[0]):
@@ -373,12 +384,8 @@
     direction = direction_ref[:, 0, :]
     residual = residual_ref[:, 0, :]
     image = total + kaula_ref[...] * direction
-    stack = jnp.concatenate([residual, image], axis=0)
-    mixed = jnp.concatenate(
-        [dot(stack[:, 128 * k : 128 * k + 128], precond_ref[0, k], ((1,), (1,))) for k in range(2)],
-        axis=1,
-    )
-    applied, image_applied = mixed[0:16], mixed[16:32]
+    applied = applied_ref[...]
+    image_applied = precondition(image, precond_ref)
     products = jnp.concatenate(
         [
             residual * applied,
@@ -392,7 +399,6 @@
     sums = dot(jnp.ones((8, 256), jnp.float32), products, ((1,), (1,)))
     message_ref[...] = jnp.broadcast_to(sums[None, 0:1, :], message_ref.shape)
     image_ref[...] = image
-    applied_ref[...] = applied
     both_ref[...] = image_applied
 
 
@@ -528,10 +534,11 @@
         limit=16 * 1024 * 1024,
     )
     arrived = exchange(gradient, TM)
-    sums, image, applied, image_applied = run(
+    (applied,) = run(applied_kernel, [((16, 256), f32)], [precond, residual], flops=10000000)
+    sums, image, image_applied = run(
         image_kernel,
-        [((everyone, 1, 128), f32)] + [((16, 256), f32)] * 3,
-        [arrived, kaula, precond, residual, direction],
+        [((everyone, 1, 128), f32)] + [((16, 256), f32)] * 2,
+        [arrived, kaula, precond, residual, direction, applied],
     )
     gathered = exchange(sums, TM_ORDER)
     return tuple(

time: 93.4 us -> 94.3 us (level)
  blocking collectives: 35.1 us -> 21.6 us
  waiting for transfers between devices: 16.1 us -> 25.5 us
  starting transfers between devices: 25.1 us -> 29.2 us
  Pallas kernels: 13.7 us -> 14.7 us
    all_to_all x2 -> x1, blocking collectives: 35.1 us -> 21.6 us  [exchange(): return lax.all_to_all(value, axes, split_axis=0, concat_axis=0, tiled=True)]
    all_to_all x3 -> x4, waiting for transfers between devices: 16.1 us -> 25.5 us  [exchange(): return lax.all_to_all(value, axes, split_axis=0, concat_axis=0, tiled=True)]
    all_to_all x3 -> x4, starting transfers between devices: 25.1 us -> 29.2 us  [exchange(): return lax.all_to_all(value, axes, split_axis=0, concat_axis=0, tiled=True)]
    pallas_call x8 -> x9, Pallas kernels: 13.7 us -> 14.7 us  [run(): pl.pallas_call(kernel, out_shape=shapes, in_specs=[pl.BlockSpec(memory_sp...]
  transfers between devices with their start and end apart: 3 -> 4, of which waited for: 3 -> 4; matrix products, arithmetic and copies ran while one was open for 2% -> 2% of each run, Pallas kernels for 6% -> 6%
where the time goes in v8:
time: 94.3 us; the launch traced here: 93.8 us
  starting transfers between devices  29.2 us (31%)
  waiting for transfers between devices  25.5 us (27%)
  blocking collectives  21.6 us (23%)
  Pallas kernels  14.7 us (16%)
  local copies, waits for them, and re-layouts  2.02 us (2%)
    all_to_all x4, starting transfers between devices, exchange(): return lax.all_to_all(value, axes, split_axis=0, concat_axis=0, tiled=True)  29.2 us
    all_to_all x4, waiting for transfers between devices, exchange(): return lax.all_to_all(value, axes, split_axis=0, concat_axis=0, tiled=True)  25.5 us
    all_to_all x1, blocking collectives, exchange(): return lax.all_to_all(value, axes, split_axis=0, concat_axis=0, tiled=True)  21.6 us
    pallas_call x9, Pallas kernels, run(): pl.pallas_call(kernel, out_shape=shapes, in_specs=[pl.BlockSpec(memory_sp...  14.7 us
    slice x1, local copies, waits for them, and re-layouts, on_device(): lax.slice_in_dim(design, 0, EARLY, axis=2)  1.96 us
  transfers between devices with their start and end apart: 4, of which 4 were waited for; matrix products, arithmetic and copies ran while one was open for 2% of the time, Pallas kernels for 6%

profile of v8, /device:TPU:1, one launch (start us, length us, event | category | flops | bytes accessed | tf_op | source)
XLA Modules:
  0.0 93.8 jit_solution(13663502687181984259)
XLA Ops:
  0.6 1.5 %shard_map.139 = bf16[32,40,128]{2,1,0:T(8,128)(2,1)} custom-call(f32[16,1,256]{2,1,0:T(1,128)} %direction_ref.3, s32[1,128]{1,0:T(1,128)} %bitcast.5), custom_call_target="tpu_custom_call" | custom-call | flops 100000 | bytes 1000000 | tf_op jit(solution)/shard_map/pallas_call | solution.py:431
  2.2 12.0 %all-to-all-start = ((bf16[32,40,128]{2,1,0:T(8,128)(2,1)}), bf16[32,40,128]{2,1,0:T(8,128)(2,1)S(1)}, u32[]{:S(2)}, u32[]{:S(2)}) async-start(bf16[32,40,128]{2,1,0:T(8,128)(2,1)} %shard_map.139), calls=%async_computation | async-start | bytes 655360 | tf_op jit(solution)/shard_map/all_to_all | solution.py:444
  14.2 2.0 %slice.3.early_ref = bf16[3,128,3584]{2,1,0:T(8,128)(2,1)S(1)} slice(bf16[3,128,8192]{2,1,0:T(8,128)(2,1)} %design_ref.3), slice={[0:3], [0:128], [0:3584]} | slice | bytes 5505024 | tf_op jit(solution)/shard_map/slice | solution.py:493
  16.2 0.0 copy-start.4
  16.2 0.0 copy-start.5
  16.2 0.0 copy-start.8
  16.2 0.0 copy-start.9
  16.2 0.0 copy-start.6
  16.2 8.2 %all-to-all-done.got_ref = bf16[32,40,128]{2,1,0:T(8,128)(2,1)S(1)} async-done(((bf16[32,40,128]{2,1,0:T(8,128)(2,1)}), bf16[32,40,128]{2,1,0:T(8,128)(2,1)S(1)}, u32[]{:S(2)}, u32[]{:S(2)}) %all-to-all-start) | async-done | bytes 327712 | tf_op jit(solution)/shard_map/all_to_all | solution.py:444
  24.4 3.2 %shard_map.140 = bf16[8,16,384]{2,1,0:T(8,128)(2,1)} custom-call(bf16[32,40,128]{2,1,0:T(8,128)(2,1)S(1)} %all-to-all-done.got_ref, bf16[3,128,8192]{2,1,0:T(8,128)(2,1)} %design_ref.3, bf16[3,128,3584]{2,1,0:T(8,128)(2,1)S(1)} %slice.3.early_ref), custom_call_target="tpu_custom_call" | custom-call | flops 100000 | bytes 1000000 | tf_op jit(solution)/shard_map/pallas_call | solution.py:431
  27.6 8.6 %all-to-all-start.1 = ((bf16[8,16,384]{2,1,0:T(8,128)(2,1)}), bf16[8,16,384]{2,1,0:T(8,128)(2,1)S(1)}, u32[]{:S(2)}, u32[]{:S(2)}) async-start(bf16[8,16,384]{2,1,0:T(8,128)(2,1)} %shard_map.140), calls=%async_computation.1 | async-start | bytes 196608 | tf_op jit(solution)/shard_map/all_to_all | solution.py:444
  36.3 0.0 copy-done.8
  36.3 0.0 copy-done.9
  36.3 2.1 %shard_map.141 = (f32[3,8,128]{2,1,0:T(8,128)S(1)}, f32[3,128,128]{2,1,0:T(8,128)S(1)}, f32[3,8,256]{2,1,0:T(8,128)S(1)}, f32[3,8,128]{2,1,0:T(8,128)S(1)}) custom-call(s32[1,1]{1,0:T(1,128)} %bitcast.2.place_ref, s32[3]{0:T(128)S(1)} %copy-done.8, s32[3]{0:T(128)S(1)} %copy-done.9, f32[3,4]{1,0:T(4,128)S(1)} %copy-done.4, f32[3,4]{1,0:T(4,128)S(1)} %copy-done.5, ...), custom_call_target="tpu_custom_call" | custom-call | flops 10000000 | bytes 1000000 | tf_op jit(solution)/shard_map/pallas_call | solution.py:431
  38.5 2.8 %all-to-all-done.1.parts_ref = bf16[8,16,384]{2,1,0:T(8,128)(2,1)S(1)} async-done(((bf16[8,16,384]{2,1,0:T(8,128)(2,1)}), bf16[8,16,384]{2,1,0:T(8,128)(2,1)S(1)}, u32[]{:S(2)}, u32[]{:S(2)}) %all-to-all-start.1) | async-done | bytes 98336 | tf_op jit(solution)/shard_map/all_to_all | solution.py:444
  41.3 0.9 shard_map.142
  42.1 4.4 %all-to-all-start.2 = ((f32[32,3,128]{2,1,0:T(4,128)}), f32[32,3,128]{2,1,0:T(4,128)S(1)}, u32[]{:S(2)}, u32[]{:S(2)}) async-start(f32[32,3,128]{2,1,0:T(4,128)} %get-tuple-element.15), calls=%async_computation.2 | async-start | bytes 131072 | tf_op jit(solution)/shard_map/all_to_all | solution.py:444
  46.6 0.0 copy-start
  46.6 0.0 copy-start.1
  46.6 0.0 copy-start.7
  46.6 3.6 %shard_map.143 = (f32[16,8192]{1,0:T(8,128)S(1)}, bf16[72,8192]{1,0:T(8,128)(2,1)S(1)}) custom-call(f32[48,128]{1,0:T(8,128)S(1)} %get-tuple-element.17.masked_ref, f32[3,128,128]{2,1,0:T(8,128)S(1)} %get-tuple-element.18.near_ref, f32[3,8,128]{2,1,0:T(8,128)S(1)} %get-tuple-element.19.edge_ref, s32[1,128]{1,0:T(1,128)S(1)} %bitcast.4, ...), custom_call_target="tpu_custom_call" | custom-call | flops 10000000 | bytes 1000000 | tf_op jit(solution)/shard_map/pallas_call | solution.py:431
  50.2 0.0 copy-start.2
  50.2 0.0 copy-start.3
  50.2 5.2 %all-to-all-done.2.states_ref = f32[32,3,128]{2,1,0:T(4,128)S(1)} async-done(((f32[32,3,128]{2,1,0:T(4,128)}), f32[32,3,128]{2,1,0:T(4,128)S(1)}, u32[]{:S(2)}, u32[]{:S(2)}) %all-to-all-start.2) | async-done | bytes 49184 | tf_op jit(solution)/shard_map/all_to_all | solution.py:444
  55.4 1.4 %shard_map.144 = bf16[32,16,256]{2,1,0:T(8,128)(2,1)} custom-call(f32[32,3,128]{2,1,0:T(4,128)S(1)} %all-to-all-done.2.states_ref, f32[3,8,256]{2,1,0:T(8,128)S(1)} %get-tuple-element.16.link_ref, f32[16,8192]{1,0:T(8,128)S(1)} %get-tuple-element.20.here_ref, bf16[72,8192]{1,0:T(8,128)(2,1)S(1)} %get-tuple-element.21.basis_ref), custom_call_target="tpu_custom_call" | custom-call | flops 100000 | bytes 1000000 | tf_op jit(solution)/shard_map/pallas_call | solution.py:431
  56.8 4.1 %all-to-all-start.3 = ((bf16[32,16,256]{2,1,0:T(8,128)(2,1)}), bf16[32,16,256]{2,1,0:T(8,128)(2,1)S(1)}, u32[]{:S(2)}, u32[]{:S(2)}) async-start(bf16[32,16,256]{2,1,0:T(8,128)(2,1)} %shard_map.144), calls=%async_computation.3 | async-start | bytes 524288 | tf_op jit(solution)/shard_map/all_to_all | solution.py:444
  60.9 0.3 shard_map.145.applied_ref
  61.2 9.3 %all-to-all-done.3.arrived_ref = bf16[32,16,256]{2,1,0:T(8,128)(2,1)S(1)} async-done(((bf16[32,16,256]{2,1,0:T(8,128)(2,1)}), bf16[32,16,256]{2,1,0:T(8,128)(2,1)S(1)}, u32[]{:S(2)}, u32[]{:S(2)}) %all-to-all-start.3) | async-done | bytes 262176 | tf_op jit(solution)/shard_map/all_to_all | solution.py:444
  70.6 0.0 copy-done.2
  70.6 0.6 shard_map.146
  71.2 21.6 %all_to_all.25.sums_ref = f32[256,1,128]{2,1,0:T(1,128)S(1)} all-to-all(f32[256,1,128]{2,1,0:T(1,128)S(1)} %get-tuple-element.22), channel_id=1, replica_groups=mesh['tm_0'=4,'tm_1'=8,'order_0'=4,'order_1'=2] {'tm_0','tm_1','order_0'..., dimensions={0} | all-to-all | bytes 262144 | tf_op jit(solution)/shard_map/all_to_all | solution.py:444
  92.8 1.0 %shard_map.147 = (f32[16,1,256]{2,1,0:T(1,128)}, f32[16,1,256]{2,1,0:T(1,128)}, f32[16,1,256]{2,1,0:T(1,128)}) custom-call(f32[256,1,128]{2,1,0:T(1,128)S(1)} %all_to_all.25.sums_ref, f32[16,256]{1,0:T(8,128)S(1)} %get-tuple-element.23.image_ref, f32[16,256]{1,0:T(8,128)S(1)} %shard_map.145.applied_ref, f32[16,256]{1,0:T(8,128)S(1)} %get-tuple-element.24.both_ref, ...), custom_call_target="tpu_custom_call" | custom-call | flops 100000 | bytes 1000000 | tf_op jit(solution)/shard_map/pallas_call | solution.py:431
  (7 shorter events, 0.0 us)
Async XLA Ops:
  2.2 22.2 %all-to-all-start = ((bf16[32,40,128]{2,1,0:T(8,128)(2,1)}), bf16[32,40,128]{2,1,0:T(8,128)(2,1)S(1)}, u32[]{:S(2)}, u32[]{:S(2)}) async-start(bf16[32,40,128]{2,1,0:T(8,128)(2,1)} %shard_map.139), calls=%async_computation | async-start | bytes 655360 | tf_op jit(solution)/shard_map/all_to_all | solution.py:444
  16.2 20.1 %copy-start.4 = (f32[3,4]{1,0:T(4,128)S(1)}, f32[3,4]{1,0:T(4,128)}, u32[]{:S(2)}) copy-start(f32[3,4]{1,0:T(4,128)} %arr_ref.1) | copy-start | bytes 148
  16.2 20.1 %copy-start.5 = (f32[3,4]{1,0:T(4,128)S(1)}, f32[3,4]{1,0:T(4,128)}, u32[]{:S(2)}) copy-start(f32[3,4]{1,0:T(4,128)} %mar_ref.1) | copy-start | bytes 148
  16.2 20.1 %copy-start.8 = (s32[3]{0:T(128)S(1)}, s32[3]{0:T(128)}, u32[]{:S(2)}) copy-start(s32[3]{0:T(128)} %aro_ref.1) | copy-start | bytes 40
  16.2 20.1 %copy-start.9 = (s32[3]{0:T(128)S(1)}, s32[3]{0:T(128)}, u32[]{:S(2)}) copy-start(s32[3]{0:T(128)} %mao_ref.1) | copy-start | bytes 40
  16.2 25.0 %copy-start.6 = (s32[128]{0:T(128)S(1)}, s32[128]{0:T(128)}, u32[]{:S(2)}) copy-start(s32[128]{0:T(128)} %param.13) | copy-start | bytes 1540
  27.6 13.6 %all-to-all-start.1 = ((bf16[8,16,384]{2,1,0:T(8,128)(2,1)}), bf16[8,16,384]{2,1,0:T(8,128)(2,1)S(1)}, u32[]{:S(2)}, u32[]{:S(2)}) async-start(bf16[8,16,384]{2,1,0:T(8,128)(2,1)} %shard_map.140), calls=%async_computation.1 | async-start | bytes 196608 | tf_op jit(solution)/shard_map/all_to_all | solution.py:444
  42.1 13.3 %all-to-all-start.2 = ((f32[32,3,128]{2,1,0:T(4,128)}), f32[32,3,128]{2,1,0:T(4,128)S(1)}, u32[]{:S(2)}, u32[]{:S(2)}) async-start(f32[32,3,128]{2,1,0:T(4,128)} %get-tuple-element.15), calls=%async_computation.2 | async-start | bytes 131072 | tf_op jit(solution)/shard_map/all_to_all | solution.py:444
  46.6 14.3 %copy-start = (f32[1,2,128,128]{3,2,1,0:T(8,128)S(1)}, f32[1,2,128,128]{3,2,1,0:T(8,128)}, u32[]{:S(2)}) copy-start(f32[1,2,128,128]{3,2,1,0:T(8,128)} %precond_ref.3) | copy-start | bytes 393220
  46.6 14.3 %copy-start.1 = (f32[16,1,256]{2,1,0:T(1,128)S(1)}, f32[16,1,256]{2,1,0:T(1,128)}, u32[]{:S(2)}) copy-start(f32[16,1,256]{2,1,0:T(1,128)} %residual_ref.5) | copy-start | bytes 49156
  46.6 24.0 %copy-start.7 = (f32[1,256]{1,0:T(1,128)S(1)}, f32[1,256]{1,0:T(1,128)}, u32[]{:S(2)}) copy-start(f32[1,256]{1,0:T(1,128)} %kaula_ref.1) | copy-start | bytes 3076
  50.2 20.4 %copy-start.2 = (f32[16,1,256]{2,1,0:T(1,128)S(1)}, f32[16,1,256]{2,1,0:T(1,128)}, u32[]{:S(2)}) copy-start(f32[16,1,256]{2,1,0:T(1,128)} %direction_ref.3) | copy-start | bytes 49156
  50.2 42.6 %copy-start.3 = (f32[16,1,256]{2,1,0:T(1,128)S(1)}, f32[16,1,256]{2,1,0:T(1,128)}, u32[]{:S(2)}) copy-start(f32[16,1,256]{2,1,0:T(1,128)} %solution_ref.1) | copy-start | bytes 49156
  56.8 13.7 %all-to-all-start.3 = ((bf16[32,16,256]{2,1,0:T(8,128)(2,1)}), bf16[32,16,256]{2,1,0:T(8,128)(2,1)S(1)}, u32[]{:S(2)}, u32[]{:S(2)}) async-start(bf16[32,16,256]{2,1,0:T(8,128)(2,1)} %shard_map.144), calls=%async_computation.3 | async-start | bytes 524288 | tf_op jit(solution)/shard_map/all_to_all | solution.py:444

commit v9 on v7

--- a/solution.py
+++ b/solution.py
@@ -11,6 +11,7 @@
 TM_ORDER = TM + ORDER
 VMEM_LIMIT = 50 * 1024 * 1024
 SMALL_LIMIT = 8 * 1024 * 1024
+KEPT = 2048
 EARLY = 3584
 
 precise = lax.Precision.HIGHEST
@@ -249,9 +250,16 @@
 
 
 def spread_kernel(
-    masked_ref, near_ref, edge_ref, gaps_ref, design_ref, here_ref, basis_ref, held_ref, sems
-):
-    copies = chunk_copies(design_ref, held_ref, sems)
+    masked_ref, near_ref, edge_ref, gaps_ref, design_ref, kept_ref, here_ref, basis_ref, held_ref, sems
+):
+    count, _, _, width = held_ref.shape
+    start = kept_ref.shape[2]
+    copies = [
+        pltpu.make_async_copy(
+            design_ref.at[:, :, pl.ds(start + width * k, width)], held_ref.at[k], sems.at[k]
+        )
+        for k in range(count)
+    ]
     for copy in copies:
         copy.start()
     gaps = gaps_ref[...].astype(jnp.float32)
@@ -266,17 +274,19 @@
     rows = jnp.concatenate(
         [*split_in_two(jnp.concatenate(pieces, axis=1)), *highs, *lows], axis=0
     )
-    count, _, _, width = held_ref.shape
+
+    def spread(at, block):
+        found = jnp.dot(rows, block, preferred_element_type=jnp.float32)
+        here_ref[:, at : at + width] = found[0:16] + found[16:32]
+        high, low = split_in_two(found[32:56] + found[56:80])
+        basis_ref[0:24, at : at + width] = high
+        basis_ref[24:48, at : at + width] = low
+
+    for at in range(0, start, width):
+        spread(at, kept_ref[:, :, at : at + width].reshape(384, width))
     for k in range(count):
         copies[k].wait()
-        found = jnp.dot(
-            rows, held_ref[k].reshape(384, width), preferred_element_type=jnp.float32
-        )
-        here_ref[:, width * k : width * k + width] = found[0:16] + found[16:32]
-        high, low = split_in_two(found[32:56] + found[56:80])
-        basis_ref[0:24, width * k : width * k + width] = high
-        basis_ref[24:48, width * k : width * k + width] = low
-        basis_ref[48:72, width * k : width * k + width] = high
+        spread(start + width * k, held_ref[k].reshape(384, width))
 
 
 def gradient_kernel(states_ref, link_ref, here_ref, basis_ref, out_ref):
@@ -285,17 +295,17 @@
         states = states_ref[:, c, :]
         turned = [states] + [pltpu.roll(states, 128 - 16 * i, 1) for i in range(1, 8)]
         parts.append(dot(link_ref[c], jnp.concatenate(turned, axis=0), ((1,), (0,))))
-    found = jnp.concatenate(parts, axis=0)
+    lane = lax.broadcasted_iota(jnp.int32, (24, 128), 1)
+    found = jnp.where(lane < 16, jnp.concatenate(parts, axis=0), 0.0)
     high = found.astype(jnp.bfloat16).astype(jnp.float32)
-    tall = jnp.concatenate(
-        [high, high, found - high, jnp.zeros((56, 128), jnp.float32)], axis=0
-    )
-    left = tall.T[0:16, 0:72].astype(jnp.bfloat16)
+    low = pltpu.roll(found - high, 16, 1)
+    tall = jnp.concatenate([high + low, high, jnp.zeros((80, 128), jnp.float32)], axis=0)
+    left = tall.T[0:32, 0:48].astype(jnp.bfloat16)
     peers = out_ref.shape[0]
     for p in range(0, peers, 4):
         span = slice(256 * p, 256 * p + 1024)
         there = jnp.dot(left, basis_ref[:, span], preferred_element_type=jnp.float32)
-        whole = (here_ref[:, span] + there).astype(out_ref.dtype)
+        whole = (here_ref[:, span] + there[0:16] + there[16:32]).astype(out_ref.dtype)
         for q in range(4):
             out_ref[p + q] = whole[:, 256 * q : 256 * q + 256]
 
@@ -322,19 +332,10 @@
     out_ref[...] = jnp.broadcast_to(sheet[None], out_ref.shape)
 
 
-def chunk_copies(design_ref, held_ref, sems):
-    width = held_ref.shape[3]
-    return [
-        pltpu.make_async_copy(
-            design_ref.at[:, :, pl.ds(width * k, width)], held_ref.at[k], sems.at[k]
-        )
-        for k in range(held_ref.shape[0])
-    ]
-
-
-def observe_kernel(got_ref, design_ref, early_ref, out_ref, held_ref, sems):
+def observe_kernel(got_ref, design_ref, kept_ref, early_ref, out_ref, held_ref, sems):
     count, _, _, width = held_ref.shape
-    start = early_ref.shape[2]
+    middle = kept_ref.shape[2]
+    start = middle + early_ref.shape[2]
     copies = [
         pltpu.make_async_copy(
             design_ref.at[:, :, pl.ds(start + width * k, width)], held_ref.at[k], sems.at[k]
@@ -356,8 +357,11 @@
         )
 
     total = jnp.zeros((16, 384), jnp.float32)
-    for at in range(0, start, width):
-        total = total + product(at // 256, early_ref[:, :, at : at + width].reshape(384, width))
+    for at in range(0, middle, width):
+        total = total + product(at // 256, kept_ref[:, :, at : at + width].reshape(384, width))
+    for at in range(middle, start, width):
+        block = early_ref[:, :, at - middle : at - middle + width].reshape(384, width)
+        total = total + product(at // 256, block)
     for k in range(count):
         copies[k].wait()
         total = total + product((start + width * k) // 256, held_ref[k].reshape(384, width))
@@ -475,16 +479,34 @@
     )
     got = exchange(sheets, TM)
 
+    (sheets,) = run(
+        pack_kernel,
+        [((count, 40, 128), bf16)],
+        [
+            pltpu.with_memory_space_constraint(direction, pltpu.HBM),
+            pltpu.with_memory_space_constraint(segment_ids.reshape(1, 128), pltpu.HBM),
+        ],
+        anywhere=(0, 1),
+        scratch=[
+            pltpu.VMEM((16, 1, 256), f32),
+            pltpu.VMEM((1, 128), jnp.int32),
+            pltpu.SemaphoreType.DMA((2,)),
+        ],
+        limit=VMEM_LIMIT,
+    )
+    got = exchange(sheets, TM)
+
     def held(chunks):
         return [
             pltpu.VMEM((chunks, 3, 128, design.shape[2] // chunks), bf16),
             pltpu.SemaphoreType.DMA((chunks,)),
         ]
 
+    kept = lax.slice_in_dim(design, 0, KEPT, axis=2)
     (partial,) = run(
         observe_kernel,
         [((others, 16, 384), bf16)],
-        [got, design, lax.slice_in_dim(design, 0, EARLY, axis=2)],
+        [got, design, kept, lax.slice_in_dim(design, KEPT, EARLY, axis=2)],
         anywhere=(1,),
         scratch=[
             pltpu.VMEM(((design.shape[2] - EARLY) // 512, 3, 128, 512), bf16),
@@ -514,10 +536,13 @@
     states = exchange(message, TM)
     here, basis = run(
         spread_kernel,
-        [((16, design.shape[2]), f32), ((72, design.shape[2]), bf16)],
-        [masked, near, edge, gaps, design],
+        [((16, design.shape[2]), f32), ((48, design.shape[2]), bf16)],
+        [masked, near, edge, gaps, design, kept],
         anywhere=(4,),
-        scratch=held(8),
+        scratch=[
+            pltpu.VMEM(((design.shape[2] - KEPT) // 1024, 3, 128, 1024), bf16),
+            pltpu.SemaphoreType.DMA(((design.shape[2] - KEPT) // 1024,)),
+        ],
         flops=10000000,
         limit=VMEM_LIMIT,
     )

time: 93.4 us -> 93.3 us (level)
    slice x1 -> x2, local copies, waits for them, and re-layouts: 1.96 us -> 2.86 us  [the longest x1 1.51 us: on_device(): kept = lax.slice_in_dim(design, 0, KEPT, axis=2)]
  transfers between devices with their start and end apart: 3 -> 3, of which waited for: 3 -> 3; matrix products, arithmetic and copies ran while one was open for 2% -> 3% of each run, Pallas kernels for 6% -> 6%
where the time goes in v9:
time: 93.3 us; the launch traced here: 92.7 us
  blocking collectives  34.9 us (37%)
  starting transfers between devices  25.1 us (27%)
  waiting for transfers between devices  15.4 us (17%)
  Pallas kernels  13.6 us (15%)
  local copies, waits for them, and re-layouts  2.93 us (3%)
    all_to_all x2, blocking collectives, exchange(): return lax.all_to_all(value, axes, split_axis=0, concat_axis=0, tiled=True)  34.9 us
    all_to_all x3, starting transfers between devices, exchange(): return lax.all_to_all(value, axes, split_axis=0, concat_axis=0, tiled=True)  25.1 us
    all_to_all x3, waiting for transfers between devices, exchange(): return lax.all_to_all(value, axes, split_axis=0, concat_axis=0, tiled=True)  15.4 us
    pallas_call x8, Pallas kernels, run(): pl.pallas_call(kernel, out_shape=shapes, in_specs=[pl.BlockSpec(memory_sp...  13.6 us
  transfers between devices with their start and end apart: 3, of which 3 were waited for; matrix products, arithmetic and copies ran while one was open for 3% of the time, Pallas kernels for 6%

profile of v9, /device:TPU:1, one launch (start us, length us, event | category | flops | bytes accessed | tf_op | source)
XLA Modules:
  0.0 92.7 jit_solution(13090573985971650903)
XLA Ops:
  0.6 1.5 %shard_map.139 = bf16[32,40,128]{2,1,0:T(8,128)(2,1)} custom-call(f32[16,1,256]{2,1,0:T(1,128)} %direction_ref.3, s32[1,128]{1,0:T(1,128)} %bitcast.5), custom_call_target="tpu_custom_call" | custom-call | flops 100000 | bytes 1000000 | tf_op jit(solution)/shard_map/pallas_call | solution.py:429
  2.2 12.0 %all-to-all-start = ((bf16[32,40,128]{2,1,0:T(8,128)(2,1)}), bf16[32,40,128]{2,1,0:T(8,128)(2,1)S(1)}, u32[]{:S(2)}, u32[]{:S(2)}) async-start(bf16[32,40,128]{2,1,0:T(8,128)(2,1)} %shard_map.139), calls=%async_computation | async-start | bytes 655360 | tf_op jit(solution)/shard_map/all_to_all | solution.py:442
  14.2 1.5 %slice.6.kept_ref = bf16[3,128,2048]{2,1,0:T(8,128)(2,1)S(1)} slice(bf16[3,128,8192]{2,1,0:T(8,128)(2,1)} %design_ref.3), slice={[0:3], [0:128], [0:2048]} | slice | bytes 3145728 | tf_op jit(solution)/shard_map/slice | solution.py:505
  15.7 1.4 %slice.7.early_ref = bf16[3,128,1536]{2,1,0:T(8,128)(2,1)S(1)} slice(bf16[3,128,8192]{2,1,0:T(8,128)(2,1)} %design_ref.3), slice={[0:3], [0:128], [2048:3584]} | slice | bytes 2359296 | tf_op jit(solution)/shard_map/slice | solution.py:509
  17.1 0.0 copy-start.4
  17.1 0.0 copy-start.5
  17.1 0.0 copy-start.8
  17.1 0.0 copy-start.9
  17.1 0.0 copy-start.6
  17.1 7.2 %all-to-all-done.got_ref = bf16[32,40,128]{2,1,0:T(8,128)(2,1)S(1)} async-done(((bf16[32,40,128]{2,1,0:T(8,128)(2,1)}), bf16[32,40,128]{2,1,0:T(8,128)(2,1)S(1)}, u32[]{:S(2)}, u32[]{:S(2)}) %all-to-all-start) | async-done | bytes 327712 | tf_op jit(solution)/shard_map/all_to_all | solution.py:442
  24.4 3.2 %shard_map.140 = bf16[8,16,384]{2,1,0:T(8,128)(2,1)} custom-call(bf16[32,40,128]{2,1,0:T(8,128)(2,1)S(1)} %all-to-all-done.got_ref, bf16[3,128,8192]{2,1,0:T(8,128)(2,1)} %design_ref.3, bf16[3,128,2048]{2,1,0:T(8,128)(2,1)S(1)} %slice.6.kept_ref, bf16[3,128,1536]{2,1,0:T(8,128)(2,1)S(1)} %slice.7.early_ref), custom_call_target="tpu_custom_call" | custom-call | flops 100000 | bytes 1000000 | tf_op jit(solution)/shard_map/pallas_call | solution.py:429
  27.6 8.6 %all-to-all-start.1 = ((bf16[8,16,384]{2,1,0:T(8,128)(2,1)}), bf16[8,16,384]{2,1,0:T(8,128)(2,1)S(1)}, u32[]{:S(2)}, u32[]{:S(2)}) async-start(bf16[8,16,384]{2,1,0:T(8,128)(2,1)} %shard_map.140), calls=%async_computation.1 | async-start | bytes 196608 | tf_op jit(solution)/shard_map/all_to_all | solution.py:442
  36.2 0.0 copy-done.4
  36.2 0.0 copy-done.5
  36.3 2.1 %shard_map.141 = (f32[3,8,128]{2,1,0:T(8,128)S(1)}, f32[3,128,128]{2,1,0:T(8,128)S(1)}, f32[3,8,256]{2,1,0:T(8,128)S(1)}, f32[3,8,128]{2,1,0:T(8,128)S(1)}) custom-call(s32[1,1]{1,0:T(1,128)} %bitcast.2.place_ref, s32[3]{0:T(128)S(1)} %copy-done.8, s32[3]{0:T(128)S(1)} %copy-done.9, f32[3,4]{1,0:T(4,128)S(1)} %copy-done.4, f32[3,4]{1,0:T(4,128)S(1)} %copy-done.5, ...), custom_call_target="tpu_custom_call" | custom-call | flops 10000000 | bytes 1000000 | tf_op jit(solution)/shard_map/pallas_call | solution.py:429
  38.4 2.8 %all-to-all-done.1.parts_ref = bf16[8,16,384]{2,1,0:T(8,128)(2,1)S(1)} async-done(((bf16[8,16,384]{2,1,0:T(8,128)(2,1)}), bf16[8,16,384]{2,1,0:T(8,128)(2,1)S(1)}, u32[]{:S(2)}, u32[]{:S(2)}) %all-to-all-start.1) | async-done | bytes 98336 | tf_op jit(solution)/shard_map/all_to_all | solution.py:442
  41.2 0.9 shard_map.142
  42.1 4.4 %all-to-all-start.2 = ((f32[32,3,128]{2,1,0:T(4,128)}), f32[32,3,128]{2,1,0:T(4,128)S(1)}, u32[]{:S(2)}, u32[]{:S(2)}) async-start(f32[32,3,128]{2,1,0:T(4,128)} %get-tuple-element.16), calls=%async_computation.2 | async-start | bytes 131072 | tf_op jit(solution)/shard_map/all_to_all | solution.py:442
  46.5 3.4 %shard_map.143 = (f32[16,8192]{1,0:T(8,128)S(1)}, bf16[48,8192]{1,0:T(8,128)(2,1)S(1)}) custom-call(f32[48,128]{1,0:T(8,128)S(1)} %get-tuple-element.18.masked_ref, f32[3,128,128]{2,1,0:T(8,128)S(1)} %get-tuple-element.19.near_ref, f32[3,8,128]{2,1,0:T(8,128)S(1)} %get-tuple-element.20.edge_ref, s32[1,128]{1,0:T(1,128)S(1)} %bitcast.4, ...), custom_call_target="tpu_custom_call" | custom-call | flops 10000000 | bytes 1000000 | tf_op jit(solution)/shard_map/pallas_call | solution.py:429
  50.0 0.0 copy-start
  50.0 0.0 copy-start.1
  50.0 0.0 copy-start.2
  50.0 0.0 copy-start.7
  50.0 0.0 copy-start.3
  50.0 5.4 %all-to-all-done.2.states_ref = f32[32,3,128]{2,1,0:T(4,128)S(1)} async-done(((f32[32,3,128]{2,1,0:T(4,128)}), f32[32,3,128]{2,1,0:T(4,128)S(1)}, u32[]{:S(2)}, u32[]{:S(2)}) %all-to-all-start.2) | async-done | bytes 49184 | tf_op jit(solution)/shard_map/all_to_all | solution.py:442
  55.4 0.8 shard_map.144
  56.2 13.3 %all_to_all.25.arrived_ref = bf16[32,16,256]{2,1,0:T(8,128)(2,1)S(1)} all-to-all(bf16[32,16,256]{2,1,0:T(8,128)(2,1)S(1)} %shard_map.144), channel_id=1, replica_groups=mesh['tm_0'=4,'tm_1'=8,'order_0'=4,'order_1'=2] {'tm_0','tm_1'}, dimensions={0} | all-to-all | bytes 524288 | tf_op jit(solution)/shard_map/all_to_all | solution.py:442
  69.5 0.0 copy-done.2
  69.5 0.0 copy-done.7
  69.5 0.6 shard_map.145
  70.2 21.6 %all_to_all.26.sums_ref = f32[256,1,128]{2,1,0:T(1,128)S(1)} all-to-all(f32[256,1,128]{2,1,0:T(1,128)S(1)} %get-tuple-element.23), channel_id=1, replica_groups=mesh['tm_0'=4,'tm_1'=8,'order_0'=4,'order_1'=2] {'tm_0','tm_1','order_0'..., dimensions={0} | all-to-all | bytes 262144 | tf_op jit(solution)/shard_map/all_to_all | solution.py:442
  91.8 1.0 %shard_map.146 = (f32[16,1,256]{2,1,0:T(1,128)}, f32[16,1,256]{2,1,0:T(1,128)}, f32[16,1,256]{2,1,0:T(1,128)}) custom-call(f32[256,1,128]{2,1,0:T(1,128)S(1)} %all_to_all.26.sums_ref, f32[16,256]{1,0:T(8,128)S(1)} %get-tuple-element.24.image_ref, f32[16,256]{1,0:T(8,128)S(1)} %get-tuple-element.25.applied_ref, f32[16,256]{1,0:T(8,128)S(1)} %get-tuple-element.26.both_ref, ...), custom_call_target="tpu_custom_call" | custom-call | flops 100000 | bytes 1000000 | tf_op jit(solution)/shard_map/pallas_call | solution.py:429
  (6 shorter events, 0.0 us)
Async XLA Ops:
  2.2 22.2 %all-to-all-start = ((bf16[32,40,128]{2,1,0:T(8,128)(2,1)}), bf16[32,40,128]{2,1,0:T(8,128)(2,1)S(1)}, u32[]{:S(2)}, u32[]{:S(2)}) async-start(bf16[32,40,128]{2,1,0:T(8,128)(2,1)} %shard_map.139), calls=%async_computation | async-start | bytes 655360 | tf_op jit(solution)/shard_map/all_to_all | solution.py:442
  17.1 19.2 %copy-start.4 = (f32[3,4]{1,0:T(4,128)S(1)}, f32[3,4]{1,0:T(4,128)}, u32[]{:S(2)}) copy-start(f32[3,4]{1,0:T(4,128)} %arr_ref.1) | copy-start | bytes 148
  17.1 19.2 %copy-start.5 = (f32[3,4]{1,0:T(4,128)S(1)}, f32[3,4]{1,0:T(4,128)}, u32[]{:S(2)}) copy-start(f32[3,4]{1,0:T(4,128)} %mar_ref.1) | copy-start | bytes 148
  17.1 19.2 %copy-start.8 = (s32[3]{0:T(128)S(1)}, s32[3]{0:T(128)}, u32[]{:S(2)}) copy-start(s32[3]{0:T(128)} %aro_ref.1) | copy-start | bytes 40
  17.1 19.2 %copy-start.9 = (s32[3]{0:T(128)S(1)}, s32[3]{0:T(128)}, u32[]{:S(2)}) copy-start(s32[3]{0:T(128)} %mao_ref.1) | copy-start | bytes 40
  17.1 24.1 %copy-start.6 = (s32[128]{0:T(128)S(1)}, s32[128]{0:T(128)}, u32[]{:S(2)}) copy-start(s32[128]{0:T(128)} %param.13) | copy-start | bytes 1540
  27.6 13.6 %all-to-all-start.1 = ((bf16[8,16,384]{2,1,0:T(8,128)(2,1)}), bf16[8,16,384]{2,1,0:T(8,128)(2,1)S(1)}, u32[]{:S(2)}, u32[]{:S(2)}) async-start(bf16[8,16,384]{2,1,0:T(8,128)(2,1)} %shard_map.140), calls=%async_computation.1 | async-start | bytes 196608 | tf_op jit(solution)/shard_map/all_to_all | solution.py:442
  42.1 13.3 %all-to-all-start.2 = ((f32[32,3,128]{2,1,0:T(4,128)}), f32[32,3,128]{2,1,0:T(4,128)S(1)}, u32[]{:S(2)}, u32[]{:S(2)}) async-start(f32[32,3,128]{2,1,0:T(4,128)} %get-tuple-element.16), calls=%async_computation.2 | async-start | bytes 131072 | tf_op jit(solution)/shard_map/all_to_all | solution.py:442
  50.0 19.6 %copy-start = (f32[16,1,256]{2,1,0:T(1,128)S(1)}, f32[16,1,256]{2,1,0:T(1,128)}, u32[]{:S(2)}) copy-start(f32[16,1,256]{2,1,0:T(1,128)} %direction_ref.3) | copy-start | bytes 49156
  50.0 19.6 %copy-start.1 = (f32[1,2,128,128]{3,2,1,0:T(8,128)S(1)}, f32[1,2,128,128]{3,2,1,0:T(8,128)}, u32[]{:S(2)}) copy-start(f32[1,2,128,128]{3,2,1,0:T(8,128)} %precond_ref.1) | copy-start | bytes 393220
  50.0 19.6 %copy-start.2 = (f32[16,1,256]{2,1,0:T(1,128)S(1)}, f32[16,1,256]{2,1,0:T(1,128)}, u32[]{:S(2)}) copy-start(f32[16,1,256]{2,1,0:T(1,128)} %residual_ref.3) | copy-start | bytes 49156
  50.0 19.5 %copy-start.7 = (f32[1,256]{1,0:T(1,128)S(1)}, f32[1,256]{1,0:T(1,128)}, u32[]{:S(2)}) copy-start(f32[1,256]{1,0:T(1,128)} %kaula_ref.1) | copy-start | bytes 3076
  50.0 41.8 %copy-start.3 = (f32[16,1,256]{2,1,0:T(1,128)S(1)}, f32[16,1,256]{2,1,0:T(1,128)}, u32[]{:S(2)}) copy-start(f32[16,1,256]{2,1,0:T(1,128)} %solution_ref.1) | copy-start | bytes 49156

commit v10 on v9

--- a/solution.py
+++ b/solution.py
@@ -264,21 +264,18 @@
         copy.start()
     gaps = gaps_ref[...].astype(jnp.float32)
     pieces = []
-    highs, lows = [], []
+    edges = []
     blank = jnp.zeros((8, 128), jnp.bfloat16)
     for c in range(3):
         pieces.append(dot(masked_ref[16 * c : 16 * c + 16, :], near_ref[c], ((1,), (0,))) * gaps)
-        high, low = split_in_two(edge_ref[c] * gaps)
-        highs.append(jnp.concatenate([high if d == c else blank for d in range(3)], axis=1))
-        lows.append(jnp.concatenate([low if d == c else blank for d in range(3)], axis=1))
-    rows = jnp.concatenate(
-        [*split_in_two(jnp.concatenate(pieces, axis=1)), *highs, *lows], axis=0
-    )
+        edge = (edge_ref[c] * gaps).astype(jnp.bfloat16)
+        edges.append(jnp.concatenate([edge if d == c else blank for d in range(3)], axis=1))
+    rows = jnp.concatenate([*split_in_two(jnp.concatenate(pieces, axis=1)), *edges], axis=0)
 
     def spread(at, block):
         found = jnp.dot(rows, block, preferred_element_type=jnp.float32)
         here_ref[:, at : at + width] = found[0:16] + found[16:32]
-        high, low = split_in_two(found[32:56] + found[56:80])
+        high, low = split_in_two(found[32:56])
         basis_ref[0:24, at : at + width] = high
         basis_ref[24:48, at : at + width] = low
 

time: 93.3 us -> 92.8 us (level)
  transfers between devices with their start and end apart: 3 -> 3, of which waited for: 3 -> 3; matrix products, arithmetic and copies ran while one was open for 3% -> 3% of each run, Pallas kernels for 6% -> 5%
where the time goes in v10:
time: 92.8 us; the launch traced here: 92.2 us
  blocking collectives  34.4 us (37%)
  starting transfers between devices  25.1 us (27%)
  waiting for transfers between devices  15.9 us (17%)
  Pallas kernels  13.1 us (14%)
  local copies, waits for them, and re-layouts  2.93 us (3%)
    all_to_all x2, blocking collectives, exchange(): return lax.all_to_all(value, axes, split_axis=0, concat_axis=0, tiled=True)  34.4 us
    all_to_all x3, starting transfers between devices, exchange(): return lax.all_to_all(value, axes, split_axis=0, concat_axis=0, tiled=True)  25.1 us
    all_to_all x3, waiting for transfers between devices, exchange(): return lax.all_to_all(value, axes, split_axis=0, concat_axis=0, tiled=True)  15.9 us
    pallas_call x8, Pallas kernels, run(): pl.pallas_call(kernel, out_shape=shapes, in_specs=[pl.BlockSpec(memory_sp...  13.1 us
  transfers between devices with their start and end apart: 3, of which 3 were waited for; matrix products, arithmetic and copies ran while one was open for 3% of the time, Pallas kernels for 5%

profile of v10, /device:TPU:1, one launch (start us, length us, event | category | flops | bytes accessed | tf_op | source)
XLA Modules:
  0.0 92.2 jit_solution(16879869569961293607)
XLA Ops:
  0.6 1.5 %shard_map.139 = bf16[32,40,128]{2,1,0:T(8,128)(2,1)} custom-call(f32[16,1,256]{2,1,0:T(1,128)} %direction_ref.3, s32[1,128]{1,0:T(1,128)} %bitcast.5), custom_call_target="tpu_custom_call" | custom-call | flops 100000 | bytes 1000000 | tf_op jit(solution)/shard_map/pallas_call | solution.py:426
  2.2 12.0 %all-to-all-start = ((bf16[32,40,128]{2,1,0:T(8,128)(2,1)}), bf16[32,40,128]{2,1,0:T(8,128)(2,1)S(1)}, u32[]{:S(2)}, u32[]{:S(2)}) async-start(bf16[32,40,128]{2,1,0:T(8,128)(2,1)} %shard_map.139), calls=%async_computation | async-start | bytes 655360 | tf_op jit(solution)/shard_map/all_to_all | solution.py:439
  14.2 1.5 %slice.6.kept_ref = bf16[3,128,2048]{2,1,0:T(8,128)(2,1)S(1)} slice(bf16[3,128,8192]{2,1,0:T(8,128)(2,1)} %design_ref.3), slice={[0:3], [0:128], [0:2048]} | slice | bytes 3145728 | tf_op jit(solution)/shard_map/slice | solution.py:502
  15.7 1.4 %slice.7.early_ref = bf16[3,128,1536]{2,1,0:T(8,128)(2,1)S(1)} slice(bf16[3,128,8192]{2,1,0:T(8,128)(2,1)} %design_ref.3), slice={[0:3], [0:128], [2048:3584]} | slice | bytes 2359296 | tf_op jit(solution)/shard_map/slice | solution.py:506
  17.1 0.0 copy-start.4
  17.1 0.0 copy-start.5
  17.1 0.0 copy-start.8
  17.1 0.0 copy-start.9
  17.1 0.0 copy-start.6
  17.1 7.2 %all-to-all-done.got_ref = bf16[32,40,128]{2,1,0:T(8,128)(2,1)S(1)} async-done(((bf16[32,40,128]{2,1,0:T(8,128)(2,1)}), bf16[32,40,128]{2,1,0:T(8,128)(2,1)S(1)}, u32[]{:S(2)}, u32[]{:S(2)}) %all-to-all-start) | async-done | bytes 327712 | tf_op jit(solution)/shard_map/all_to_all | solution.py:439
  24.4 3.2 %shard_map.140 = bf16[8,16,384]{2,1,0:T(8,128)(2,1)} custom-call(bf16[32,40,128]{2,1,0:T(8,128)(2,1)S(1)} %all-to-all-done.got_ref, bf16[3,128,8192]{2,1,0:T(8,128)(2,1)} %design_ref.3, bf16[3,128,2048]{2,1,0:T(8,128)(2,1)S(1)} %slice.6.kept_ref, bf16[3,128,1536]{2,1,0:T(8,128)(2,1)S(1)} %slice.7.early_ref), custom_call_target="tpu_custom_call" | custom-call | flops 100000 | bytes 1000000 | tf_op jit(solution)/shard_map/pallas_call | solution.py:426
  27.6 8.6 %all-to-all-start.1 = ((bf16[8,16,384]{2,1,0:T(8,128)(2,1)}), bf16[8,16,384]{2,1,0:T(8,128)(2,1)S(1)}, u32[]{:S(2)}, u32[]{:S(2)}) async-start(bf16[8,16,384]{2,1,0:T(8,128)(2,1)} %shard_map.140), calls=%async_computation.1 | async-start | bytes 196608 | tf_op jit(solution)/shard_map/all_to_all | solution.py:439
  36.2 0.0 copy-done.4
  36.2 0.0 copy-done.5
  36.3 0.0 copy-done.8
  36.3 2.1 %shard_map.141 = (f32[3,8,128]{2,1,0:T(8,128)S(1)}, f32[3,128,128]{2,1,0:T(8,128)S(1)}, f32[3,8,256]{2,1,0:T(8,128)S(1)}, f32[3,8,128]{2,1,0:T(8,128)S(1)}) custom-call(s32[1,1]{1,0:T(1,128)} %bitcast.2.place_ref, s32[3]{0:T(128)S(1)} %copy-done.8, s32[3]{0:T(128)S(1)} %copy-done.9, f32[3,4]{1,0:T(4,128)S(1)} %copy-done.4, f32[3,4]{1,0:T(4,128)S(1)} %copy-done.5, ...), custom_call_target="tpu_custom_call" | custom-call | flops 10000000 | bytes 1000000 | tf_op jit(solution)/shard_map/pallas_call | solution.py:426
  38.4 2.8 %all-to-all-done.1.parts_ref = bf16[8,16,384]{2,1,0:T(8,128)(2,1)S(1)} async-done(((bf16[8,16,384]{2,1,0:T(8,128)(2,1)}), bf16[8,16,384]{2,1,0:T(8,128)(2,1)S(1)}, u32[]{:S(2)}, u32[]{:S(2)}) %all-to-all-start.1) | async-done | bytes 98336 | tf_op jit(solution)/shard_map/all_to_all | solution.py:439
  41.2 0.9 shard_map.142
  42.1 4.4 %all-to-all-start.2 = ((f32[32,3,128]{2,1,0:T(4,128)}), f32[32,3,128]{2,1,0:T(4,128)S(1)}, u32[]{:S(2)}, u32[]{:S(2)}) async-start(f32[32,3,128]{2,1,0:T(4,128)} %get-tuple-element.16), calls=%async_computation.2 | async-start | bytes 131072 | tf_op jit(solution)/shard_map/all_to_all | solution.py:439
  46.5 2.9 %shard_map.143 = (f32[16,8192]{1,0:T(8,128)S(1)}, bf16[48,8192]{1,0:T(8,128)(2,1)S(1)}) custom-call(f32[48,128]{1,0:T(8,128)S(1)} %get-tuple-element.18.masked_ref, f32[3,128,128]{2,1,0:T(8,128)S(1)} %get-tuple-element.19.near_ref, f32[3,8,128]{2,1,0:T(8,128)S(1)} %get-tuple-element.20.edge_ref, s32[1,128]{1,0:T(1,128)S(1)} %bitcast.4, ...), custom_call_target="tpu_custom_call" | custom-call | flops 10000000 | bytes 1000000 | tf_op jit(solution)/shard_map/pallas_call | solution.py:426
  49.4 0.0 copy-start
  49.5 0.0 copy-start.1
  49.5 0.0 copy-start.2
  49.5 0.0 copy-start.7
  49.5 0.0 copy-start.3
  49.5 5.9 %all-to-all-done.2.states_ref = f32[32,3,128]{2,1,0:T(4,128)S(1)} async-done(((f32[32,3,128]{2,1,0:T(4,128)}), f32[32,3,128]{2,1,0:T(4,128)S(1)}, u32[]{:S(2)}, u32[]{:S(2)}) %all-to-all-start.2) | async-done | bytes 49184 | tf_op jit(solution)/shard_map/all_to_all | solution.py:439
  55.4 0.8 shard_map.144
  56.2 12.8 %all_to_all.25.arrived_ref = bf16[32,16,256]{2,1,0:T(8,128)(2,1)S(1)} all-to-all(bf16[32,16,256]{2,1,0:T(8,128)(2,1)S(1)} %shard_map.144), channel_id=1, replica_groups=mesh['tm_0'=4,'tm_1'=8,'order_0'=4,'order_1'=2] {'tm_0','tm_1'}, dimensions={0} | all-to-all | bytes 524288 | tf_op jit(solution)/shard_map/all_to_all | solution.py:439
  69.0 0.0 copy-done.1
  69.0 0.6 shard_map.145
  69.7 21.6 %all_to_all.26.sums_ref = f32[256,1,128]{2,1,0:T(1,128)S(1)} all-to-all(f32[256,1,128]{2,1,0:T(1,128)S(1)} %get-tuple-element.23), channel_id=1, replica_groups=mesh['tm_0'=4,'tm_1'=8,'order_0'=4,'order_1'=2] {'tm_0','tm_1','order_0'..., dimensions={0} | all-to-all | bytes 262144 | tf_op jit(solution)/shard_map/all_to_all | solution.py:439
  91.2 1.0 %shard_map.146 = (f32[16,1,256]{2,1,0:T(1,128)}, f32[16,1,256]{2,1,0:T(1,128)}, f32[16,1,256]{2,1,0:T(1,128)}) custom-call(f32[256,1,128]{2,1,0:T(1,128)S(1)} %all_to_all.26.sums_ref, f32[16,256]{1,0:T(8,128)S(1)} %get-tuple-element.24.image_ref, f32[16,256]{1,0:T(8,128)S(1)} %get-tuple-element.25.applied_ref, f32[16,256]{1,0:T(8,128)S(1)} %get-tuple-element.26.both_ref, ...), custom_call_target="tpu_custom_call" | custom-call | flops 100000 | bytes 1000000 | tf_op jit(solution)/shard_map/pallas_call | solution.py:426
  (6 shorter events, 0.0 us)
Async XLA Ops:
  2.2 22.2 %all-to-all-start = ((bf16[32,40,128]{2,1,0:T(8,128)(2,1)}), bf16[32,40,128]{2,1,0:T(8,128)(2,1)S(1)}, u32[]{:S(2)}, u32[]{:S(2)}) async-start(bf16[32,40,128]{2,1,0:T(8,128)(2,1)} %shard_map.139), calls=%async_computation | async-start | bytes 655360 | tf_op jit(solution)/shard_map/all_to_all | solution.py:439
  17.1 19.2 %copy-start.4 = (f32[3,4]{1,0:T(4,128)S(1)}, f32[3,4]{1,0:T(4,128)}, u32[]{:S(2)}) copy-start(f32[3,4]{1,0:T(4,128)} %arr_ref.1) | copy-start | bytes 148
  17.1 19.2 %copy-start.5 = (f32[3,4]{1,0:T(4,128)S(1)}, f32[3,4]{1,0:T(4,128)}, u32[]{:S(2)}) copy-start(f32[3,4]{1,0:T(4,128)} %mar_ref.1) | copy-start | bytes 148
  17.1 19.2 %copy-start.8 = (s32[3]{0:T(128)S(1)}, s32[3]{0:T(128)}, u32[]{:S(2)}) copy-start(s32[3]{0:T(128)} %aro_ref.1) | copy-start | bytes 40
  17.1 19.2 %copy-start.9 = (s32[3]{0:T(128)S(1)}, s32[3]{0:T(128)}, u32[]{:S(2)}) copy-start(s32[3]{0:T(128)} %mao_ref.1) | copy-start | bytes 40
  17.1 24.1 %copy-start.6 = (s32[128]{0:T(128)S(1)}, s32[128]{0:T(128)}, u32[]{:S(2)}) copy-start(s32[128]{0:T(128)} %param.13) | copy-start | bytes 1540
  27.6 13.6 %all-to-all-start.1 = ((bf16[8,16,384]{2,1,0:T(8,128)(2,1)}), bf16[8,16,384]{2,1,0:T(8,128)(2,1)S(1)}, u32[]{:S(2)}, u32[]{:S(2)}) async-start(bf16[8,16,384]{2,1,0:T(8,128)(2,1)} %shard_map.140), calls=%async_computation.1 | async-start | bytes 196608 | tf_op jit(solution)/shard_map/all_to_all | solution.py:439
  42.1 13.3 %all-to-all-start.2 = ((f32[32,3,128]{2,1,0:T(4,128)}), f32[32,3,128]{2,1,0:T(4,128)S(1)}, u32[]{:S(2)}, u32[]{:S(2)}) async-start(f32[32,3,128]{2,1,0:T(4,128)} %get-tuple-element.16), calls=%async_computation.2 | async-start | bytes 131072 | tf_op jit(solution)/shard_map/all_to_all | solution.py:439
  49.4 19.6 %copy-start = (f32[16,1,256]{2,1,0:T(1,128)S(1)}, f32[16,1,256]{2,1,0:T(1,128)}, u32[]{:S(2)}) copy-start(f32[16,1,256]{2,1,0:T(1,128)} %direction_ref.3) | copy-start | bytes 49156
  49.5 19.6 %copy-start.1 = (f32[1,2,128,128]{3,2,1,0:T(8,128)S(1)}, f32[1,2,128,128]{3,2,1,0:T(8,128)}, u32[]{:S(2)}) copy-start(f32[1,2,128,128]{3,2,1,0:T(8,128)} %precond_ref.1) | copy-start | bytes 393220
  49.5 19.6 %copy-start.2 = (f32[16,1,256]{2,1,0:T(1,128)S(1)}, f32[16,1,256]{2,1,0:T(1,128)}, u32[]{:S(2)}) copy-start(f32[16,1,256]{2,1,0:T(1,128)} %residual_ref.3) | copy-start | bytes 49156
  49.5 19.6 %copy-start.7 = (f32[1,256]{1,0:T(1,128)S(1)}, f32[1,256]{1,0:T(1,128)}, u32[]{:S(2)}) copy-start(f32[1,256]{1,0:T(1,128)} %kaula_ref.1) | copy-start | bytes 3076
  49.5 41.8 %copy-start.3 = (f32[16,1,256]{2,1,0:T(1,128)S(1)}, f32[16,1,256]{2,1,0:T(1,128)}, u32[]{:S(2)}) copy-start(f32[16,1,256]{2,1,0:T(1,128)} %solution_ref.1) | copy-start | bytes 49156

commit v11 on v10

--- a/solution.py
+++ b/solution.py
@@ -275,9 +275,7 @@
     def spread(at, block):
         found = jnp.dot(rows, block, preferred_element_type=jnp.float32)
         here_ref[:, at : at + width] = found[0:16] + found[16:32]
-        high, low = split_in_two(found[32:56])
-        basis_ref[0:24, at : at + width] = high
-        basis_ref[24:48, at : at + width] = low
+        basis_ref[:, at : at + width] = found[32:56].astype(jnp.bfloat16)
 
     for at in range(0, start, width):
         spread(at, kept_ref[:, :, at : at + width].reshape(384, width))
@@ -296,8 +294,8 @@
     found = jnp.where(lane < 16, jnp.concatenate(parts, axis=0), 0.0)
     high = found.astype(jnp.bfloat16).astype(jnp.float32)
     low = pltpu.roll(found - high, 16, 1)
-    tall = jnp.concatenate([high + low, high, jnp.zeros((80, 128), jnp.float32)], axis=0)
-    left = tall.T[0:32, 0:48].astype(jnp.bfloat16)
+    tall = jnp.concatenate([high + low, jnp.zeros((104, 128), jnp.float32)], axis=0)
+    left = tall.T[0:32, 0:24].astype(jnp.bfloat16)
     peers = out_ref.shape[0]
     for p in range(0, peers, 4):
         span = slice(256 * p, 256 * p + 1024)
@@ -533,7 +531,7 @@
     states = exchange(message, TM)
     here, basis = run(
         spread_kernel,
-        [((16, design.shape[2]), f32), ((48, design.shape[2]), bf16)],
+        [((16, design.shape[2]), f32), ((24, design.shape[2]), bf16)],
         [masked, near, edge, gaps, design, kept],
         anywhere=(4,),
         scratch=[

time: 92.8 us -> 93.1 us (level)
  transfers between devices with their start and end apart: 3 -> 3, of which waited for: 3 -> 3; matrix products, arithmetic and copies ran while one was open for 3% -> 3% of each run, Pallas kernels for 5% -> 6%
where the time goes in v11:
time: 93.1 us; the launch traced here: 92.6 us
  blocking collectives  34.8 us (37%)
  starting transfers between devices  25.1 us (27%)
  waiting for transfers between devices  15.6 us (17%)
  Pallas kernels  13.4 us (14%)
  local copies, waits for them, and re-layouts  2.93 us (3%)
    all_to_all x2, blocking collectives, exchange(): return lax.all_to_all(value, axes, split_axis=0, concat_axis=0, tiled=True)  34.8 us
    all_to_all x3, starting transfers between devices, exchange(): return lax.all_to_all(value, axes, split_axis=0, concat_axis=0, tiled=True)  25.1 us
    all_to_all x3, waiting for transfers between devices, exchange(): return lax.all_to_all(value, axes, split_axis=0, concat_axis=0, tiled=True)  15.6 us
    pallas_call x8, Pallas kernels, run(): pl.pallas_call(kernel, out_shape=shapes, in_specs=[pl.BlockSpec(memory_sp...  13.4 us
  transfers between devices with their start and end apart: 3, of which 3 were waited for; matrix products, arithmetic and copies ran while one was open for 3% of the time, Pallas kernels for 6%

profile of v11, /device:TPU:1, one launch (start us, length us, event | category | flops | bytes accessed | tf_op | source)
XLA Modules:
  0.0 92.6 jit_solution(10892215115764881872)
XLA Ops:
  0.6 1.5 %shard_map.139 = bf16[32,40,128]{2,1,0:T(8,128)(2,1)} custom-call(f32[16,1,256]{2,1,0:T(1,128)} %direction_ref.3, s32[1,128]{1,0:T(1,128)} %bitcast.5), custom_call_target="tpu_custom_call" | custom-call | flops 100000 | bytes 1000000 | tf_op jit(solution)/shard_map/pallas_call | solution.py:424
  2.2 12.0 %all-to-all-start = ((bf16[32,40,128]{2,1,0:T(8,128)(2,1)}), bf16[32,40,128]{2,1,0:T(8,128)(2,1)S(1)}, u32[]{:S(2)}, u32[]{:S(2)}) async-start(bf16[32,40,128]{2,1,0:T(8,128)(2,1)} %shard_map.139), calls=%async_computation | async-start | bytes 655360 | tf_op jit(solution)/shard_map/all_to_all | solution.py:437
  14.2 1.5 %slice.6.kept_ref = bf16[3,128,2048]{2,1,0:T(8,128)(2,1)S(1)} slice(bf16[3,128,8192]{2,1,0:T(8,128)(2,1)} %design_ref.3), slice={[0:3], [0:128], [0:2048]} | slice | bytes 3145728 | tf_op jit(solution)/shard_map/slice | solution.py:500
  15.7 1.4 %slice.7.early_ref = bf16[3,128,1536]{2,1,0:T(8,128)(2,1)S(1)} slice(bf16[3,128,8192]{2,1,0:T(8,128)(2,1)} %design_ref.3), slice={[0:3], [0:128], [2048:3584]} | slice | bytes 2359296 | tf_op jit(solution)/shard_map/slice | solution.py:504
  17.1 0.0 copy-start.4
  17.1 0.0 copy-start.5
  17.1 0.0 copy-start.8
  17.1 0.0 copy-start.9
  17.1 0.0 copy-start.6
  17.1 7.2 %all-to-all-done.got_ref = bf16[32,40,128]{2,1,0:T(8,128)(2,1)S(1)} async-done(((bf16[32,40,128]{2,1,0:T(8,128)(2,1)}), bf16[32,40,128]{2,1,0:T(8,128)(2,1)S(1)}, u32[]{:S(2)}, u32[]{:S(2)}) %all-to-all-start) | async-done | bytes 327712 | tf_op jit(solution)/shard_map/all_to_all | solution.py:437
  24.4 3.2 %shard_map.140 = bf16[8,16,384]{2,1,0:T(8,128)(2,1)} custom-call(bf16[32,40,128]{2,1,0:T(8,128)(2,1)S(1)} %all-to-all-done.got_ref, bf16[3,128,8192]{2,1,0:T(8,128)(2,1)} %design_ref.3, bf16[3,128,2048]{2,1,0:T(8,128)(2,1)S(1)} %slice.6.kept_ref, bf16[3,128,1536]{2,1,0:T(8,128)(2,1)S(1)} %slice.7.early_ref), custom_call_target="tpu_custom_call" | custom-call | flops 100000 | bytes 1000000 | tf_op jit(solution)/shard_map/pallas_call | solution.py:424
  27.6 8.6 %all-to-all-start.1 = ((bf16[8,16,384]{2,1,0:T(8,128)(2,1)}), bf16[8,16,384]{2,1,0:T(8,128)(2,1)S(1)}, u32[]{:S(2)}, u32[]{:S(2)}) async-start(bf16[8,16,384]{2,1,0:T(8,128)(2,1)} %shard_map.140), calls=%async_computation.1 | async-start | bytes 196608 | tf_op jit(solution)/shard_map/all_to_all | solution.py:437
  36.2 0.0 copy-done.4
  36.2 0.0 copy-done.5
  36.3 0.0 copy-done.8
  36.3 2.1 %shard_map.141 = (f32[3,8,128]{2,1,0:T(8,128)S(1)}, f32[3,128,128]{2,1,0:T(8,128)S(1)}, f32[3,8,256]{2,1,0:T(8,128)S(1)}, f32[3,8,128]{2,1,0:T(8,128)S(1)}) custom-call(s32[1,1]{1,0:T(1,128)} %bitcast.2.place_ref, s32[3]{0:T(128)S(1)} %copy-done.8, s32[3]{0:T(128)S(1)} %copy-done.9, f32[3,4]{1,0:T(4,128)S(1)} %copy-done.4, f32[3,4]{1,0:T(4,128)S(1)} %copy-done.5, ...), custom_call_target="tpu_custom_call" | custom-call | flops 10000000 | bytes 1000000 | tf_op jit(solution)/shard_map/pallas_call | solution.py:424
  38.4 2.8 %all-to-all-done.1.parts_ref = bf16[8,16,384]{2,1,0:T(8,128)(2,1)S(1)} async-done(((bf16[8,16,384]{2,1,0:T(8,128)(2,1)}), bf16[8,16,384]{2,1,0:T(8,128)(2,1)S(1)}, u32[]{:S(2)}, u32[]{:S(2)}) %all-to-all-start.1) | async-done | bytes 98336 | tf_op jit(solution)/shard_map/all_to_all | solution.py:437
  41.2 0.9 shard_map.142
  42.1 4.4 %all-to-all-start.2 = ((f32[32,3,128]{2,1,0:T(4,128)}), f32[32,3,128]{2,1,0:T(4,128)S(1)}, u32[]{:S(2)}, u32[]{:S(2)}) async-start(f32[32,3,128]{2,1,0:T(4,128)} %get-tuple-element.16), calls=%async_computation.2 | async-start | bytes 131072 | tf_op jit(solution)/shard_map/all_to_all | solution.py:437
  46.5 3.3 %shard_map.143 = (f32[16,8192]{1,0:T(8,128)S(1)}, bf16[24,8192]{1,0:T(8,128)(2,1)S(1)}) custom-call(f32[48,128]{1,0:T(8,128)S(1)} %get-tuple-element.18.masked_ref, f32[3,128,128]{2,1,0:T(8,128)S(1)} %get-tuple-element.19.near_ref, f32[3,8,128]{2,1,0:T(8,128)S(1)} %get-tuple-element.20.edge_ref, s32[1,128]{1,0:T(1,128)S(1)} %bitcast.4, ...), custom_call_target="tpu_custom_call" | custom-call | flops 10000000 | bytes 1000000 | tf_op jit(solution)/shard_map/pallas_call | solution.py:424
  49.8 0.0 copy-start
  49.8 0.0 copy-start.1
  49.8 0.0 copy-start.2
  49.8 0.0 copy-start.7
  49.9 0.0 copy-start.3
  49.9 5.5 %all-to-all-done.2.states_ref = f32[32,3,128]{2,1,0:T(4,128)S(1)} async-done(((f32[32,3,128]{2,1,0:T(4,128)}), f32[32,3,128]{2,1,0:T(4,128)S(1)}, u32[]{:S(2)}, u32[]{:S(2)}) %all-to-all-start.2) | async-done | bytes 49184 | tf_op jit(solution)/shard_map/all_to_all | solution.py:437
  55.4 0.8 shard_map.144
  56.2 13.2 %all_to_all.25.arrived_ref = bf16[32,16,256]{2,1,0:T(8,128)(2,1)S(1)} all-to-all(bf16[32,16,256]{2,1,0:T(8,128)(2,1)S(1)} %shard_map.144), channel_id=1, replica_groups=mesh['tm_0'=4,'tm_1'=8,'order_0'=4,'order_1'=2] {'tm_0','tm_1'}, dimensions={0} | all-to-all | bytes 524288 | tf_op jit(solution)/shard_map/all_to_all | solution.py:437
  69.4 0.0 copy-done.2
  69.4 0.6 shard_map.145
  70.0 21.6 %all_to_all.26.sums_ref = f32[256,1,128]{2,1,0:T(1,128)S(1)} all-to-all(f32[256,1,128]{2,1,0:T(1,128)S(1)} %get-tuple-element.23), channel_id=1, replica_groups=mesh['tm_0'=4,'tm_1'=8,'order_0'=4,'order_1'=2] {'tm_0','tm_1','order_0'..., dimensions={0} | all-to-all | bytes 262144 | tf_op jit(solution)/shard_map/all_to_all | solution.py:437
  91.6 1.0 %shard_map.146 = (f32[16,1,256]{2,1,0:T(1,128)}, f32[16,1,256]{2,1,0:T(1,128)}, f32[16,1,256]{2,1,0:T(1,128)}) custom-call(f32[256,1,128]{2,1,0:T(1,128)S(1)} %all_to_all.26.sums_ref, f32[16,256]{1,0:T(8,128)S(1)} %get-tuple-element.24.image_ref, f32[16,256]{1,0:T(8,128)S(1)} %get-tuple-element.25.applied_ref, f32[16,256]{1,0:T(8,128)S(1)} %get-tuple-element.26.both_ref, ...), custom_call_target="tpu_custom_call" | custom-call | flops 100000 | bytes 1000000 | tf_op jit(solution)/shard_map/pallas_call | solution.py:424
  (6 shorter events, 0.0 us)
Async XLA Ops:
  2.2 22.2 %all-to-all-start = ((bf16[32,40,128]{2,1,0:T(8,128)(2,1)}), bf16[32,40,128]{2,1,0:T(8,128)(2,1)S(1)}, u32[]{:S(2)}, u32[]{:S(2)}) async-start(bf16[32,40,128]{2,1,0:T(8,128)(2,1)} %shard_map.139), calls=%async_computation | async-start | bytes 655360 | tf_op jit(solution)/shard_map/all_to_all | solution.py:437
  17.1 19.2 %copy-start.4 = (f32[3,4]{1,0:T(4,128)S(1)}, f32[3,4]{1,0:T(4,128)}, u32[]{:S(2)}) copy-start(f32[3,4]{1,0:T(4,128)} %arr_ref.1) | copy-start | bytes 148
  17.1 19.2 %copy-start.5 = (f32[3,4]{1,0:T(4,128)S(1)}, f32[3,4]{1,0:T(4,128)}, u32[]{:S(2)}) copy-start(f32[3,4]{1,0:T(4,128)} %mar_ref.1) | copy-start | bytes 148
  17.1 19.2 %copy-start.8 = (s32[3]{0:T(128)S(1)}, s32[3]{0:T(128)}, u32[]{:S(2)}) copy-start(s32[3]{0:T(128)} %aro_ref.1) | copy-start | bytes 40
  17.1 19.2 %copy-start.9 = (s32[3]{0:T(128)S(1)}, s32[3]{0:T(128)}, u32[]{:S(2)}) copy-start(s32[3]{0:T(128)} %mao_ref.1) | copy-start | bytes 40
  17.1 24.1 %copy-start.6 = (s32[128]{0:T(128)S(1)}, s32[128]{0:T(128)}, u32[]{:S(2)}) copy-start(s32[128]{0:T(128)} %param.13) | copy-start | bytes 1540
  27.6 13.6 %all-to-all-start.1 = ((bf16[8,16,384]{2,1,0:T(8,128)(2,1)}), bf16[8,16,384]{2,1,0:T(8,128)(2,1)S(1)}, u32[]{:S(2)}, u32[]{:S(2)}) async-start(bf16[8,16,384]{2,1,0:T(8,128)(2,1)} %shard_map.140), calls=%async_computation.1 | async-start | bytes 196608 | tf_op jit(solution)/shard_map/all_to_all | solution.py:437
  42.1 13.3 %all-to-all-start.2 = ((f32[32,3,128]{2,1,0:T(4,128)}), f32[32,3,128]{2,1,0:T(4,128)S(1)}, u32[]{:S(2)}, u32[]{:S(2)}) async-start(f32[32,3,128]{2,1,0:T(4,128)} %get-tuple-element.16), calls=%async_computation.2 | async-start | bytes 131072 | tf_op jit(solution)/shard_map/all_to_all | solution.py:437
  49.8 19.6 %copy-start = (f32[16,1,256]{2,1,0:T(1,128)S(1)}, f32[16,1,256]{2,1,0:T(1,128)}, u32[]{:S(2)}) copy-start(f32[16,1,256]{2,1,0:T(1,128)} %direction_ref.3) | copy-start | bytes 49156
  49.8 19.5 %copy-start.1 = (f32[1,2,128,128]{3,2,1,0:T(8,128)S(1)}, f32[1,2,128,128]{3,2,1,0:T(8,128)}, u32[]{:S(2)}) copy-start(f32[1,2,128,128]{3,2,1,0:T(8,128)} %precond_ref.1) | copy-start | bytes 393220
  49.8 19.5 %copy-start.2 = (f32[16,1,256]{2,1,0:T(1,128)S(1)}, f32[16,1,256]{2,1,0:T(1,128)}, u32[]{:S(2)}) copy-start(f32[16,1,256]{2,1,0:T(1,128)} %residual_ref.3) | copy-start | bytes 49156
  49.8 19.5 %copy-start.7 = (f32[1,256]{1,0:T(1,128)S(1)}, f32[1,256]{1,0:T(1,128)}, u32[]{:S(2)}) copy-start(f32[1,256]{1,0:T(1,128)} %kaula_ref.1) | copy-start | bytes 3076
  49.9 41.7 %copy-start.3 = (f32[16,1,256]{2,1,0:T(1,128)S(1)}, f32[16,1,256]{2,1,0:T(1,128)}, u32[]{:S(2)}) copy-start(f32[16,1,256]{2,1,0:T(1,128)} %solution_ref.1) | copy-start | bytes 49156
